TPU v7x, 32 devices: a whole 2x2x4 slice. The times are simulated.
32 devices in a mesh: pipe: 4 (over y, core), band: 8 (over z, x).
Axes of the slice: x: 2, y: 2, z: 4, core: 2. Of those that a mesh axis runs over, the one named last changes fastest.
Arguments:
- memory: float32 [4, 512, 512, 128], P('pipe', 'band'), may hold values from -6 to 6
- shear_blocks: bfloat16 [4, 3, 4, 4, 2, 128, 128], P('pipe'), may hold values from -0.375 to 0.375
- shear_offsets: int32 [4, 3, 4], P('pipe'), may hold values from 0 to 3
- block_lists: int32 [4, 3, 4, 2], P('pipe'), may hold values from 0 to 3
- mix_weight: bfloat16 [4, 128, 128], P('pipe'), may hold values from -0.5 to 0.5
Outputs:
- memory_out: float32 [4, 512, 512, 128], P('pipe', 'band')
All inputs are finite; a program needn't handle non-finite values.
Results may differ from a plain program's by a relative error of at most 0.008.
Values may be sent and summed in bfloat16 or wider, within the bound.
No kernel may reach another device: no remote copies, remote signals or barrier semaphores. Data moves between devices by JAX's collectives and lax.ppermute only.
A program may use at most 192 MiB of HBM per device.

v0:
```python
import jax
import jax.numpy as jnp
from jax import lax
from jax.sharding import PartitionSpec as P

TICKS = 2


def passed_along(block, axis, distance):
    devices = range(lax.axis_size(axis))
    route = [((i - distance) % len(devices), i) for i in devices]
    return lax.ppermute(block, axis, route)


def source_blocks(offsets, list_table, line_block):
    block_count = list_table.shape[0]
    return (
        jnp.arange(block_count, dtype=jnp.int32)[:, None] + offsets[line_block] + list_table
    ) % block_count


def along_rows(values, weights, offsets, list_table, line_block):
    block_count = list_table.shape[0]
    block_width = weights.shape[-1]
    shifted = source_blocks(offsets, list_table, line_block)
    blocked = values.reshape(values.shape[0], block_count, block_width, values.shape[-1])
    picked = blocked[:, shifted]
    chosen = weights[line_block]
    output = jnp.einsum("qtab,lqtbc->lqac", chosen, picked, preferred_element_type=jnp.float32)
    return output.reshape(values.shape)


def along_columns(values, weights, offsets, list_table, line_block):
    block_count = list_table.shape[0]
    block_width = weights.shape[-1]
    shifted = source_blocks(offsets, list_table, line_block)
    blocked = values.reshape(block_count, block_width, values.shape[1], values.shape[2])
    picked = blocked[shifted]
    chosen = weights[line_block]
    output = jnp.einsum("qtab,qtbwc->qawc", chosen, picked, preferred_element_type=jnp.float32)
    return output.reshape(values.shape)


def one_step(memory_state, blocks, offsets, list_table, mixing, line_block):
    channels = memory_state.shape[-1]
    rounded = memory_state.astype(jnp.bfloat16)
    sheared_one = along_rows(rounded, blocks[0], offsets[0], list_table[0], line_block).astype(
        jnp.bfloat16
    )
    turned = lax.all_to_all(sheared_one, "band", split_axis=1, concat_axis=0, tiled=True)
    shorn_rows = along_columns(turned, blocks[1], offsets[1], list_table[1], line_block).astype(
        jnp.bfloat16
    )
    sheared_two = lax.all_to_all(shorn_rows, "band", split_axis=0, concat_axis=1, tiled=True)
    sheared_three = along_rows(
        sheared_two, blocks[2], offsets[2], list_table[2], line_block
    ).astype(jnp.bfloat16)
    mixed_term = jnp.dot(
        sheared_three.reshape(-1, channels), mixing, preferred_element_type=jnp.float32
    )
    return memory_state + mixed_term.reshape(memory_state.shape)


def on_device(memory, shear_blocks, shear_offsets, block_lists, mix_weight):
    row_count = memory.shape[1]
    block_width = shear_blocks.shape[-1]
    line_block = lax.axis_index("band") * row_count // block_width
    memory_state = memory[0]
    blocks = shear_blocks[0]
    offsets = shear_offsets[0]
    list_table = block_lists[0]
    mixing = mix_weight[0]
    for window_step in range(TICKS):
        result = one_step(memory_state, blocks, offsets, list_table, mixing, line_block)
        memory_state = passed_along(result, "pipe", 1)
    return memory_state[None]


def solution(mesh):
    return jax.shard_map(
        on_device,
        mesh=mesh,
        in_specs=(
            P("pipe", "band", None, None),
            P("pipe", None, None, None, None, None, None),
            P("pipe", None, None),
            P("pipe", None, None, None),
            P("pipe", None, None),
        ),
        out_specs=P("pipe", "band", None, None),
        check_vma=False,
    )
```

profile of v0, /device:TPU:1, one launch (start us, length us, event | category | flops | bytes accessed | tf_op | source)
XLA Modules:
  0.0 1656.3 jit_solution(17067395586670115867)
XLA Ops:
  4.7 9.2 convert_element_type.62
  14.0 6.4 broadcast.244.clone
  20.3 34.4 %while.6 = (s32[]{:T(128)}, bf16[64,4,128,128]{3,2,1,0:T(8,128)(2,1)}, s32[8,1]{0,1:T(1,128)S(1)}, bf16[8,64,128,128]{3,2,1,0:T(8,128)(2,1)}, s32[]{:T(128)}) while((s32[]{:T(128)}, bf16[64,4,128,128]{3,2,1,0:T(8,128)(2,1)}, s32[8,1]{0,1:T(1,128)S(1)}, bf16[8,64,128,128]{3,2,1,0:T(8,128)(2,1)}, s32[]{:T(128)}) %tuple.97), condition=%wide.while_cond, body=%wide.while_body.sunk | while | flops 2 | bytes 4195401 | solution.py:27
  20.9 3.7 bitcast_dynamic-update-slice_fusion.8
  25.2 3.7 bitcast_dynamic-update-slice_fusion.8
  29.5 3.7 bitcast_dynamic-update-slice_fusion.8
  56.5 11.5 fusion.16
  68.0 10.5 copy.51
  78.5 12.0 copy.52
  90.5 6.7 all-to-all-start
  97.4 182.0 %all-to-all-done = bf16[64,512,128]{2,0,1:T(8,128)(2,1)} async-done(((bf16[64,512,128]{2,0,1:T(8,128)(2,1)}), bf16[64,512,128]{2,0,1:T(8,128)(2,1)}, u32[]{:S(2)}, u32[]{:S(2)}) %all-to-all-start) | async-done | bytes 8388640 | tf_op jit(solution)/shard_map/all_to_all | solution.py:50
  279.4 12.0 copy.54
  291.5 6.4 broadcast.251.clone
  297.8 34.6 %while.7 = (s32[]{:T(128)}, bf16[4,128,64,128]{3,2,1,0:T(8,128)(2,1)}, s32[8,1]{0,1:T(1,128)S(1)}, bf16[8,128,64,128]{3,2,1,0:T(8,128)(2,1)}, s32[]{:T(128)}) while((s32[]{:T(128)}, bf16[4,128,64,128]{3,2,1,0:T(8,128)(2,1)}, s32[8,1]{0,1:T(1,128)S(1)}, bf16[8,128,64,128]{3,2,1,0:T(8,128)(2,1)}, s32[]{:T(128)}) %tuple.100), condition=%wide.while_cond.1, body=%wide.while_body.1.sunk | while | flops 2 | bytes 4195401 | solution.py:38
  332.4 20.2 %bitcast_convert_fusion.4 = bf16[4,128,64,128]{3,1,2,0:T(8,128)(2,1)} fusion(bf16[4,2,128,64,128]{4,3,2,1,0:T(8,128)(2,1)} %bitcast.179, bf16[1,1,4,4,2,128,128]{6,5,4,3,2,1,0:T(8,128)(2,1)S(1)} %copy-done.3, s32[]{:T(128)S(6)} %select_n.94), kind=kOutput, calls=%fused_computation.22 | convolution fusion | flops 2151677952 | bytes 25427972 | tf_op jit(solution)/shard_map/qtab,qtbwc->qawc/dot_general | solution.py:40
  352.7 22.2 %copy.57 = bf16[4,128,64,128]{3,2,1,0:T(8,128)(2,1)} copy(bf16[4,128,64,128]{3,1,2,0:T(8,128)(2,1)} %bitcast_convert_fusion.4) | data formatting | bytes 16777216 | tf_op jit(solution)/shard_map/convert_element_type | solution.py:51
  374.9 5.0 all-to-all-start.1
  380.1 181.1 %all-to-all-done.1 = bf16[512,64,128]{2,1,0:T(8,128)(2,1)} async-done(((bf16[512,64,128]{2,1,0:T(8,128)(2,1)}), bf16[512,64,128]{2,1,0:T(8,128)(2,1)}, u32[]{:S(2)}, u32[]{:S(2)}) %all-to-all-start.1) | async-done | bytes 8388640 | tf_op jit(solution)/shard_map/all_to_all | solution.py:54
  561.3 9.6 copy.58
  570.9 6.4 broadcast.244.clone.1
  577.3 34.2 %while.8 = (s32[]{:T(128)}, bf16[64,4,128,128]{3,2,1,0:T(8,128)(2,1)}, s32[8,1]{0,1:T(1,128)S(1)}, bf16[8,64,128,128]{3,2,1,0:T(8,128)(2,1)}, s32[]{:T(128)}) while((s32[]{:T(128)}, bf16[64,4,128,128]{3,2,1,0:T(8,128)(2,1)}, s32[8,1]{0,1:T(1,128)S(1)}, bf16[8,64,128,128]{3,2,1,0:T(8,128)(2,1)}, s32[]{:T(128)}) %tuple.101), condition=%wide.while_cond.2, body=%wide.while_body.2.sunk | while | flops 2 | bytes 4195401 | solution.py:27
  611.5 11.4 fusion.17
  622.8 10.3 copy.61
  633.2 16.7 %bitcast_add_fusion = f32[64,512,128]{2,1,0:T(8,128)} fusion(f32[1,64,512,128]{3,2,1,0:T(8,128)} %param.5, bf16[64,512,128]{2,1,0:T(8,128)(2,1)} %bitcast.195, bf16[1,128,128]{2,1,0:T(8,128)(2,1)S(1)} %copy-done), kind=kOutput, calls=%fused_computation.26 | convolution fusion | flops 1077936128 | bytes 41975808 | tf_op jit(solution)/shard_map/dot_general | solution.py:58
  649.8 3.8 collective-permute-start
  653.7 180.6 %collective-permute-done = f32[64,512,128]{2,1,0:T(8,128)} collective-permute-done((f32[64,512,128]{2,1,0:T(8,128)}, f32[64,512,128]{2,1,0:T(8,128)}, u32[]{:S(2)}, u32[]{:S(2)}) %collective-permute-start) | collective-permute-done | bytes 16777248 | tf_op jit(solution)/shard_map/ppermute | solution.py:12
  834.3 9.6 convert_element_type.72
  843.9 6.4 broadcast.244.clone.2
  850.2 35.0 %while.9 = (s32[]{:T(128)}, bf16[64,4,128,128]{3,2,1,0:T(8,128)(2,1)}, s32[8,1]{0,1:T(1,128)S(1)}, bf16[8,64,128,128]{3,2,1,0:T(8,128)(2,1)}, s32[]{:T(128)}) while((s32[]{:T(128)}, bf16[64,4,128,128]{3,2,1,0:T(8,128)(2,1)}, s32[8,1]{0,1:T(1,128)S(1)}, bf16[8,64,128,128]{3,2,1,0:T(8,128)(2,1)}, s32[]{:T(128)}) %tuple.102), condition=%wide.while_cond.3, body=%wide.while_body.3.sunk | while | flops 2 | bytes 4195401 | solution.py:27
  850.8 3.8 bitcast_dynamic-update-slice_fusion.10
  855.2 3.8 bitcast_dynamic-update-slice_fusion.10
  859.6 3.8 bitcast_dynamic-update-slice_fusion.10
  863.9 3.8 bitcast_dynamic-update-slice_fusion.10
  868.3 3.8 bitcast_dynamic-update-slice_fusion.10
  872.7 3.8 bitcast_dynamic-update-slice_fusion.10
  877.1 3.8 bitcast_dynamic-update-slice_fusion.10
  881.4 3.8 bitcast_dynamic-update-slice_fusion.10
  885.2 11.5 fusion.18
  896.7 10.5 copy.63
  907.2 12.0 copy.64
  919.3 5.2 all-to-all-start.2
  924.5 181.8 %all-to-all-done.2 = bf16[64,512,128]{2,0,1:T(8,128)(2,1)} async-done(((bf16[64,512,128]{2,0,1:T(8,128)(2,1)}), bf16[64,512,128]{2,0,1:T(8,128)(2,1)}, u32[]{:S(2)}, u32[]{:S(2)}) %all-to-all-start.2) | async-done | bytes 8388640 | tf_op jit(solution)/shard_map/all_to_all | solution.py:50
  1106.2 12.0 copy.66
  1118.3 6.4 broadcast.251
  1124.6 33.6 %while.10 = (s32[]{:T(128)}, bf16[4,128,64,128]{3,2,1,0:T(8,128)(2,1)}, s32[8,1]{0,1:T(1,128)S(1)}, bf16[8,128,64,128]{3,2,1,0:T(8,128)(2,1)}, s32[]{:T(128)}) while((s32[]{:T(128)}, bf16[4,128,64,128]{3,2,1,0:T(8,128)(2,1)}, s32[8,1]{0,1:T(1,128)S(1)}, bf16[8,128,64,128]{3,2,1,0:T(8,128)(2,1)}, s32[]{:T(128)}) %tuple.103), condition=%wide.while_cond.4, body=%wide.while_body.4.sunk | while | flops 2 | bytes 4195401 | solution.py:38
  1158.3 20.2 %bitcast_convert_fusion.1 = bf16[4,128,64,128]{3,1,2,0:T(8,128)(2,1)} fusion(bf16[4,2,128,64,128]{4,3,2,1,0:T(8,128)(2,1)} %bitcast.182, bf16[1,1,4,4,2,128,128]{6,5,4,3,2,1,0:T(8,128)(2,1)S(1)} %copy-done.3, s32[]{:T(128)S(6)} %select_n.94), kind=kOutput, calls=%fused_computation.15 | convolution fusion | flops 2151677952 | bytes 25427972 | tf_op jit(solution)/shard_map/qtab,qtbwc->qawc/dot_general | solution.py:40
  1178.5 12.4 copy.68
  1190.9 187.0 %all_to_all.60 = bf16[512,64,128]{2,1,0:T(8,128)(2,1)} all-to-all(bf16[512,64,128]{2,1,0:T(8,128)(2,1)} %bitcast.192), channel_id=1, replica_groups=mesh['pipe'=4,'band'=8] {'band'}, dimensions={0} | all-to-all | bytes 16777216 | tf_op jit(solution)/shard_map/all_to_all | solution.py:54
  1377.9 9.6 copy.69
  1387.6 6.4 broadcast.244
  1393.9 34.4 %while.11 = (s32[]{:T(128)}, bf16[64,4,128,128]{3,2,1,0:T(8,128)(2,1)}, s32[8,1]{0,1:T(1,128)S(1)}, bf16[8,64,128,128]{3,2,1,0:T(8,128)(2,1)}, s32[]{:T(128)}) while((s32[]{:T(128)}, bf16[64,4,128,128]{3,2,1,0:T(8,128)(2,1)}, s32[8,1]{0,1:T(1,128)S(1)}, bf16[8,64,128,128]{3,2,1,0:T(8,128)(2,1)}, s32[]{:T(128)}) %tuple.104), condition=%wide.while_cond.5, body=%wide.while_body.5.sunk | while | flops 2 | bytes 4195401 | solution.py:27
  1394.5 3.7 bitcast_dynamic-update-slice_fusion.11
  1398.8 3.7 bitcast_dynamic-update-slice_fusion.11
  1403.1 3.7 bitcast_dynamic-update-slice_fusion.11
  1407.4 3.7 bitcast_dynamic-update-slice_fusion.11
  1411.7 3.7 bitcast_dynamic-update-slice_fusion.11
  1416.0 3.7 bitcast_dynamic-update-slice_fusion.11
  1420.3 3.7 bitcast_dynamic-update-slice_fusion.11
  1424.5 3.7 bitcast_dynamic-update-slice_fusion.11
  1428.3 11.4 fusion.19
  1439.7 10.4 copy.71
  1450.0 16.6 %convolution_add_fusion = f32[64,512,128]{2,1,0:T(8,128)} fusion(f32[64,512,128]{2,1,0:T(8,128)} %collective-permute-done, bf16[64,512,128]{2,1,0:T(8,128)(2,1)} %bitcast.194, bf16[1,128,128]{2,1,0:T(8,128)(2,1)S(1)} %copy-done), kind=kOutput, calls=%fused_computation.35 | convolution fusion | flops 1077936128 | bytes 41975808 | tf_op jit(solution)/shard_map/dot_general | solution.py:58
  1469.2 180.6 %collective-permute-done.1 = f32[64,512,128]{2,1,0:T(8,128)S(1)} collective-permute-done((f32[64,512,128]{2,1,0:T(8,128)}, f32[64,512,128]{2,1,0:T(8,128)S(1)}, u32[]{:S(2)}, u32[]{:S(2)}) %collective-permute-start.1) | collective-permute-done | bytes 16777248 | tf_op jit(solution)/shard_map/ppermute | solution.py:12
  1649.8 6.2 copy.160
  (100 shorter events, 144.1 us)
Async XLA Ops:
  0.0 633.2 %copy-start = (bf16[1,128,128]{2,1,0:T(8,128)(2,1)S(1)}, bf16[1,128,128]{2,1,0:T(8,128)(2,1)}, u32[]{:S(2)}) copy-start(bf16[1,128,128]{2,1,0:T(8,128)(2,1)} %param.9) | copy-start | bytes 98308
  14.0 40.8 %copy-start.1 = (bf16[1,3,4,4,2,128,128]{6,5,4,3,2,1,0:T(8,128)(2,1)S(1)}, bf16[1,3,4,4,2,128,128]{6,5,4,3,2,1,0:T(8,128)(2,1)}, u32[]{:S(2)}) copy-start(bf16[1,3,4,4,2,128,128]{6,5,4,3,2,1,0:T(8,128)(2,1)} %param.6) | copy-start | bytes 9437188
  90.5 188.9 %all-to-all-start = ((bf16[64,512,128]{2,0,1:T(8,128)(2,1)}), bf16[64,512,128]{2,0,1:T(8,128)(2,1)}, u32[]{:S(2)}, u32[]{:S(2)}) async-start(bf16[64,512,128]{2,0,1:T(8,128)(2,1)} %copy.52), calls=%async_computation | async-start | bytes 16777216 | tf_op jit(solution)/shard_map/all_to_all | solution.py:50
  291.5 41.0 %copy-start.3 = (bf16[1,1,4,4,2,128,128]{6,5,4,3,2,1,0:T(8,128)(2,1)S(1)}, bf16[1,1,4,4,2,128,128]{6,5,4,3,2,1,0:T(8,128)(2,1)}, u32[]{:S(2)}) copy-start(bf16[1,1,4,4,2,128,128]{6,5,4,3,2,1,0:T(8,128)(2,1)} %get-tuple-element.102) | copy-start | bytes 3145732
  374.9 186.4 %all-to-all-start.1 = ((bf16[512,64,128]{2,1,0:T(8,128)(2,1)}), bf16[512,64,128]{2,1,0:T(8,128)(2,1)}, u32[]{:S(2)}, u32[]{:S(2)}) async-start(bf16[512,64,128]{2,1,0:T(8,128)(2,1)} %bitcast.189), calls=%async_computation.1 | async-start | bytes 16777216 | tf_op jit(solution)/shard_map/all_to_all | solution.py:54
  570.9 40.6 %copy-start.2 = (bf16[1,1,4,4,2,128,128]{6,5,4,3,2,1,0:T(8,128)(2,1)S(1)}, bf16[1,1,4,4,2,128,128]{6,5,4,3,2,1,0:T(8,128)(2,1)}, u32[]{:S(2)}) copy-start(bf16[1,1,4,4,2,128,128]{6,5,4,3,2,1,0:T(8,128)(2,1)} %get-tuple-element.101) | copy-start | bytes 3145732
  649.8 184.4 %collective-permute-start = (f32[64,512,128]{2,1,0:T(8,128)}, f32[64,512,128]{2,1,0:T(8,128)}, u32[]{:S(2)}, u32[]{:S(2)}) collective-permute-start(f32[64,512,128]{2,1,0:T(8,128)} %bitcast_add_fusion), channel_id=1, source_target_pairs={{24,0},{0,8},{8,16},{16,24},{25,1},{1,9},{9,17},{17,25},{26,2},{2,... | collective-permute-start | bytes 50331656 | tf_op jit(solution)/shard_map/ppermute | solution.py:12
  919.3 187.0 %all-to-all-start.2 = ((bf16[64,512,128]{2,0,1:T(8,128)(2,1)}), bf16[64,512,128]{2,0,1:T(8,128)(2,1)}, u32[]{:S(2)}, u32[]{:S(2)}) async-start(bf16[64,512,128]{2,0,1:T(8,128)(2,1)} %copy.64), calls=%async_computation.2 | async-start | bytes 16777216 | tf_op jit(solution)/shard_map/all_to_all | solution.py:50
  1466.7 183.1 %collective-permute-start.1 = (f32[64,512,128]{2,1,0:T(8,128)}, f32[64,512,128]{2,1,0:T(8,128)S(1)}, u32[]{:S(2)}, u32[]{:S(2)}) collective-permute-start(f32[64,512,128]{2,1,0:T(8,128)} %convolution_add_fusion), channel_id=1, source_target_pairs={{24,0},{0,8},{8,16},{16,24},{25,1},{1,9},{9,17},{17,25},{26,2},{2,... | collective-permute-start | bytes 50331656 | tf_op jit(solution)/shard_map/ppermute | solution.py:12
where the time goes:
time: 1670 us; the launch traced here: 1660 us
  waiting for transfers between devices  906 us (54%)
  local copies, waits for them, and re-layouts  398 us (24%)
  blocking collectives  187 us (11%)
  matrix products  119 us (7%)
  starting transfers between devices  23.3 us (1%)
  other arithmetic  21.5 us (1%)
    all_to_all x2, waiting for transfers between devices, one_step(): lax.all_to_all(sheared_one, 'band', split_axis=1, concat_axis=0, tiled=True)  364 us
    ppermute x2, waiting for transfers between devices, passed_along(): return lax.ppermute(block, axis, route)  361 us
    gather x96, local copies, waits for them, and re-layouts  206 us
    all_to_all x1, blocking collectives, one_step(): lax.all_to_all(shorn_rows, 'band', split_axis=0, concat_axis=1, tiled=True)  187 us
    all_to_all x1, waiting for transfers between devices, one_step(): lax.all_to_all(shorn_rows, 'band', split_axis=0, concat_axis=1, tiled=True)  181 us
    dot_general x4, matrix products, along_rows(): jnp.einsum('qtab,lqtbc->lqac', chosen, picked, preferred_element_type=jnp...  45.7 us
    convert_element_type x4, local copies, waits for them, and re-layouts, one_step(): along_rows(rounded, blocks[0], offsets[0], list_table[0], line_block)  45.1 us
    unnamed x15, local copies, waits for them, and re-layouts  44.4 us
  transfers between devices with their start and end apart: 5, of which 5 were waited for; matrix products, arithmetic and copies ran while one was open for 0% of the time, Pallas kernels for 0%

commit v1 on v0

v1 whole, which is shorter than its diff:
```python
import jax
import jax.numpy as jnp
from jax import lax
from jax.experimental import pallas as pl
from jax.experimental.pallas import tpu as pltpu
from jax.sharding import Mesh, PartitionSpec as P

TICKS = 2
CHANNEL_CHUNKS = 4
ROW_TILE = 16
AXES = ("lane", "core", "half", "rest")
GROUP = ("core", "rest")
VMEM = pltpu.CompilerParams(vmem_limit_bytes=58 << 20)


def whole(shape):
    return pl.BlockSpec(shape, lambda *_: (0,) * len(shape))


def turn(memory, parts, members):
    rows, width, channels = memory.shape
    each = channels // members // parts

    def body(source, *outs):
        turned = jnp.transpose(source[...].astype(jnp.bfloat16), (2, 0, 1))
        split = turned.reshape(members, parts, each, ROW_TILE, width)
        for part in range(parts):
            outs[part][...] = split[:, part]

    return pl.pallas_call(
        body,
        grid=(rows // ROW_TILE,),
        in_specs=[pl.BlockSpec((ROW_TILE, width, channels), lambda i: (i, 0, 0))],
        out_specs=[pl.BlockSpec((members, each, ROW_TILE, width), lambda i: (0, 0, i, 0))] * parts,
        out_shape=[jax.ShapeDtypeStruct((members, each, rows, width), jnp.bfloat16)] * parts,
        compiler_params=VMEM,
        name="turn",
    )(memory)


def dense(blocks, table, which, shear, transposed):
    lines, outs_count, slots, wide = blocks.shape[2:6]
    size = outs_count * wide

    def body(table_ref, which_ref, source, out):
        line = pl.program_id(0)
        out[...] = jnp.zeros(out.shape, out.dtype)
        for q in range(outs_count):
            for t in range(slots):
                place = table_ref[((which_ref[0] * 3 + shear) * lines + line) * outs_count * slots + q * slots + t]
                start = pl.multiple_of(place * wide, wide)
                block = source[0, 0, 0, q, t]
                fixed = pl.ds(q * wide, wide)
                moved = pl.ds(start, wide)
                if transposed:
                    out[0, moved, fixed] += block.T
                else:
                    out[0, fixed, moved] += block

    return pl.pallas_call(
        body,
        grid_spec=pltpu.PrefetchScalarGridSpec(
            num_scalar_prefetch=2,
            grid=(lines,),
            in_specs=[
                pl.BlockSpec(
                    (1, 1, 1, outs_count, slots, wide, wide),
                    lambda i, table_ref, which_ref: (which_ref[0], shear, i, 0, 0, 0, 0),
                )
            ],
            out_specs=pl.BlockSpec((1, size, size), lambda i, *_: (i, 0, 0)),
        ),
        out_shape=jax.ShapeDtypeStruct((lines, size, size), jnp.bfloat16),
        compiler_params=VMEM,
        name="dense",
    )(table, which, blocks)


def sheared(values, first, second, third, targets, part):
    members, each, rows, width = values.shape
    lines = first.shape[0]
    wide = width // lines
    per = wide // rows
    pair = 2 if each % 2 == 0 else 1
    by_rows = targets is not None
    count = rows // ROW_TILE if by_rows else 1

    def body(source, first_ref, second_ref, third_ref, *refs):
        outs, (one, two) = refs[-2 - count : -2], refs[-2:]
        for ch in range(pair):
            for i in range(lines):
                lhs = source[per * i : per * (i + 1), ch].reshape(wide, width)
                got = jnp.dot(lhs, first_ref[i], preferred_element_type=jnp.float32).astype(jnp.bfloat16)
                for j in range(lines):
                    one[j, i * wide : (i + 1) * wide, ch * wide : (ch + 1) * wide] = got[:, j * wide : (j + 1) * wide]
        for j in range(lines):
            got = jnp.dot(second_ref[j], one[j], preferred_element_type=jnp.float32).astype(jnp.bfloat16)
            for ch in range(pair):
                two[ch, :, j * wide : (j + 1) * wide] = got[:, ch * wide : (ch + 1) * wide]
        for ch in range(pair):
            for i in range(lines):
                lhs = two[ch, i * wide : (i + 1) * wide]
                got = jnp.dot(lhs, third_ref[i], preferred_element_type=jnp.float32).astype(jnp.bfloat16)
                split = got.reshape(per, count, rows // count, width)
                for r in range(count):
                    outs[r][per * i : per * (i + 1), ch] = split[:, r]

    steps = each // pair
    out_each = targets[0].shape[1] if by_rows else each
    base = part * steps if by_rows else 0
    given = [t for t in targets if t is not None] if by_rows and part else []
    out_rows = rows // count
    return pl.pallas_call(
        body,
        grid=(steps,),
        in_specs=[pl.BlockSpec((members, pair, rows, width), lambda c: (0, c, 0, 0))]
        + [whole(first.shape)] * 3
        + [pl.BlockSpec(memory_space=pl.ANY)] * len(given),
        out_specs=[pl.BlockSpec((members, pair, out_rows, width), lambda c: (0, base + c, 0, 0))] * count,
        out_shape=[jax.ShapeDtypeStruct((members, out_each, out_rows, width), jnp.bfloat16)] * count,
        scratch_shapes=[
            pltpu.VMEM((lines, width, pair * wide), jnp.bfloat16),
            pltpu.VMEM((pair, width, width), jnp.bfloat16),
        ],
        input_output_aliases={4 + r: r for r in range(len(given))},
        compiler_params=VMEM,
        name="sheared",
    )(values, first, second, third, *given)


def joined(refs, members):
    return jnp.concatenate([ref[j] for j in range(members) for ref in refs], axis=0)


def mixed(fields, state, mixing):
    parts = len(fields)
    members, each, rows, width = fields[0].shape
    channels = mixing.shape[0]

    def body(*refs):
        mix = refs[2 * parts][...]
        outs = refs[2 * parts + 1 :]
        turned = jnp.swapaxes(joined(refs[:parts], members), 0, 1)
        got = [
            lax.dot_general(mix, turned[l], (((0,), (0,)), ((), ())), preferred_element_type=jnp.float32)
            for l in range(ROW_TILE)
        ]
        back = jnp.swapaxes(jnp.stack([g.astype(jnp.bfloat16) for g in got], 0), 0, 1)
        split = back.reshape(members, parts, each, ROW_TILE, width)
        for k in range(parts):
            total = refs[parts + k][...].astype(jnp.float32) + split[:, k].astype(jnp.float32)
            outs[k][...] = total.astype(jnp.bfloat16)

    block = pl.BlockSpec((members, each, ROW_TILE, width), lambda i: (0, 0, i, 0))
    return pl.pallas_call(
        body,
        grid=(rows // ROW_TILE,),
        in_specs=[block] * (2 * parts) + [whole((channels, channels))],
        out_specs=[block] * parts,
        out_shape=[jax.ShapeDtypeStruct(fields[0].shape, jnp.bfloat16)] * parts,
        compiler_params=VMEM,
        name="mixed",
    )(*fields, *state, mixing)


def finished(field, state, mixing, row_chunk):
    channels, rows, width = field.shape
    parts = len(state)
    members, each = state[0].shape[:2]
    piece = min(width, 128)

    def body(*refs):
        mix = refs[1 + parts][...]
        out = refs[2 + parts]
        turned = jnp.swapaxes(refs[0][...], 0, 1)
        old = jnp.swapaxes(joined(refs[1 : 1 + parts], members), 0, 1)
        for l in range(rows):
            got = lax.dot_general(mix, turned[l], (((0,), (0,)), ((), ())), preferred_element_type=jnp.float32)
            out[l] = (got + old[l].astype(jnp.float32)).astype(jnp.bfloat16).T

    return pl.pallas_call(
        body,
        grid=(width // piece,),
        in_specs=[pl.BlockSpec((channels, rows, piece), lambda i: (0, 0, i))]
        + [pl.BlockSpec((members, each, rows, piece), lambda i: (0, 0, row_chunk, i))] * parts
        + [whole((channels, channels))],
        out_specs=pl.BlockSpec((rows, piece, channels), lambda i: (0, i, 0)),
        out_shape=jax.ShapeDtypeStruct((rows, width, channels), jnp.bfloat16),
        compiler_params=VMEM,
        name="finished",
    )(field, *state, mixing)


def placed(rows_in, target, row_chunk, shape):
    rows, width, channels = rows_in.shape
    piece = min(width, 128)

    def body(source, *refs):
        refs[-1][...] = source[...].astype(jnp.float32)

    given = [] if target is None else [target]
    return pl.pallas_call(
        body,
        grid=(width // piece,),
        in_specs=[pl.BlockSpec((rows, piece, channels), lambda i: (0, i, 0))]
        + [pl.BlockSpec(memory_space=pl.ANY)] * len(given),
        out_specs=pl.BlockSpec((rows, piece, channels), lambda i: (row_chunk, i, 0)),
        out_shape=jax.ShapeDtypeStruct(shape, jnp.float32),
        input_output_aliases={1: 0} if given else {},
        compiler_params=VMEM,
        name="placed",
    )(rows_in, *given)


def exchanged(values):
    return lax.all_to_all(values, GROUP, split_axis=0, concat_axis=0, tiled=True)


def solution(mesh):
    sections = mesh.shape["pipe"]
    bands = mesh.shape["band"]
    lanes, rest = sections // 2, bands // 2
    fine = Mesh(mesh.devices.reshape(lanes, 2, 2, rest), AXES)

    def flat(pipe, half, place):
        return (pipe * 2 + half) * rest + place

    gather_route = []
    return_route = []
    for lane in range(lanes):
        for core in range(2):
            for half in range(2):
                for place in range(rest):
                    here = flat(lane * 2 + core, half, place)
                    gather_route.append((here, flat(lane * 2 + half, core, place)))
                    owner = (lane * 2 + half + TICKS) % sections
                    return_route.append((here, flat(owner, core, place)))

    def on_device(memory, shear_blocks, shear_offsets, block_lists, mix_weight):
        line_count = shear_blocks.shape[2]
        source = (
            jnp.arange(line_count, dtype=jnp.int32)[None, None, :, None]
            + shear_offsets[0][:, :, None, None]
            + block_lists[0][:, None]
        ) % line_count
        pipe = ("lane", "core")
        all_blocks = lax.all_gather(shear_blocks[0], pipe)
        table = lax.all_gather(source.reshape(-1), pipe).reshape(-1)
        all_mixes = lax.all_gather(mix_weight[0], pipe)
        own = lax.axis_index("lane") * 2 + lax.axis_index("half")

        parts = CHANNEL_CHUNKS
        state = turn(memory[0], parts, bands)
        state = [lax.ppermute(chunk, AXES, gather_route) for chunk in state]
        row_chunks = memory.shape[1] // ROW_TILE
        each = memory.shape[3] // bands
        out_shape = memory.shape[1:]
        for tick in range(TICKS):
            which = ((own + tick) % sections).astype(jnp.int32)[None]
            first = dense(all_blocks, table, which, 0, True)
            second = dense(all_blocks, table, which, 1, False)
            third = dense(all_blocks, table, which, 2, True)
            mixing = lax.dynamic_index_in_dim(all_mixes, which[0], keepdims=False)
            if tick < TICKS - 1:
                fields = []
                for chunk in state:
                    done = sheared(exchanged(chunk), first, second, third, None, 0)[0]
                    fields.append(exchanged(done))
                state = mixed(fields, state, mixing)
            else:
                chunk_shape = (bands, each, ROW_TILE, memory.shape[2])
                targets = [jax.ShapeDtypeStruct(chunk_shape, jnp.bfloat16)] * row_chunks
                for part, chunk in enumerate(state):
                    targets = sheared(exchanged(chunk), first, second, third, targets, part)
                out = None
                for r in range(row_chunks):
                    field = exchanged(targets[r]).reshape(-1, ROW_TILE, memory.shape[2])
                    rows = finished(field, state, mixing, r)
                    rows = lax.ppermute(rows, AXES, return_route)
                    out = placed(rows, out, r, out_shape)
        return out[None]

    return jax.shard_map(
        on_device,
        mesh=fine,
        in_specs=(
            P(("lane", "core"), ("half", "rest"), None, None),
            P(("lane", "core"), None, None, None, None, None, None),
            P(("lane", "core"), None, None),
            P(("lane", "core"), None, None, None),
            P(("lane", "core"), None, None),
        ),
        out_specs=P(("lane", "core"), ("half", "rest"), None, None),
        check_vma=False,
    )
```

time: 1670 us -> 859 us (0.51)
  waiting for transfers between devices: 906 us -> 420 us
  local copies, waits for them, and re-layouts: 398 us -> 9.99 us
  Pallas kernels: 0 us -> 151 us
  matrix products: 119 us -> 0 us
  starting transfers between devices: 23.3 us -> 67.9 us
  other arithmetic: 21.5 us -> 0.81 us
    all_to_all x3 -> x10, waiting for transfers between devices: 545 us -> 83.8 us  [exchanged(): lax.all_to_all(values, GROUP, split_axis=0, concat_axis=0, tiled=True)]
    gather x96 -> x0, local copies, waits for them, and re-layouts: 206 us -> none
    pallas_call x0 -> x24, Pallas kernels: none -> 151 us  [the longest x8 63.3 us: sheared(): pl.pallas_call(body, grid=(steps,), in_specs=[pl.BlockSpec((members, pair...]
    dot_general x8 -> x0, matrix products: 119 us -> none  [the longest x4 45.7 us: along_rows(): jnp.einsum('qtab,lqtbc->lqac', chosen, picked, preferred_element_type=jnp...]
    convert_element_type x8 -> x0, local copies, waits for them, and re-layouts: 100 us -> none  [the longest x4 45.1 us: one_step(): along_rows(rounded, blocks[0], offsets[0], list_table[0], line_block)]
    all_to_all x4 -> x0, local copies, waits for them, and re-layouts: 43.3 us -> none  [the longest x2 24.1 us: one_step(): lax.all_to_all(sheared_one, 'band', split_axis=1, concat_axis=0, tiled=True)]
    unnamed x15 -> x29, local copies, waits for them, and re-layouts: 44.4 us -> 7.98 us
    ppermute x2 -> x8, waiting for transfers between devices: 361 us -> 335 us  [the longest x4 186 us: on_device(): state = [lax.ppermute(chunk, AXES, gather_route) for chunk in state]]
  transfers between devices with their start and end apart: 5 -> 19, of which waited for: 5 -> 13; matrix products, arithmetic and copies ran while one was open for 0% -> 0% of each run, Pallas kernels for 0% -> 15%
where the time goes in v1:
time: 859 us; the launch traced here: 852 us
  waiting for transfers between devices  420 us (49%)
  blocking collectives  189 us (22%)
  Pallas kernels  151 us (18%)
  starting transfers between devices  67.9 us (8%)
  between operations  13.6 us (2%)
  local copies, waits for them, and re-layouts  9.99 us (1%)
    ppermute x4, waiting for transfers between devices, on_device(): state = [lax.ppermute(chunk, AXES, gather_route) for chunk in state]  186 us
    all_to_all x6, blocking collectives, exchanged(): lax.all_to_all(values, GROUP, split_axis=0, concat_axis=0, tiled=True)  179 us
    ppermute x4, waiting for transfers between devices, on_device(): rows = lax.ppermute(rows, AXES, return_route)  149 us
    all_to_all x10, waiting for transfers between devices, exchanged(): lax.all_to_all(values, GROUP, split_axis=0, concat_axis=0, tiled=True)  83.8 us
    pallas_call x8, Pallas kernels, sheared(): pl.pallas_call(body, grid=(steps,), in_specs=[pl.BlockSpec((members, pair...  63.3 us
    all_to_all x10, starting transfers between devices, exchanged(): lax.all_to_all(values, GROUP, split_axis=0, concat_axis=0, tiled=True)  39.8 us
    pallas_call x6, Pallas kernels, dense(): pl.pallas_call(body, grid_spec=pltpu.PrefetchScalarGridSpec(num_scalar_pr...  26.9 us
    pallas_call x4, Pallas kernels, finished(): pl.pallas_call(body, grid=(width // piece,), in_specs=[pl.BlockSpec((chan...  20.6 us
  transfers between devices with their start and end apart: 19, of which 13 were waited for; matrix products, arithmetic and copies ran while one was open for 0% of the time, Pallas kernels for 15%

profile of v1, /device:TPU:1, one launch (start us, length us, event | category | flops | bytes accessed | tf_op | source)
XLA Modules:
  0.0 852.2 jit_solution(2302401502572688807)
XLA Ops:
  7.3 10.6 %turn.1 = (bf16[8,4,64,512]{3,2,1,0:T(8,128)(2,1)}, bf16[8,4,64,512]{3,2,1,0:T(8,128)(2,1)}, bf16[8,4,64,512]{3,2,1,0:T(8,128)(2,1)}, bf16[8,4,64,512]{3,2,1,0:T(8,128)(2,1)}) custom-call(f32[64,512,128]{2,1,0:T(8,128)} %bitcast.18), custom_call_target="tpu_custom_call" | custom-call | tf_op jit(solution)/shard_map/turn/pallas_call | solution.py:30
  17.8 5.6 collective-permute-start
  23.4 46.5 %collective-permute-done.refs_4_ = bf16[8,4,64,512]{3,2,1,0:T(8,128)(2,1)} collective-permute-done((bf16[8,4,64,512]{3,2,1,0:T(8,128)(2,1)}, bf16[8,4,64,512]{3,2,1,0:T(8,128)(2,1)}, u32[]{:S(2)}, u32[]{:S(2)}) %collective-permute-start) | collective-permute-done | bytes 2097184 | tf_op jit(solution)/shard_map/ppermute | solution.py:254
  69.9 3.6 all-to-all-start
  73.5 4.6 collective-permute-start.1
  78.1 46.5 %collective-permute-done.1.refs_5_ = bf16[8,4,64,512]{3,2,1,0:T(8,128)(2,1)} collective-permute-done((bf16[8,4,64,512]{3,2,1,0:T(8,128)(2,1)}, bf16[8,4,64,512]{3,2,1,0:T(8,128)(2,1)}, u32[]{:S(2)}, u32[]{:S(2)}) %collective-permute-start.1) | collective-permute-done | bytes 2097184 | tf_op jit(solution)/shard_map/ppermute | solution.py:254
  124.7 4.3 all-to-all-start.2
  129.0 4.4 collective-permute-start.2
  133.4 46.7 %collective-permute-done.2.refs_6_ = bf16[8,4,64,512]{3,2,1,0:T(8,128)(2,1)} collective-permute-done((bf16[8,4,64,512]{3,2,1,0:T(8,128)(2,1)}, bf16[8,4,64,512]{3,2,1,0:T(8,128)(2,1)}, u32[]{:S(2)}, u32[]{:S(2)}) %collective-permute-start.2) | collective-permute-done | bytes 2097184 | tf_op jit(solution)/shard_map/ppermute | solution.py:254
  180.1 3.6 all-to-all-start.4
  183.7 5.3 collective-permute-start.3
  189.0 46.5 %collective-permute-done.3.refs_7_ = bf16[8,4,64,512]{3,2,1,0:T(8,128)(2,1)} collective-permute-done((bf16[8,4,64,512]{3,2,1,0:T(8,128)(2,1)}, bf16[8,4,64,512]{3,2,1,0:T(8,128)(2,1)}, u32[]{:S(2)}, u32[]{:S(2)}) %collective-permute-start.3) | collective-permute-done | bytes 2097184 | tf_op jit(solution)/shard_map/ppermute | solution.py:254
  235.5 1.3 copy-done.5
  236.8 4.3 all-to-all-start.6
  241.6 4.8 all-gather
  248.2 4.5 dense.8.third_ref
  252.7 4.4 dense.7.second_ref
  257.2 4.5 dense.6.first_ref
  261.7 7.9 sheared.8
  269.6 3.7 all-to-all-start.1
  273.3 7.9 sheared.9
  281.2 18.0 %all-to-all-done.1.refs_0_ = bf16[8,4,64,512]{3,2,1,0:T(8,128)(2,1)S(1)} async-done(((bf16[8,4,64,512]{3,2,1,0:T(8,128)(2,1)}), bf16[8,4,64,512]{3,2,1,0:T(8,128)(2,1)S(1)}, u32[]{:S(2)}, u32[]{:S(2)}) %all-to-all-start.1) | async-done | bytes 2097184 | tf_op jit(solution)/shard_map/all_to_all | solution.py:216
  300.5 4.5 all-to-all-start.3
  305.0 7.9 sheared.10
  312.8 18.2 %all-to-all-done.3.refs_1_ = bf16[8,4,64,512]{3,2,1,0:T(8,128)(2,1)} async-done(((bf16[8,4,64,512]{3,2,1,0:T(8,128)(2,1)}), bf16[8,4,64,512]{3,2,1,0:T(8,128)(2,1)}, u32[]{:S(2)}, u32[]{:S(2)}) %all-to-all-start.3) | async-done | bytes 2097184 | tf_op jit(solution)/shard_map/all_to_all | solution.py:216
  331.0 3.7 all-to-all-start.5
  334.7 7.9 sheared.11
  342.6 18.0 %all-to-all-done.5.refs_2_ = bf16[8,4,64,512]{3,2,1,0:T(8,128)(2,1)S(1)} async-done(((bf16[8,4,64,512]{3,2,1,0:T(8,128)(2,1)}), bf16[8,4,64,512]{3,2,1,0:T(8,128)(2,1)S(1)}, u32[]{:S(2)}, u32[]{:S(2)}) %all-to-all-start.5) | async-done | bytes 2097184 | tf_op jit(solution)/shard_map/all_to_all | solution.py:216
  360.7 1.3 copy-done.8
  362.0 4.5 all-to-all-start.7
  366.4 5.6 all_gather.11
  372.6 19.8 %all-to-all-done.7.refs_3_ = bf16[8,4,64,512]{3,2,1,0:T(8,128)(2,1)} async-done(((bf16[8,4,64,512]{3,2,1,0:T(8,128)(2,1)}), bf16[8,4,64,512]{3,2,1,0:T(8,128)(2,1)}, u32[]{:S(2)}, u32[]{:S(2)}) %all-to-all-start.7) | async-done | bytes 2097184 | tf_op jit(solution)/shard_map/all_to_all | solution.py:216
  392.5 12.9 %mixed.1 = (bf16[8,4,64,512]{3,2,1,0:T(8,128)(2,1)}, bf16[8,4,64,512]{3,2,1,0:T(8,128)(2,1)}, bf16[8,4,64,512]{3,2,1,0:T(8,128)(2,1)}, bf16[8,4,64,512]{3,2,1,0:T(8,128)(2,1)}) custom-call(bf16[8,4,64,512]{3,2,1,0:T(8,128)(2,1)} %copy-done.7, bf16[8,4,64,512]{3,2,1,0:T(8,128)(2,1)} %all-to-all-done.3.refs_1_, bf16[8,4,64,512]{3,2,1,0:T(8,128)(2,1)} %copy-done.8, ...), custom_call_target="tpu_custom_call" | custom-call | tf_op jit(solution)/shard_map/mixed/pallas_call | solution.py:155
  405.4 30.6 %all_to_all.80.source = bf16[8,4,64,512]{3,2,1,0:T(8,128)(2,1)} all-to-all(bf16[8,4,64,512]{3,2,1,0:T(8,128)(2,1)} %get-tuple-element.34.refs_3_), channel_id=1, replica_groups=mesh['lane'=2,'core'=2,'half'=2,'rest'=4] {'core','rest'}, dimensions={0} | all-to-all | bytes 4194304 | tf_op jit(solution)/shard_map/all_to_all | solution.py:216
  436.0 29.5 %all_to_all.81.source = bf16[8,4,64,512]{3,2,1,0:T(8,128)(2,1)} all-to-all(bf16[8,4,64,512]{3,2,1,0:T(8,128)(2,1)S(1)} %copy-done.1), channel_id=1, replica_groups=mesh['lane'=2,'core'=2,'half'=2,'rest'=4] {'core','rest'}, dimensions={0} | all-to-all | bytes 4194304 | tf_op jit(solution)/shard_map/all_to_all | solution.py:216
  465.5 29.4 %all_to_all.82.source = bf16[8,4,64,512]{3,2,1,0:T(8,128)(2,1)} all-to-all(bf16[8,4,64,512]{3,2,1,0:T(8,128)(2,1)S(1)} %copy-done), channel_id=1, replica_groups=mesh['lane'=2,'core'=2,'half'=2,'rest'=4] {'core','rest'}, dimensions={0} | all-to-all | bytes 4194304 | tf_op jit(solution)/shard_map/all_to_all | solution.py:216
  494.9 3.9 all-to-all-start.8
  498.7 4.5 dense.11.third_ref
  503.3 4.5 dense.10.second_ref
  507.7 4.5 dense.9.first_ref
  512.2 7.9 sheared.12
  520.1 7.9 sheared.13
  528.1 8.0 sheared.14
  537.4 7.9 sheared.15
  545.3 30.5 %all_to_all.83 = bf16[8,16,16,512]{3,2,1,0:T(8,128)(2,1)} all-to-all(bf16[8,16,16,512]{3,2,1,0:T(8,128)(2,1)} %get-tuple-element.50), channel_id=1, replica_groups=mesh['lane'=2,'core'=2,'half'=2,'rest'=4] {'core','rest'}, dimensions={0} | all-to-all | bytes 4194304 | tf_op jit(solution)/shard_map/all_to_all | solution.py:216
  575.7 29.5 %all_to_all.84 = bf16[8,16,16,512]{3,2,1,0:T(8,128)(2,1)} all-to-all(bf16[8,16,16,512]{3,2,1,0:T(8,128)(2,1)S(1)} %copy-done.3), channel_id=1, replica_groups=mesh['lane'=2,'core'=2,'half'=2,'rest'=4] {'core','rest'}, dimensions={0} | all-to-all | bytes 4194304 | tf_op jit(solution)/shard_map/all_to_all | solution.py:216
  605.3 29.4 %all_to_all.85 = bf16[8,16,16,512]{3,2,1,0:T(8,128)(2,1)} all-to-all(bf16[8,16,16,512]{3,2,1,0:T(8,128)(2,1)S(1)} %copy-done.2), channel_id=1, replica_groups=mesh['lane'=2,'core'=2,'half'=2,'rest'=4] {'core','rest'}, dimensions={0} | all-to-all | bytes 4194304 | tf_op jit(solution)/shard_map/all_to_all | solution.py:216
  634.7 3.9 all-to-all-start.12
  638.5 5.1 finished.5
  643.7 5.2 finished.6
  648.8 5.2 finished.7
  654.0 4.5 collective-permute-start.7
  658.6 3.5 collective-permute-start.5
  662.1 9.8 %all-to-all-done.12 = bf16[8,16,16,512]{3,2,1,0:T(8,128)(2,1)S(1)} async-done(((bf16[8,16,16,512]{3,2,1,0:T(8,128)(2,1)}), bf16[8,16,16,512]{3,2,1,0:T(8,128)(2,1)S(1)}, u32[]{:S(2)}, u32[]{:S(2)}) %all-to-all-start.12) | async-done | bytes 2097184 | tf_op jit(solution)/shard_map/all_to_all | solution.py:216
  673.2 5.1 finished.4
  678.3 94.2 %collective-permute-done.7.source = bf16[16,512,128]{2,1,0:T(8,128)(2,1)} collective-permute-done((bf16[16,512,128]{2,1,0:T(8,128)(2,1)}, bf16[16,512,128]{2,1,0:T(8,128)(2,1)}, u32[]{:S(2)}, u32[]{:S(2)}) %collective-permute-start.7) | collective-permute-done | bytes 2097184 | tf_op jit(solution)/shard_map/ppermute | solution.py:279
  772.5 4.2 placed.4.refs_0_
  776.7 18.3 %collective-permute-done.6.source = bf16[16,512,128]{2,1,0:T(8,128)(2,1)} collective-permute-done((bf16[16,512,128]{2,1,0:T(8,128)(2,1)}, bf16[16,512,128]{2,1,0:T(8,128)(2,1)}, u32[]{:S(2)}, u32[]{:S(2)}) %collective-permute-start.6) | collective-permute-done | bytes 2097184 | tf_op jit(solution)/shard_map/ppermute | solution.py:279
  795.0 4.2 placed.5.refs_0_
  799.2 18.3 %collective-permute-done.5.source = bf16[16,512,128]{2,1,0:T(8,128)(2,1)} collective-permute-done((bf16[16,512,128]{2,1,0:T(8,128)(2,1)}, bf16[16,512,128]{2,1,0:T(8,128)(2,1)}, u32[]{:S(2)}, u32[]{:S(2)}) %collective-permute-start.5) | collective-permute-done | bytes 2097184 | tf_op jit(solution)/shard_map/ppermute | solution.py:279
  817.4 4.2 placed.6.refs_0_
  821.6 18.2 %collective-permute-done.4.source = bf16[16,512,128]{2,1,0:T(8,128)(2,1)S(1)} collective-permute-done((bf16[16,512,128]{2,1,0:T(8,128)(2,1)}, bf16[16,512,128]{2,1,0:T(8,128)(2,1)S(1)}, u32[]{:S(2)}, u32[]{:S(2)}) %collective-permute-start.4) | collective-permute-done | bytes 2097184 | tf_op jit(solution)/shard_map/ppermute | solution.py:279
  839.8 1.3 copy-done.10
  841.1 4.2 placed.7
  (45 shorter events, 7.6 us)
Async XLA Ops:
  6.5 241.7 %all-gather.3.cloned.1.call-start = ((), (), s32[]{:S(2)}) async-start(), calls=%async_computation.16 | async-start | bytes 15728640 | tf_op jit(solution)/shard_map/all_gather | solution.py:247
  17.8 52.1 %collective-permute-start = (bf16[8,4,64,512]{3,2,1,0:T(8,128)(2,1)}, bf16[8,4,64,512]{3,2,1,0:T(8,128)(2,1)}, u32[]{:S(2)}, u32[]{:S(2)}) collective-permute-start(bf16[8,4,64,512]{3,2,1,0:T(8,128)(2,1)} %get-tuple-element.29), channel_id=1, source_target_pairs={{0,0},{1,1},{2,2},{3,3},{4,8},{5,9},{6,10},{7,11},{8,4},{9,5},{10,... | collective-permute-start | bytes 6291464 | tf_op jit(solution)/shard_map/ppermute | solution.py:254
  69.9 54.7 %all-to-all-start = ((bf16[8,4,64,512]{3,2,1,0:T(8,128)(2,1)}), bf16[8,4,64,512]{3,2,1,0:T(8,128)(2,1)S(1)}, u32[]{:S(2)}, u32[]{:S(2)}) async-start(bf16[8,4,64,512]{3,2,1,0:T(8,128)(2,1)} %collective-permute-done.refs_4_), calls=%async_computation | async-start | bytes 4194304 | tf_op jit(solution)/shard_map/all_to_all | solution.py:216
  73.5 51.2 %collective-permute-start.1 = (bf16[8,4,64,512]{3,2,1,0:T(8,128)(2,1)}, bf16[8,4,64,512]{3,2,1,0:T(8,128)(2,1)}, u32[]{:S(2)}, u32[]{:S(2)}) collective-permute-start(bf16[8,4,64,512]{3,2,1,0:T(8,128)(2,1)} %get-tuple-element.30), channel_id=1, source_target_pairs={{0,0},{1,1},{2,2},{3,3},{4,8},{5,9},{6,10},{7,11},{8,4},{9,5},{10,... | collective-permute-start | bytes 6291464 | tf_op jit(solution)/shard_map/ppermute | solution.py:254
  124.7 4.3 copy-start.4
  124.7 55.4 %all-to-all-start.2 = ((bf16[8,4,64,512]{3,2,1,0:T(8,128)(2,1)}), bf16[8,4,64,512]{3,2,1,0:T(8,128)(2,1)}, u32[]{:S(2)}, u32[]{:S(2)}) async-start(bf16[8,4,64,512]{3,2,1,0:T(8,128)(2,1)} %collective-permute-done.1.refs_5_), calls=%async_computation.2 | async-start | bytes 4194304 | tf_op jit(solution)/shard_map/all_to_all | solution.py:216
  129.0 51.1 %collective-permute-start.2 = (bf16[8,4,64,512]{3,2,1,0:T(8,128)(2,1)}, bf16[8,4,64,512]{3,2,1,0:T(8,128)(2,1)}, u32[]{:S(2)}, u32[]{:S(2)}) collective-permute-start(bf16[8,4,64,512]{3,2,1,0:T(8,128)(2,1)} %get-tuple-element.31), channel_id=1, source_target_pairs={{0,0},{1,1},{2,2},{3,3},{4,8},{5,9},{6,10},{7,11},{8,4},{9,5},{10,... | collective-permute-start | bytes 6291464 | tf_op jit(solution)/shard_map/ppermute | solution.py:254
  180.1 55.4 %all-to-all-start.4 = ((bf16[8,4,64,512]{3,2,1,0:T(8,128)(2,1)}), bf16[8,4,64,512]{3,2,1,0:T(8,128)(2,1)S(1)}, u32[]{:S(2)}, u32[]{:S(2)}) async-start(bf16[8,4,64,512]{3,2,1,0:T(8,128)(2,1)} %collective-permute-done.2.refs_6_), calls=%async_computation.4 | async-start | bytes 4194304 | tf_op jit(solution)/shard_map/all_to_all | solution.py:216
  183.7 57.5 %copy-start.13 = (s32[1,3,4]{2,0,1:T(1,128)S(1)}, s32[1,3,4]{2,0,1:T(1,128)}, u32[]{:S(2)}) copy-start(s32[1,3,4]{2,0,1:T(1,128)} %param.7) | copy-start | bytes 148
  183.7 57.5 %copy-start.12 = (s32[1,3,4,2]{2,3,1,0:T(2,128)S(1)}, s32[1,3,4,2]{2,3,1,0:T(2,128)}, u32[]{:S(2)}) copy-start(s32[1,3,4,2]{2,3,1,0:T(2,128)} %param.8) | copy-start | bytes 292
  183.7 51.8 %collective-permute-start.3 = (bf16[8,4,64,512]{3,2,1,0:T(8,128)(2,1)}, bf16[8,4,64,512]{3,2,1,0:T(8,128)(2,1)}, u32[]{:S(2)}, u32[]{:S(2)}) collective-permute-start(bf16[8,4,64,512]{3,2,1,0:T(8,128)(2,1)} %get-tuple-element.32), channel_id=1, source_target_pairs={{0,0},{1,1},{2,2},{3,3},{4,8},{5,9},{6,10},{7,11},{8,4},{9,5},{10,... | collective-permute-start | bytes 6291464 | tf_op jit(solution)/shard_map/ppermute | solution.py:254
  235.5 1.3 copy-start.5
  236.8 32.7 %all-to-all-start.6 = ((bf16[8,4,64,512]{3,2,1,0:T(8,128)(2,1)}), bf16[8,4,64,512]{3,2,1,0:T(8,128)(2,1)}, u32[]{:S(2)}, u32[]{:S(2)}) async-start(bf16[8,4,64,512]{3,2,1,0:T(8,128)(2,1)} %collective-permute-done.3.refs_7_), calls=%async_computation.6 | async-start | bytes 4194304 | tf_op jit(solution)/shard_map/all_to_all | solution.py:216
  269.6 29.6 %all-to-all-start.1 = ((bf16[8,4,64,512]{3,2,1,0:T(8,128)(2,1)}), bf16[8,4,64,512]{3,2,1,0:T(8,128)(2,1)S(1)}, u32[]{:S(2)}, u32[]{:S(2)}) async-start(bf16[8,4,64,512]{3,2,1,0:T(8,128)(2,1)} %sheared.8), calls=%async_computation.1 | async-start | bytes 4194304 | tf_op jit(solution)/shard_map/all_to_all | solution.py:216
  299.2 1.3 copy-start.7
  300.5 30.5 %all-to-all-start.3 = ((bf16[8,4,64,512]{3,2,1,0:T(8,128)(2,1)}), bf16[8,4,64,512]{3,2,1,0:T(8,128)(2,1)}, u32[]{:S(2)}, u32[]{:S(2)}) async-start(bf16[8,4,64,512]{3,2,1,0:T(8,128)(2,1)} %sheared.9), calls=%async_computation.3 | async-start | bytes 4194304 | tf_op jit(solution)/shard_map/all_to_all | solution.py:216
  331.0 29.7 %all-to-all-start.5 = ((bf16[8,4,64,512]{3,2,1,0:T(8,128)(2,1)}), bf16[8,4,64,512]{3,2,1,0:T(8,128)(2,1)S(1)}, u32[]{:S(2)}, u32[]{:S(2)}) async-start(bf16[8,4,64,512]{3,2,1,0:T(8,128)(2,1)} %sheared.10), calls=%async_computation.5 | async-start | bytes 4194304 | tf_op jit(solution)/shard_map/all_to_all | solution.py:216
  342.6 23.8 %copy-start.11 = (bf16[1,128,128]{2,1,0:T(8,128)(2,1)S(1)}, bf16[1,128,128]{2,1,0:T(8,128)(2,1)}, u32[]{:S(2)}) copy-start(bf16[1,128,128]{2,1,0:T(8,128)(2,1)} %param.9) | copy-start | bytes 98308
  360.7 1.3 copy-start.8
  362.0 30.5 %all-to-all-start.7 = ((bf16[8,4,64,512]{3,2,1,0:T(8,128)(2,1)}), bf16[8,4,64,512]{3,2,1,0:T(8,128)(2,1)}, u32[]{:S(2)}, u32[]{:S(2)}) async-start(bf16[8,4,64,512]{3,2,1,0:T(8,128)(2,1)} %sheared.11), calls=%async_computation.7 | async-start | bytes 4194304 | tf_op jit(solution)/shard_map/all_to_all | solution.py:216
  405.4 30.6 %copy-start.1 = (bf16[8,4,64,512]{3,2,1,0:T(8,128)(2,1)S(1)}, bf16[8,4,64,512]{3,2,1,0:T(8,128)(2,1)}, u32[]{:S(2)}) copy-start(bf16[8,4,64,512]{3,2,1,0:T(8,128)(2,1)} %get-tuple-element.35.refs_2_) | copy-start | bytes 6291460
  436.0 29.5 %copy-start = (bf16[8,4,64,512]{3,2,1,0:T(8,128)(2,1)S(1)}, bf16[8,4,64,512]{3,2,1,0:T(8,128)(2,1)}, u32[]{:S(2)}) copy-start(bf16[8,4,64,512]{3,2,1,0:T(8,128)(2,1)} %get-tuple-element.36.refs_1_) | copy-start | bytes 6291460
  494.9 41.1 %all-to-all-start.8 = ((bf16[8,4,64,512]{3,2,1,0:T(8,128)(2,1)}), bf16[8,4,64,512]{3,2,1,0:T(8,128)(2,1)S(1)}, u32[]{:S(2)}, u32[]{:S(2)}) async-start(bf16[8,4,64,512]{3,2,1,0:T(8,128)(2,1)} %get-tuple-element.33.refs_4_), calls=%async_computation.8 | async-start | bytes 4194304 | tf_op jit(solution)/shard_map/all_to_all | solution.py:216
  536.0 1.3 copy-start.9
  545.3 30.5 %copy-start.3 = (bf16[8,16,16,512]{3,2,1,0:T(8,128)(2,1)S(1)}, bf16[8,16,16,512]{3,2,1,0:T(8,128)(2,1)}, u32[]{:S(2)}) copy-start(bf16[8,16,16,512]{3,2,1,0:T(8,128)(2,1)} %get-tuple-element.51) | copy-start | bytes 6291460
  575.7 29.5 %copy-start.2 = (bf16[8,16,16,512]{3,2,1,0:T(8,128)(2,1)S(1)}, bf16[8,16,16,512]{3,2,1,0:T(8,128)(2,1)}, u32[]{:S(2)}) copy-start(bf16[8,16,16,512]{3,2,1,0:T(8,128)(2,1)} %get-tuple-element.52) | copy-start | bytes 6291460
  634.7 37.2 %all-to-all-start.12 = ((bf16[8,16,16,512]{3,2,1,0:T(8,128)(2,1)}), bf16[8,16,16,512]{3,2,1,0:T(8,128)(2,1)S(1)}, u32[]{:S(2)}, u32[]{:S(2)}) async-start(bf16[8,16,16,512]{3,2,1,0:T(8,128)(2,1)} %get-tuple-element.49), calls=%async_computation.12 | async-start | bytes 4194304 | tf_op jit(solution)/shard_map/all_to_all | solution.py:216
  654.0 118.5 %collective-permute-start.7 = (bf16[16,512,128]{2,1,0:T(8,128)(2,1)}, bf16[16,512,128]{2,1,0:T(8,128)(2,1)}, u32[]{:S(2)}, u32[]{:S(2)}) collective-permute-start(bf16[16,512,128]{2,1,0:T(8,128)(2,1)} %finished.7), channel_id=1, source_target_pairs={{0,16},{1,17},{2,18},{3,19},{4,24},{5,25},{6,26},{7,27},{8,20},{9,... | collective-permute-start | bytes 6291464 | tf_op jit(solution)/shard_map/ppermute | solution.py:279
  658.5 136.4 %collective-permute-start.6 = (bf16[16,512,128]{2,1,0:T(8,128)(2,1)}, bf16[16,512,128]{2,1,0:T(8,128)(2,1)}, u32[]{:S(2)}, u32[]{:S(2)}) collective-permute-start(bf16[16,512,128]{2,1,0:T(8,128)(2,1)} %finished.6), channel_id=1, source_target_pairs={{0,16},{1,17},{2,18},{3,19},{4,24},{5,25},{6,26},{7,27},{8,20},{9,... | collective-permute-start | bytes 6291464 | tf_op jit(solution)/shard_map/ppermute | solution.py:279
  658.6 158.9 %collective-permute-start.5 = (bf16[16,512,128]{2,1,0:T(8,128)(2,1)}, bf16[16,512,128]{2,1,0:T(8,128)(2,1)}, u32[]{:S(2)}, u32[]{:S(2)}) collective-permute-start(bf16[16,512,128]{2,1,0:T(8,128)(2,1)} %finished.5), channel_id=1, source_target_pairs={{0,16},{1,17},{2,18},{3,19},{4,24},{5,25},{6,26},{7,27},{8,20},{9,... | collective-permute-start | bytes 6291464 | tf_op jit(solution)/shard_map/ppermute | solution.py:279
  671.9 1.3 copy-start.6
  678.3 161.5 %collective-permute-start.4 = (bf16[16,512,128]{2,1,0:T(8,128)(2,1)}, bf16[16,512,128]{2,1,0:T(8,128)(2,1)S(1)}, u32[]{:S(2)}, u32[]{:S(2)}) collective-permute-start(bf16[16,512,128]{2,1,0:T(8,128)(2,1)} %finished.4), channel_id=1, source_target_pairs={{0,16},{1,17},{2,18},{3,19},{4,24},{5,25},{6,26},{7,27},{8,20},{9,... | collective-permute-start | bytes 6291464 | tf_op jit(solution)/shard_map/ppermute | solution.py:279
  839.8 1.3 copy-start.10
Sparse Core Ops, SparseCore 0:
  8.9 84.6 all-gather.2

commit v2 on v1

--- a/solution.py
+++ b/solution.py
@@ -6,39 +6,59 @@
 from jax.sharding import Mesh, PartitionSpec as P
 
 TICKS = 2
-CHANNEL_CHUNKS = 4
+FIRST_ENDS = (5, 10, 14, 16)
+LATER_ENDS = (8, 14, 16)
 ROW_TILE = 16
 AXES = ("lane", "core", "half", "rest")
 GROUP = ("core", "rest")
 VMEM = pltpu.CompilerParams(vmem_limit_bytes=58 << 20)
 
 
+def cost(*arrays, products=0):
+    size = sum(a.size * a.dtype.itemsize for a in arrays)
+    return pl.CostEstimate(flops=2 * products, transcendentals=0, bytes_accessed=size)
+
+
 def whole(shape):
     return pl.BlockSpec(shape, lambda *_: (0,) * len(shape))
 
 
-def turn(memory, parts, members):
+def tied(value, *others):
+    return lax.optimization_barrier((value, *others))[0]
+
+
+def starts_of(sizes):
+    return [sum(sizes[:k]) for k in range(len(sizes))]
+
+
+def cut(count, ends):
+    edges = [0] + [count * end // 16 for end in ends]
+    return [high - low for low, high in zip(edges, edges[1:])]
+
+
+def turn(memory, sizes, members):
     rows, width, channels = memory.shape
-    each = channels // members // parts
+    starts = starts_of(sizes)
 
     def body(source, *outs):
         turned = jnp.transpose(source[...].astype(jnp.bfloat16), (2, 0, 1))
-        split = turned.reshape(members, parts, each, ROW_TILE, width)
-        for part in range(parts):
-            outs[part][...] = split[:, part]
+        split = turned.reshape(members, channels // members, ROW_TILE, width)
+        for out, start, size in zip(outs, starts, sizes):
+            out[...] = split[:, start : start + size]
 
     return pl.pallas_call(
         body,
         grid=(rows // ROW_TILE,),
         in_specs=[pl.BlockSpec((ROW_TILE, width, channels), lambda i: (i, 0, 0))],
-        out_specs=[pl.BlockSpec((members, each, ROW_TILE, width), lambda i: (0, 0, i, 0))] * parts,
-        out_shape=[jax.ShapeDtypeStruct((members, each, rows, width), jnp.bfloat16)] * parts,
-        compiler_params=VMEM,
+        out_specs=[pl.BlockSpec((members, size, ROW_TILE, width), lambda i: (0, 0, i, 0)) for size in sizes],
+        out_shape=[jax.ShapeDtypeStruct((members, size, rows, width), jnp.bfloat16) for size in sizes],
+        compiler_params=VMEM,
+        cost_estimate=cost(memory, memory),
         name="turn",
     )(memory)
 
 
-def dense(blocks, table, which, shear, transposed):
+def dense(blocks, table, which, shear, transposed, only):
     lines, outs_count, slots, wide = blocks.shape[2:6]
     size = outs_count * wide
 
@@ -65,25 +85,25 @@
             in_specs=[
                 pl.BlockSpec(
                     (1, 1, 1, outs_count, slots, wide, wide),
-                    lambda i, table_ref, which_ref: (which_ref[0], shear, i, 0, 0, 0, 0),
+                    lambda i, table_ref, which_ref: (0 if only else which_ref[0], shear, i, 0, 0, 0, 0),
                 )
             ],
             out_specs=pl.BlockSpec((1, size, size), lambda i, *_: (i, 0, 0)),
         ),
         out_shape=jax.ShapeDtypeStruct((lines, size, size), jnp.bfloat16),
         compiler_params=VMEM,
+        cost_estimate=pl.CostEstimate(flops=0, transcendentals=0, bytes_accessed=8 * lines * size * size),
         name="dense",
     )(table, which, blocks)
 
 
-def sheared(values, first, second, third, targets, part):
+def sheared(values, first, second, third, targets, start):
     members, each, rows, width = values.shape
     lines = first.shape[0]
     wide = width // lines
     per = wide // rows
-    pair = 2 if each % 2 == 0 else 1
-    by_rows = targets is not None
-    count = rows // ROW_TILE if by_rows else 1
+    pair = 2 if each % 2 == 0 and start % 2 == 0 else 1
+    count = len(targets)
 
     def body(source, first_ref, second_ref, third_ref, *refs):
         outs, (one, two) = refs[-2 - count : -2], refs[-2:]
@@ -105,10 +125,8 @@
                 for r in range(count):
                     outs[r][per * i : per * (i + 1), ch] = split[:, r]
 
-    steps = each // pair
-    out_each = targets[0].shape[1] if by_rows else each
-    base = part * steps if by_rows else 0
-    given = [t for t in targets if t is not None] if by_rows and part else []
+    steps, base = each // pair, start // pair
+    given = targets if start else []
     out_rows = rows // count
     return pl.pallas_call(
         body,
@@ -117,13 +135,14 @@
         + [whole(first.shape)] * 3
         + [pl.BlockSpec(memory_space=pl.ANY)] * len(given),
         out_specs=[pl.BlockSpec((members, pair, out_rows, width), lambda c: (0, base + c, 0, 0))] * count,
-        out_shape=[jax.ShapeDtypeStruct((members, out_each, out_rows, width), jnp.bfloat16)] * count,
+        out_shape=[jax.ShapeDtypeStruct(target.shape, jnp.bfloat16) for target in targets],
         scratch_shapes=[
             pltpu.VMEM((lines, width, pair * wide), jnp.bfloat16),
             pltpu.VMEM((pair, width, width), jnp.bfloat16),
         ],
         input_output_aliases={4 + r: r for r in range(len(given))},
         compiler_params=VMEM,
+        cost_estimate=cost(values, values, first, first, first, products=6 * values.size * width),
         name="sheared",
     )(values, first, second, third, *given)
 
@@ -132,33 +151,37 @@
     return jnp.concatenate([ref[j] for j in range(members) for ref in refs], axis=0)
 
 
-def mixed(fields, state, mixing):
-    parts = len(fields)
-    members, each, rows, width = fields[0].shape
+def mixed(fields, state, mixing, sizes):
+    members, _, rows, width = fields[0].shape
+    starts = starts_of(sizes)
     channels = mixing.shape[0]
+    ends = len(fields), len(fields) + len(state)
 
     def body(*refs):
-        mix = refs[2 * parts][...]
-        outs = refs[2 * parts + 1 :]
-        turned = jnp.swapaxes(joined(refs[:parts], members), 0, 1)
+        mix = refs[ends[1]][...]
+        outs = refs[ends[1] + 1 :]
+        turned = jnp.swapaxes(joined(refs[: ends[0]], members), 0, 1)
         got = [
             lax.dot_general(mix, turned[l], (((0,), (0,)), ((), ())), preferred_element_type=jnp.float32)
             for l in range(ROW_TILE)
         ]
         back = jnp.swapaxes(jnp.stack([g.astype(jnp.bfloat16) for g in got], 0), 0, 1)
-        split = back.reshape(members, parts, each, ROW_TILE, width)
-        for k in range(parts):
-            total = refs[parts + k][...].astype(jnp.float32) + split[:, k].astype(jnp.float32)
-            outs[k][...] = total.astype(jnp.bfloat16)
-
-    block = pl.BlockSpec((members, each, ROW_TILE, width), lambda i: (0, 0, i, 0))
+        total = joined(refs[ends[0] : ends[1]], members).astype(jnp.float32) + back.astype(jnp.float32)
+        split = total.astype(jnp.bfloat16).reshape(members, channels // members, ROW_TILE, width)
+        for out, start, size in zip(outs, starts, sizes):
+            out[...] = split[:, start : start + size]
+
+    def block(size):
+        return pl.BlockSpec((members, size, ROW_TILE, width), lambda i: (0, 0, i, 0))
+
     return pl.pallas_call(
         body,
         grid=(rows // ROW_TILE,),
-        in_specs=[block] * (2 * parts) + [whole((channels, channels))],
-        out_specs=[block] * parts,
-        out_shape=[jax.ShapeDtypeStruct(fields[0].shape, jnp.bfloat16)] * parts,
-        compiler_params=VMEM,
+        in_specs=[block(a.shape[1]) for a in (*fields, *state)] + [whole((channels, channels))],
+        out_specs=[block(size) for size in sizes],
+        out_shape=[jax.ShapeDtypeStruct((members, size, rows, width), jnp.bfloat16) for size in sizes],
+        compiler_params=VMEM,
+        cost_estimate=cost(*fields, *fields, *fields, *state, *state),
         name="mixed",
     )(*fields, *state, mixing)
 
@@ -166,7 +189,7 @@
 def finished(field, state, mixing, row_chunk):
     channels, rows, width = field.shape
     parts = len(state)
-    members, each = state[0].shape[:2]
+    members = state[0].shape[0]
     piece = min(width, 128)
 
     def body(*refs):
@@ -182,11 +205,12 @@
         body,
         grid=(width // piece,),
         in_specs=[pl.BlockSpec((channels, rows, piece), lambda i: (0, 0, i))]
-        + [pl.BlockSpec((members, each, rows, piece), lambda i: (0, 0, row_chunk, i))] * parts
+        + [pl.BlockSpec((members, old.shape[1], rows, piece), lambda i: (0, 0, row_chunk, i)) for old in state]
         + [whole((channels, channels))],
         out_specs=pl.BlockSpec((rows, piece, channels), lambda i: (0, i, 0)),
         out_shape=jax.ShapeDtypeStruct((rows, width, channels), jnp.bfloat16),
         compiler_params=VMEM,
+        cost_estimate=cost(*[field] * 8),
         name="finished",
     )(field, *state, mixing)
 
@@ -208,6 +232,7 @@
         out_shape=jax.ShapeDtypeStruct(shape, jnp.float32),
         input_output_aliases={1: 0} if given else {},
         compiler_params=VMEM,
+        cost_estimate=cost(*[rows_in] * 4),
         name="placed",
     )(rows_in, *given)
 
@@ -244,40 +269,61 @@
             + block_lists[0][:, None]
         ) % line_count
         pipe = ("lane", "core")
+        core, half = lax.axis_index("core"), lax.axis_index("half")
+        own = lax.axis_index("lane") * 2 + half
+        other_blocks = lax.ppermute(shear_blocks[0], "core", [(0, 1), (1, 0)])
+        blocks = jnp.where(core == half, shear_blocks[0], other_blocks)[None]
+        table = lax.all_gather(source.reshape(-1), pipe).reshape(-1)
         all_blocks = lax.all_gather(shear_blocks[0], pipe)
-        table = lax.all_gather(source.reshape(-1), pipe).reshape(-1)
         all_mixes = lax.all_gather(mix_weight[0], pipe)
-        own = lax.axis_index("lane") * 2 + lax.axis_index("half")
-
-        parts = CHANNEL_CHUNKS
-        state = turn(memory[0], parts, bands)
-        state = [lax.ppermute(chunk, AXES, gather_route) for chunk in state]
-        row_chunks = memory.shape[1] // ROW_TILE
-        each = memory.shape[3] // bands
+
+        members, (_, height, width, channels) = bands, memory.shape
+        each = channels // members
+        row_chunks = height // ROW_TILE
         out_shape = memory.shape[1:]
+
+        def room(rows):
+            return jax.ShapeDtypeStruct((members, each, rows, width), jnp.bfloat16)
+
+        def matrices(tick, held):
+            which = ((own + tick) % sections).astype(jnp.int32)[None]
+            only = tick == 0
+            mixing = lax.dynamic_index_in_dim(all_mixes, which[0], keepdims=False)
+            return [dense(held, table, which, k, k != 1, only) for k in range(3)], mixing
+
+        def section_shears(sent, weights, targets, route):
+            starts = starts_of([chunk.shape[1] for chunk in sent])
+            here, full = [], []
+            for k, chunk in enumerate(sent):
+                if route:
+                    chunk = lax.ppermute(tied(chunk, here[-1]) if k else chunk, AXES, gather_route)
+                here.append(chunk)
+                arrived = exchanged(tied(chunk, *targets) if k > 1 else chunk)
+                if k:
+                    targets = sheared(full[-1], *weights, targets, starts[k - 1])
+                    arrived = tied(arrived, *targets)
+                full.append(arrived)
+            return here, sheared(full[-1], *weights, targets, starts[-1])
+
+        sent = turn(memory[0], cut(each, FIRST_ENDS), members)
         for tick in range(TICKS):
-            which = ((own + tick) % sections).astype(jnp.int32)[None]
-            first = dense(all_blocks, table, which, 0, True)
-            second = dense(all_blocks, table, which, 1, False)
-            third = dense(all_blocks, table, which, 2, True)
-            mixing = lax.dynamic_index_in_dim(all_mixes, which[0], keepdims=False)
-            if tick < TICKS - 1:
-                fields = []
-                for chunk in state:
-                    done = sheared(exchanged(chunk), first, second, third, None, 0)[0]
-                    fields.append(exchanged(done))
-                state = mixed(fields, state, mixing)
-            else:
-                chunk_shape = (bands, each, ROW_TILE, memory.shape[2])
-                targets = [jax.ShapeDtypeStruct(chunk_shape, jnp.bfloat16)] * row_chunks
-                for part, chunk in enumerate(state):
-                    targets = sheared(exchanged(chunk), first, second, third, targets, part)
-                out = None
-                for r in range(row_chunks):
-                    field = exchanged(targets[r]).reshape(-1, ROW_TILE, memory.shape[2])
-                    rows = finished(field, state, mixing, r)
-                    rows = lax.ppermute(rows, AXES, return_route)
-                    out = placed(rows, out, r, out_shape)
+            last = tick == TICKS - 1
+            weights, mixing = matrices(tick, all_blocks if tick else blocks)
+            targets = [room(ROW_TILE)] * row_chunks if last else [room(height)]
+            state, targets = section_shears(sent, weights, targets, tick == 0)
+            if not last:
+                sent = mixed([exchanged(targets[0])], state, mixing, cut(each, LATER_ENDS))
+        out, rows = None, None
+        moved = []
+        for r in range(row_chunks):
+            waits = ([rows] if r else []) + (moved[r - 2 : r - 1] if r > 1 else [])
+            field = exchanged(tied(targets[r], *waits) if waits else targets[r])
+            if r > 1 and r == row_chunks - 1:
+                field = tied(field, moved[-1])
+            rows = finished(field.reshape(-1, ROW_TILE, width), state, mixing, r)
+            moved.append(lax.ppermute(rows, AXES, return_route))
+        for r in range(row_chunks):
+            out = placed(moved[r], out, r, out_shape)
         return out[None]
 
     return jax.shard_map(

time: 859 us -> 781 us (0.909)
  blocking collectives: 189 us -> 107 us
    ppermute x8 -> x9, waiting for transfers between devices: 335 us -> 212 us  [the longest x4 137 us: section_shears(): lax.ppermute(tied(chunk, here[-1]) if k else chunk, AXES, gather_route)]
    all_to_all x10, waiting for transfers between devices: 83.8 us -> 200 us  [exchanged(): lax.all_to_all(values, GROUP, split_axis=0, concat_axis=0, tiled=True)]
    all_to_all x6 -> x2, blocking collectives: 179 us -> 83.5 us  [exchanged(): lax.all_to_all(values, GROUP, split_axis=0, concat_axis=0, tiled=True)]
    all_gather x1, blocking collectives: 4.81 us -> 18.3 us  [on_device(): table = lax.all_gather(source.reshape(-1), pipe).reshape(-1)]
    ppermute x8 -> x9, starting transfers between devices: 28 us -> 29.7 us  [the longest x4 16.9 us: section_shears(): lax.ppermute(tied(chunk, here[-1]) if k else chunk, AXES, gather_route)]
    pallas_call x8 -> x7, Pallas kernels: 63.3 us -> 62.7 us  [sheared(): pl.pallas_call(body, grid=(steps,), in_specs=[pl.BlockSpec((members, pair...]
  transfers between devices with their start and end apart: 19 -> 20, of which waited for: 13 -> 13; matrix products, arithmetic and copies ran while one was open for 0% -> 1% of each run, Pallas kernels for 15% -> 15%
where the time goes in v2:
time: 781 us; the launch traced here: 771 us
  waiting for transfers between devices  413 us (53%)
  Pallas kernels  150 us (19%)
  blocking collectives  107 us (14%)
  starting transfers between devices  70.7 us (9%)
  between operations  13.6 us (2%)
  local copies, waits for them, and re-layouts  11.2 us (1%)
    all_to_all x10, waiting for transfers between devices, exchanged(): lax.all_to_all(values, GROUP, split_axis=0, concat_axis=0, tiled=True)  200 us
    ppermute x4, waiting for transfers between devices, section_shears(): lax.ppermute(tied(chunk, here[-1]) if k else chunk, AXES, gather_route)  137 us
    all_to_all x2, blocking collectives, exchanged(): lax.all_to_all(values, GROUP, split_axis=0, concat_axis=0, tiled=True)  83.5 us
    ppermute x4, waiting for transfers between devices, on_device(): moved.append(lax.ppermute(rows, AXES, return_route))  75.1 us
    pallas_call x7, Pallas kernels, sheared(): pl.pallas_call(body, grid=(steps,), in_specs=[pl.BlockSpec((members, pair...  62.7 us
    all_to_all x10, starting transfers between devices, exchanged(): lax.all_to_all(values, GROUP, split_axis=0, concat_axis=0, tiled=True)  41 us
    pallas_call x6, Pallas kernels, dense(): pl.pallas_call(body, grid_spec=pltpu.PrefetchScalarGridSpec(num_scalar_pr...  26.9 us
    pallas_call x4, Pallas kernels, finished(): pl.pallas_call(body, grid=(width // piece,), in_specs=[pl.BlockSpec((chan...  20.8 us
  transfers between devices with their start and end apart: 20, of which 13 were waited for; matrix products, arithmetic and copies ran while one was open for 1% of the time, Pallas kernels for 15%

profile of v2, /device:TPU:1, one launch (start us, length us, event | category | flops | bytes accessed | tf_op | source)
XLA Modules:
  0.0 771.0 jit_solution(17868643237457218913)
XLA Ops:
  6.5 10.5 %turn.1 = (bf16[8,5,64,512]{3,2,1,0:T(8,128)(2,1)}, bf16[8,5,64,512]{3,2,1,0:T(8,128)(2,1)}, bf16[8,4,64,512]{3,2,1,0:T(8,128)(2,1)}, bf16[8,2,64,512]{3,2,1,0:T(8,128)(2,1)}) custom-call(f32[64,512,128]{2,1,0:T(8,128)} %bitcast.22), custom_call_target="tpu_custom_call" | custom-call | bytes 33554432 | tf_op jit(solution)/shard_map/turn/pallas_call | solution.py:49
  17.1 5.6 collective-permute-start
  22.7 57.7 %collective-permute-done.refs_1_ = bf16[8,5,64,512]{3,2,1,0:T(8,128)(2,1)} collective-permute-done((bf16[8,5,64,512]{3,2,1,0:T(8,128)(2,1)}, bf16[8,5,64,512]{3,2,1,0:T(8,128)(2,1)}, u32[]{:S(2)}, u32[]{:S(2)}) %collective-permute-start) | collective-permute-done | bytes 2621472 | tf_op jit(solution)/shard_map/ppermute | solution.py:299
  80.4 4.4 all-to-all-start.1
  84.8 4.1 collective-permute-start.1
  88.9 58.5 %collective-permute-done.1.refs_2_ = bf16[8,5,64,512]{3,2,1,0:T(8,128)(2,1)} collective-permute-done((bf16[8,5,64,512]{3,2,1,0:T(8,128)(2,1)}, bf16[8,5,64,512]{3,2,1,0:T(8,128)(2,1)}, u32[]{:S(2)}, u32[]{:S(2)}) %collective-permute-start.1) | collective-permute-done | bytes 2621472 | tf_op jit(solution)/shard_map/ppermute | solution.py:299
  147.4 4.3 all-to-all-start
  151.8 4.2 collective-permute-start.2
  156.5 18.3 %all-gather = s32[4,1,96]{2,1,0:T(1,128)S(1)} all-gather(s32[1,1,96]{2,1,0:T(1,128)S(1)} %fusion), channel_id=1, replica_groups=mesh['lane'=2,'core'=2,'half'=2,'rest'=4] {'lane','core'}, dimensions={0}, use_global_device_ids=true | all-gather | bytes 1920 | tf_op jit(solution)/shard_map/all_gather | solution.py:276
  176.6 3.9 select_bitcast_fusion.source
  180.5 4.5 dense.6.first_ref
  185.0 4.4 dense.7.second_ref
  189.5 4.5 dense.8.third_ref
  194.0 10.5 %sheared.7.refs_0_ = bf16[8,16,64,512]{3,2,1,0:T(8,128)(2,1)} custom-call(bf16[8,5,64,512]{3,2,1,0:T(8,128)(2,1)} %all-to-all-done.1.source, bf16[4,512,512]{2,1,0:T(8,128)(2,1)} %dense.6.first_ref, bf16[4,512,512]{2,1,0:T(8,128)(2,1)} %dense.7.second_ref, bf16[4,512,512]{2,1,0:T(8,128)(2,1)} %dense.8.third_ref), custom_call_target="tpu_custom_call" | custom-call | flops 8053063680 | bytes 11534336 | tf_op jit(solution)/shard_map/sheared/pallas_call | solution.py:131
  205.0 4.6 all-to-all-start.3
  209.6 2.9 collective-permute-start.3
  212.5 10.6 %sheared.8.refs_0_ = bf16[8,16,64,512]{3,2,1,0:T(8,128)(2,1)} custom-call(bf16[8,5,64,512]{3,2,1,0:T(8,128)(2,1)} %all-to-all-done.source, bf16[4,512,512]{2,1,0:T(8,128)(2,1)} %dense.6.first_ref, bf16[4,512,512]{2,1,0:T(8,128)(2,1)} %dense.7.second_ref, bf16[4,512,512]{2,1,0:T(8,128)(2,1)} %dense.8.third_ref, ...), custom_call_target="tpu_custom_call", output_to_operand_aliasing={{}: (4, {})} | custom-call | flops 8053063680 | bytes 11534336 | tf_op jit(solution)/shard_map/sheared/pallas_call | solution.py:131
  223.1 20.9 %collective-permute-done.3.refs_4_ = bf16[8,2,64,512]{3,2,1,0:T(8,128)(2,1)} collective-permute-done((bf16[8,2,64,512]{3,2,1,0:T(8,128)(2,1)S(1)}, bf16[8,2,64,512]{3,2,1,0:T(8,128)(2,1)}, u32[]{:S(2)}, u32[]{:S(2)}) %collective-permute-start.3) | collective-permute-done | bytes 1048608 | tf_op jit(solution)/shard_map/ppermute | solution.py:299
  244.0 2.7 all-to-all-done.3.source
  246.7 3.7 all-to-all-start.2
  250.4 7.9 %sheared.9.refs_0_ = bf16[8,16,64,512]{3,2,1,0:T(8,128)(2,1)} custom-call(bf16[8,4,64,512]{3,2,1,0:T(8,128)(2,1)} %copy-done.1, bf16[4,512,512]{2,1,0:T(8,128)(2,1)} %dense.6.first_ref, bf16[4,512,512]{2,1,0:T(8,128)(2,1)} %dense.7.second_ref, bf16[4,512,512]{2,1,0:T(8,128)(2,1)} %dense.8.third_ref, ...), custom_call_target="tpu_custom_call", output_to_operand_aliasing={{}: (4, {})} | custom-call | flops 6442450944 | bytes 10485760 | tf_op jit(solution)/shard_map/sheared/pallas_call | solution.py:131
  258.3 6.8 all-to-all-done.2.source
  266.1 6.0 sheared.10
  272.0 5.1 all-to-all-start.4
  277.9 5.4 all_gather.10
  283.9 86.6 %all-to-all-done.4.refs_0_ = bf16[8,16,64,512]{3,2,1,0:T(8,128)(2,1)} async-done(((bf16[8,16,64,512]{3,2,1,0:T(8,128)(2,1)}), bf16[8,16,64,512]{3,2,1,0:T(8,128)(2,1)}, u32[]{:S(2)}, u32[]{:S(2)}) %all-to-all-start.4) | async-done | bytes 8388640 | tf_op jit(solution)/shard_map/all_to_all | solution.py:241
  370.5 12.7 %mixed.1 = (bf16[8,8,64,512]{3,2,1,0:T(8,128)(2,1)}, bf16[8,6,64,512]{3,2,1,0:T(8,128)(2,1)}, bf16[8,2,64,512]{3,2,1,0:T(8,128)(2,1)}) custom-call(bf16[8,16,64,512]{3,2,1,0:T(8,128)(2,1)} %all-to-all-done.4.refs_0_, bf16[8,5,64,512]{3,2,1,0:T(8,128)(2,1)} %collective-permute-done.refs_1_, bf16[8,5,64,512]{3,2,1,0:T(8,128)(2,1)} %collective-permute-done.1.refs_2_, ...), custom_call_target="tpu_custom_call" | custom-call | bytes 41943040 | tf_op jit(solution)/shard_map/mixed/pallas_call | solution.py:177
  383.2 53.1 %all_to_all.60.source = bf16[8,8,64,512]{3,2,1,0:T(8,128)(2,1)} all-to-all(bf16[8,8,64,512]{3,2,1,0:T(8,128)(2,1)} %get-tuple-element.52.refs_1_), channel_id=1, replica_groups=mesh['lane'=2,'core'=2,'half'=2,'rest'=4] {'core','rest'}, dimensions={0} | all-to-all | bytes 8388608 | tf_op jit(solution)/shard_map/all_to_all | solution.py:241
  436.3 3.9 all-to-all-start.7
  440.2 4.5 dense.9.first_ref
  444.7 4.4 dense.10.second_ref
  449.2 4.6 dense.11.third_ref
  453.7 11.8 %sheared.11 = (bf16[8,16,16,512]{3,2,1,0:T(8,128)(2,1)}, bf16[8,16,16,512]{3,2,1,0:T(8,128)(2,1)}, bf16[8,16,16,512]{3,2,1,0:T(8,128)(2,1)}, bf16[8,16,16,512]{3,2,1,0:T(8,128)(2,1)}) custom-call(bf16[8,8,64,512]{3,2,1,0:T(8,128)(2,1)} %all_to_all.60.source, bf16[4,512,512]{2,1,0:T(8,128)(2,1)} %dense.9.first_ref, bf16[4,512,512]{2,1,0:T(8,128)(2,1)} %dense.10.second_ref, ...), custom_call_target="tpu_custom_call" | custom-call | flops 12884901888 | bytes 14680064 | tf_op jit(solution)/shard_map/sheared/pallas_call | solution.py:131
  465.5 11.9 %all-to-all-done.7.source = bf16[8,6,64,512]{3,2,1,0:T(8,128)(2,1)S(1)} async-done(((bf16[8,6,64,512]{3,2,1,0:T(8,128)(2,1)}), bf16[8,6,64,512]{3,2,1,0:T(8,128)(2,1)S(1)}, u32[]{:S(2)}, u32[]{:S(2)}) %all-to-all-start.7) | async-done | bytes 3145760 | tf_op jit(solution)/shard_map/all_to_all | solution.py:241
  477.4 1.6 copy-done.7
  479.0 3.7 all-to-all-start.6
  482.7 9.9 %sheared.12 = (bf16[8,16,16,512]{3,2,1,0:T(8,128)(2,1)}, bf16[8,16,16,512]{3,2,1,0:T(8,128)(2,1)}, bf16[8,16,16,512]{3,2,1,0:T(8,128)(2,1)}, bf16[8,16,16,512]{3,2,1,0:T(8,128)(2,1)}) custom-call(bf16[8,6,64,512]{3,2,1,0:T(8,128)(2,1)} %copy-done.7, ...), custom_call_target="tpu_custom_call", output_to_operand_aliasing={{0}: (4, {}), {1}: (5, {}), {2}: (6, {}), {3}: (7, {})} | custom-call | flops 9663676416 | bytes 12582912 | tf_op jit(solution)/shard_map/sheared/pallas_call | solution.py:131
  492.6 4.8 all-to-all-done.6.source
  497.4 1.0 copy-done.6
  498.4 6.1 sheared.13
  504.5 30.4 %all_to_all.61 = bf16[8,16,16,512]{3,2,1,0:T(8,128)(2,1)} all-to-all(bf16[8,16,16,512]{3,2,1,0:T(8,128)(2,1)} %get-tuple-element.68), channel_id=1, replica_groups=mesh['lane'=2,'core'=2,'half'=2,'rest'=4] {'core','rest'}, dimensions={0} | all-to-all | bytes 4194304 | tf_op jit(solution)/shard_map/all_to_all | solution.py:241
  534.9 5.2 finished.4
  540.1 3.9 all-to-all-start.9
  544.0 1.7 collective-permute-start.5
  545.7 44.5 %all-to-all-done.9 = bf16[8,16,16,512]{3,2,1,0:T(8,128)(2,1)S(1)} async-done(((bf16[8,16,16,512]{3,2,1,0:T(8,128)(2,1)}), bf16[8,16,16,512]{3,2,1,0:T(8,128)(2,1)S(1)}, u32[]{:S(2)}, u32[]{:S(2)}) %all-to-all-start.9) | async-done | bytes 2097184 | tf_op jit(solution)/shard_map/all_to_all | solution.py:241
  590.1 1.4 copy-done.3
  591.5 5.2 finished.5
  596.7 3.7 all-to-all-start.10
  600.4 1.7 collective-permute-start.6
  602.1 42.6 %all-to-all-done.10 = bf16[8,16,16,512]{3,2,1,0:T(8,128)(2,1)S(1)} async-done(((bf16[8,16,16,512]{3,2,1,0:T(8,128)(2,1)}), bf16[8,16,16,512]{3,2,1,0:T(8,128)(2,1)S(1)}, u32[]{:S(2)}, u32[]{:S(2)}) %all-to-all-start.10) | async-done | bytes 2097184 | tf_op jit(solution)/shard_map/all_to_all | solution.py:241
  644.7 1.4 copy-done.4
  646.1 5.2 finished.6
  651.3 3.7 all-to-all-start.11
  655.0 4.6 collective-permute-start.7
  659.6 41.3 %collective-permute-done.7.source = bf16[16,512,128]{2,1,0:T(8,128)(2,1)} collective-permute-done((bf16[16,512,128]{2,1,0:T(8,128)(2,1)}, bf16[16,512,128]{2,1,0:T(8,128)(2,1)}, u32[]{:S(2)}, u32[]{:S(2)}) %collective-permute-start.7) | collective-permute-done | bytes 2097184 | tf_op jit(solution)/shard_map/ppermute | solution.py:324
  700.9 1.3 copy-done.2
  702.2 5.2 finished.7
  707.4 4.8 collective-permute-start.8
  712.2 4.2 placed.4.refs_0_
  716.4 4.2 placed.5.refs_0_
  720.6 4.2 placed.6.refs_0_
  724.8 33.8 %collective-permute-done.8.source = bf16[16,512,128]{2,1,0:T(8,128)(2,1)S(1)} collective-permute-done((bf16[16,512,128]{2,1,0:T(8,128)(2,1)}, bf16[16,512,128]{2,1,0:T(8,128)(2,1)S(1)}, u32[]{:S(2)}, u32[]{:S(2)}) %collective-permute-start.8) | collective-permute-done | bytes 2097184 | tf_op jit(solution)/shard_map/ppermute | solution.py:324
  758.6 1.3 copy-done.8
  760.0 4.2 placed.7
  (41 shorter events, 5.2 us)
Async XLA Ops:
  17.1 63.3 %collective-permute-start = (bf16[8,5,64,512]{3,2,1,0:T(8,128)(2,1)}, bf16[8,5,64,512]{3,2,1,0:T(8,128)(2,1)}, u32[]{:S(2)}, u32[]{:S(2)}) collective-permute-start(bf16[8,5,64,512]{3,2,1,0:T(8,128)(2,1)} %get-tuple-element.42), channel_id=1, source_target_pairs={{0,0},{1,1},{2,2},{3,3},{4,8},{5,9},{6,10},{7,11},{8,4},{9,5},{10,... | collective-permute-start | bytes 7864328 | tf_op jit(solution)/shard_map/ppermute | solution.py:299
  80.4 67.0 %all-to-all-start.1 = ((bf16[8,5,64,512]{3,2,1,0:T(8,128)(2,1)}), bf16[8,5,64,512]{3,2,1,0:T(8,128)(2,1)}, u32[]{:S(2)}, u32[]{:S(2)}) async-start(bf16[8,5,64,512]{3,2,1,0:T(8,128)(2,1)} %collective-permute-done.refs_1_), calls=%async_computation.1 | async-start | bytes 5242880 | tf_op jit(solution)/shard_map/all_to_all | solution.py:241
  84.8 67.0 %copy-start = (bf16[1,3,4,4,2,128,128]{6,5,4,3,2,1,0:T(8,128)(2,1)S(1)}, bf16[1,3,4,4,2,128,128]{6,5,4,3,2,1,0:T(8,128)(2,1)}, u32[]{:S(2)}) copy-start(bf16[1,3,4,4,2,128,128]{6,5,4,3,2,1,0:T(8,128)(2,1)} %param.6) | copy-start | bytes 9437188
  84.8 71.3 %copy-start.10 = (s32[1,3,4,2]{2,3,1,0:T(2,128)S(1)}, s32[1,3,4,2]{2,3,1,0:T(2,128)}, u32[]{:S(2)}) copy-start(s32[1,3,4,2]{2,3,1,0:T(2,128)} %param.8) | copy-start | bytes 292
  84.8 71.4 %copy-start.11 = (s32[1,3,4]{2,0,1:T(1,128)S(1)}, s32[1,3,4]{2,0,1:T(1,128)}, u32[]{:S(2)}) copy-start(s32[1,3,4]{2,0,1:T(1,128)} %param.7) | copy-start | bytes 148
  84.8 62.6 %collective-permute-start.1 = (bf16[8,5,64,512]{3,2,1,0:T(8,128)(2,1)}, bf16[8,5,64,512]{3,2,1,0:T(8,128)(2,1)}, u32[]{:S(2)}, u32[]{:S(2)}) collective-permute-start(bf16[8,5,64,512]{3,2,1,0:T(8,128)(2,1)} %get-tuple-element.43), channel_id=1, source_target_pairs={{0,0},{1,1},{2,2},{3,3},{4,8},{5,9},{6,10},{7,11},{8,4},{9,5},{10,... | collective-permute-start | bytes 7864328 | tf_op jit(solution)/shard_map/ppermute | solution.py:299
  147.4 57.6 %all-to-all-start = ((bf16[8,5,64,512]{3,2,1,0:T(8,128)(2,1)}), bf16[8,5,64,512]{3,2,1,0:T(8,128)(2,1)}, u32[]{:S(2)}, u32[]{:S(2)}) async-start(bf16[8,5,64,512]{3,2,1,0:T(8,128)(2,1)} %collective-permute-done.1.refs_2_), calls=%async_computation | async-start | bytes 5242880 | tf_op jit(solution)/shard_map/all_to_all | solution.py:241
  151.8 24.9 %collective-permute-start.4 = (bf16[3,4,4,2,128,128]{5,4,3,2,1,0:T(8,128)(2,1)S(1)}, bf16[3,4,4,2,128,128]{5,4,3,2,1,0:T(8,128)(2,1)}, u32[]{:S(2)}, u32[]{:S(2)}) collective-permute-start(bf16[3,4,4,2,128,128]{5,4,3,2,1,0:T(8,128)(2,1)S(1)} %bitcast.23), channel_id=1, source_target_pairs={{0,8},{8,0},{1,9},{9,1},{2,10},{10,2},{3,11},{11,3},{4,12},{12,4},... | collective-permute-start | bytes 9437192 | tf_op jit(solution)/shard_map/ppermute | solution.py:274
  151.8 52.6 %collective-permute-start.2 = (bf16[8,4,64,512]{3,2,1,0:T(8,128)(2,1)}, bf16[8,4,64,512]{3,2,1,0:T(8,128)(2,1)}, u32[]{:S(2)}, u32[]{:S(2)}) collective-permute-start(bf16[8,4,64,512]{3,2,1,0:T(8,128)(2,1)} %get-tuple-element.44), channel_id=1, source_target_pairs={{0,0},{1,1},{2,2},{3,3},{4,8},{5,9},{6,10},{7,11},{8,4},{9,5},{10,... | collective-permute-start | bytes 6291464 | tf_op jit(solution)/shard_map/ppermute | solution.py:299
  204.5 5.1 copy-start.12
  205.0 41.7 %all-to-all-start.3 = ((bf16[8,4,64,512]{3,2,1,0:T(8,128)(2,1)}), bf16[8,4,64,512]{3,2,1,0:T(8,128)(2,1)S(1)}, u32[]{:S(2)}, u32[]{:S(2)}) async-start(bf16[8,4,64,512]{3,2,1,0:T(8,128)(2,1)} %collective-permute-done.2.refs_3_), calls=%async_computation.3 | async-start | bytes 4194304 | tf_op jit(solution)/shard_map/all_to_all | solution.py:241
  209.6 34.5 %collective-permute-start.3 = (bf16[8,2,64,512]{3,2,1,0:T(8,128)(2,1)S(1)}, bf16[8,2,64,512]{3,2,1,0:T(8,128)(2,1)}, u32[]{:S(2)}, u32[]{:S(2)}) collective-permute-start(bf16[8,2,64,512]{3,2,1,0:T(8,128)(2,1)S(1)} %copy-done.12), channel_id=1, source_target_pairs={{0,0},{1,1},{2,2},{3,3},{4,8},{5,9},{6,10},{7,11},{8,4},{9,5},{10,... | collective-permute-start | bytes 3145736 | tf_op jit(solution)/shard_map/ppermute | solution.py:299
  246.7 3.7 copy-start.1
  246.7 18.4 %all-to-all-start.2 = ((bf16[8,2,64,512]{3,2,1,0:T(8,128)(2,1)}), bf16[8,2,64,512]{3,2,1,0:T(8,128)(2,1)S(1)}, u32[]{:S(2)}, u32[]{:S(2)}) async-start(bf16[8,2,64,512]{3,2,1,0:T(8,128)(2,1)} %collective-permute-done.3.refs_4_), calls=%async_computation.2 | async-start | bytes 2097152 | tf_op jit(solution)/shard_map/all_to_all | solution.py:241
  265.1 1.0 copy-start.5
  272.0 98.5 %all-to-all-start.4 = ((bf16[8,16,64,512]{3,2,1,0:T(8,128)(2,1)}), bf16[8,16,64,512]{3,2,1,0:T(8,128)(2,1)}, u32[]{:S(2)}, u32[]{:S(2)}) async-start(bf16[8,16,64,512]{3,2,1,0:T(8,128)(2,1)} %sheared.10), calls=%async_computation.4 | async-start | bytes 16777216 | tf_op jit(solution)/shard_map/all_to_all | solution.py:241
  277.1 0.8 copy-start.9
  277.1 163.1 %all-gather.3.cloned.1.call-start = ((), (), s32[]{:S(2)}) async-start(), calls=%async_computation.12 | async-start | bytes 15728640 | tf_op jit(solution)/shard_map/all_gather | solution.py:277
  436.3 41.1 %all-to-all-start.7 = ((bf16[8,6,64,512]{3,2,1,0:T(8,128)(2,1)}), bf16[8,6,64,512]{3,2,1,0:T(8,128)(2,1)S(1)}, u32[]{:S(2)}, u32[]{:S(2)}) async-start(bf16[8,6,64,512]{3,2,1,0:T(8,128)(2,1)} %get-tuple-element.58.refs_2_), calls=%async_computation.7 | async-start | bytes 6291456 | tf_op jit(solution)/shard_map/all_to_all | solution.py:241
  477.4 1.6 copy-start.7
  479.0 18.4 %all-to-all-start.6 = ((bf16[8,2,64,512]{3,2,1,0:T(8,128)(2,1)}), bf16[8,2,64,512]{3,2,1,0:T(8,128)(2,1)S(1)}, u32[]{:S(2)}, u32[]{:S(2)}) async-start(bf16[8,2,64,512]{3,2,1,0:T(8,128)(2,1)} %get-tuple-element.57.refs_3_), calls=%async_computation.6 | async-start | bytes 2097152 | tf_op jit(solution)/shard_map/all_to_all | solution.py:241
  497.4 1.0 copy-start.6
  540.1 50.0 %all-to-all-start.9 = ((bf16[8,16,16,512]{3,2,1,0:T(8,128)(2,1)}), bf16[8,16,16,512]{3,2,1,0:T(8,128)(2,1)S(1)}, u32[]{:S(2)}, u32[]{:S(2)}) async-start(bf16[8,16,16,512]{3,2,1,0:T(8,128)(2,1)} %get-tuple-element.69), calls=%async_computation.9 | async-start | bytes 4194304 | tf_op jit(solution)/shard_map/all_to_all | solution.py:241
  544.0 52.7 %collective-permute-start.5 = (bf16[16,512,128]{2,1,0:T(8,128)(2,1)}, bf16[16,512,128]{2,1,0:T(8,128)(2,1)}, u32[]{:S(2)}, u32[]{:S(2)}) collective-permute-start(bf16[16,512,128]{2,1,0:T(8,128)(2,1)} %finished.4), channel_id=1, source_target_pairs={{0,16},{1,17},{2,18},{3,19},{4,24},{5,25},{6,26},{7,27},{8,20},{9,... | collective-permute-start | bytes 6291464 | tf_op jit(solution)/shard_map/ppermute | solution.py:324
  590.1 1.4 copy-start.3
  596.7 48.0 %all-to-all-start.10 = ((bf16[8,16,16,512]{3,2,1,0:T(8,128)(2,1)}), bf16[8,16,16,512]{3,2,1,0:T(8,128)(2,1)S(1)}, u32[]{:S(2)}, u32[]{:S(2)}) async-start(bf16[8,16,16,512]{3,2,1,0:T(8,128)(2,1)} %get-tuple-element.70), calls=%async_computation.10 | async-start | bytes 4194304 | tf_op jit(solution)/shard_map/all_to_all | solution.py:241
  600.4 50.9 %collective-permute-start.6 = (bf16[16,512,128]{2,1,0:T(8,128)(2,1)}, bf16[16,512,128]{2,1,0:T(8,128)(2,1)}, u32[]{:S(2)}, u32[]{:S(2)}) collective-permute-start(bf16[16,512,128]{2,1,0:T(8,128)(2,1)} %finished.5), channel_id=1, source_target_pairs={{0,16},{1,17},{2,18},{3,19},{4,24},{5,25},{6,26},{7,27},{8,20},{9,... | collective-permute-start | bytes 6291464 | tf_op jit(solution)/shard_map/ppermute | solution.py:324
  644.7 1.4 copy-start.4
  651.3 49.6 %all-to-all-start.11 = ((bf16[8,16,16,512]{3,2,1,0:T(8,128)(2,1)}), bf16[8,16,16,512]{3,2,1,0:T(8,128)(2,1)S(1)}, u32[]{:S(2)}, u32[]{:S(2)}) async-start(bf16[8,16,16,512]{3,2,1,0:T(8,128)(2,1)} %get-tuple-element.71), calls=%async_computation.11 | async-start | bytes 4194304 | tf_op jit(solution)/shard_map/all_to_all | solution.py:241
  655.0 45.8 %collective-permute-start.7 = (bf16[16,512,128]{2,1,0:T(8,128)(2,1)}, bf16[16,512,128]{2,1,0:T(8,128)(2,1)}, u32[]{:S(2)}, u32[]{:S(2)}) collective-permute-start(bf16[16,512,128]{2,1,0:T(8,128)(2,1)} %finished.6), channel_id=1, source_target_pairs={{0,16},{1,17},{2,18},{3,19},{4,24},{5,25},{6,26},{7,27},{8,20},{9,... | collective-permute-start | bytes 6291464 | tf_op jit(solution)/shard_map/ppermute | solution.py:324
  700.9 1.3 copy-start.2
  707.4 51.2 %collective-permute-start.8 = (bf16[16,512,128]{2,1,0:T(8,128)(2,1)}, bf16[16,512,128]{2,1,0:T(8,128)(2,1)S(1)}, u32[]{:S(2)}, u32[]{:S(2)}) collective-permute-start(bf16[16,512,128]{2,1,0:T(8,128)(2,1)} %finished.7), channel_id=1, source_target_pairs={{0,16},{1,17},{2,18},{3,19},{4,24},{5,25},{6,26},{7,27},{8,20},{9,... | collective-permute-start | bytes 6291464 | tf_op jit(solution)/shard_map/ppermute | solution.py:324
  758.6 1.3 copy-start.8
Sparse Core Ops, SparseCore 0:
  279.5 81.9 all-gather.2

commit v3 on v2

v3 whole, which is shorter than its diff:
```python
import jax
import jax.numpy as jnp
from jax import lax
from jax.experimental import pallas as pl
from jax.experimental.pallas import tpu as pltpu
from jax.sharding import Mesh, PartitionSpec as P

TICKS = 2
ENDS = (4, 8, 12, 16)
ROW_TILE = 16
AXES = ("lane", "core", "half", "rest")
GROUP = ("core", "rest")
VMEM = pltpu.CompilerParams(vmem_limit_bytes=58 << 20)


def cost(*arrays, products=0):
    size = sum(a.size * a.dtype.itemsize for a in arrays)
    return pl.CostEstimate(flops=2 * products, transcendentals=0, bytes_accessed=size)


def whole(shape):
    return pl.BlockSpec(shape, lambda *_: (0,) * len(shape))


def tied(value, *others):
    return lax.optimization_barrier((value, *others))[0]


def starts_of(sizes):
    return [sum(sizes[:k]) for k in range(len(sizes))]


def cut(count, ends):
    edges = [0] + [count * end // 16 for end in ends]
    return [high - low for low, high in zip(edges, edges[1:])]


def spread(memory, sizes, members, band):
    rows, width, channels = memory.shape
    each = channels // members
    starts = starts_of(sizes)

    def body(band_ref, source, *refs):
        outs, kept = refs[:-1], refs[-1]
        turned = jnp.transpose(source[...].astype(jnp.bfloat16), (2, 0, 1))
        kept[...] = turned.reshape(members, each, ROW_TILE, width)
        for c, (start, size) in enumerate(zip(starts, sizes)):
            for k in range(members):
                outs[c * members + k][...] = kept[band_ref[0] ^ k, start : start + size]

    pieces = [size for size in sizes for _ in range(members)]
    outs = pl.pallas_call(
        body,
        grid_spec=pltpu.PrefetchScalarGridSpec(
            num_scalar_prefetch=1,
            grid=(rows // ROW_TILE,),
            in_specs=[pl.BlockSpec((ROW_TILE, width, channels), lambda i, _: (i, 0, 0))],
            out_specs=[pl.BlockSpec((size, ROW_TILE, width), lambda i, _: (0, i, 0)) for size in pieces],
            scratch_shapes=[pltpu.VMEM((members, each, ROW_TILE, width), jnp.bfloat16)],
        ),
        out_shape=[jax.ShapeDtypeStruct((size, rows, width), jnp.bfloat16) for size in pieces],
        compiler_params=VMEM,
        cost_estimate=cost(memory, memory),
        name="spread",
    )(band, memory)
    return [outs[c * members : (c + 1) * members] for c in range(len(sizes))]


def packed(table, mixing):
    wide = mixing.shape[-1]
    numbers = table.reshape(-1).astype(jnp.bfloat16)
    short = -(-numbers.size // wide)
    short += -short % 16
    numbers = jnp.pad(numbers, (0, short * wide - numbers.size)).reshape(short, wide)
    return jnp.concatenate([mixing, numbers], axis=0)


def dense(blocks, table, which, shear, transposed):
    lines, outs_count, slots, wide = blocks.shape[2:6]
    size = outs_count * wide

    def body(table_ref, _, source, out):
        line = pl.program_id(0)
        out[...] = jnp.zeros(out.shape, out.dtype)
        for q in range(outs_count):
            for t in range(slots):
                place = table_ref[((shear * lines + line) * outs_count + q) * slots + t]
                start = pl.multiple_of(place * wide, wide)
                block = source[0, 0, 0, q, t]
                fixed = pl.ds(q * wide, wide)
                moved = pl.ds(start, wide)
                if transposed:
                    out[0, moved, fixed] += block.T
                else:
                    out[0, fixed, moved] += block

    return pl.pallas_call(
        body,
        grid_spec=pltpu.PrefetchScalarGridSpec(
            num_scalar_prefetch=2,
            grid=(lines,),
            in_specs=[
                pl.BlockSpec(
                    (1, 1, 1, outs_count, slots, wide, wide),
                    lambda i, _, which_ref: (which_ref[0], shear, i, 0, 0, 0, 0),
                )
            ],
            out_specs=pl.BlockSpec((1, size, size), lambda i, *_: (i, 0, 0)),
        ),
        out_shape=jax.ShapeDtypeStruct((lines, size, size), jnp.bfloat16),
        compiler_params=VMEM,
        cost_estimate=pl.CostEstimate(flops=0, transcendentals=0, bytes_accessed=8 * lines * size * size),
        name="dense",
    )(table, which, blocks)


def relayed(values, member, first, second, row_chunks):
    members = len(values)
    each, rows, width = values[0].shape
    lines = first[0].shape[0]
    wide = width // lines
    per = wide // rows
    pair = 2 if each % 2 == 0 else 1
    height = rows // row_chunks

    def body(member_ref, *refs):
        pieces, mats = refs[:members], refs[members : members + 6]
        outs, (source, kept, one, two) = refs[members + 6 : members + 6 + row_chunks], refs[members + 6 + row_chunks :]
        for k in range(members):
            source[member_ref[0] ^ k] = pieces[k][...]

        def shears(load, k, slots):
            for s in range(len(slots)):
                for i in range(lines):
                    got = jnp.dot(load(s, i), mats[3 * k][i], preferred_element_type=jnp.float32).astype(jnp.bfloat16)
                    for j in range(lines):
                        one[j, i * wide : (i + 1) * wide, s * wide : (s + 1) * wide] = got[:, j * wide : (j + 1) * wide]
            span = len(slots) * wide
            for j in range(lines):
                got = jnp.dot(mats[3 * k + 1][j], one[j, :, :span], preferred_element_type=jnp.float32)
                got = got.astype(jnp.bfloat16)
                for s in range(len(slots)):
                    two[s, :, j * wide : (j + 1) * wide] = got[:, s * wide : (s + 1) * wide]
            for s, (term, ch) in enumerate(slots):
                for i in range(lines):
                    lhs = two[s, i * wide : (i + 1) * wide]
                    got = jnp.dot(lhs, mats[3 * k + 2][i], preferred_element_type=jnp.float32).astype(jnp.bfloat16)
                    if term == 0:
                        kept[ch, i * wide : (i + 1) * wide] = got
                    split = got.reshape(per, row_chunks, height, width)
                    for r in range(row_chunks):
                        outs[r][per * i : per * (i + 1), term, ch] = split[:, r]

        def given(ch, i):
            return source[per * i : per * (i + 1), ch].reshape(wide, width)

        def held(s, i):
            if s < pair:
                return given(s, i)
            return kept[s - pair, i * wide : (i + 1) * wide]

        shears(given, 0, [(0, ch) for ch in range(pair)])
        shears(held, 1, [(term, ch) for term in (1, 2) for ch in range(pair)])

    mat = pl.BlockSpec(first[0].shape, lambda c, _: (0, 0, 0), pipeline_mode=pl.Buffered(1))
    return pl.pallas_call(
        body,
        grid_spec=pltpu.PrefetchScalarGridSpec(
            num_scalar_prefetch=1,
            grid=(each // pair,),
            in_specs=[pl.BlockSpec((pair, rows, width), lambda c, _: (c, 0, 0))] * members + [mat] * 6,
            out_specs=[pl.BlockSpec((members, 3, pair, height, width), lambda c, _: (0, 0, c, 0, 0))] * row_chunks,
            scratch_shapes=[
                pltpu.VMEM((members, pair, rows, width), jnp.bfloat16),
                pltpu.VMEM((pair, width, width), jnp.bfloat16),
                pltpu.VMEM((lines, width, 2 * pair * wide), jnp.bfloat16),
                pltpu.VMEM((2 * pair, width, width), jnp.bfloat16),
            ],
        ),
        out_shape=[jax.ShapeDtypeStruct((members, 3, each, height, width), jnp.bfloat16)] * row_chunks,
        compiler_params=VMEM,
        cost_estimate=cost(*values * 4, *first, *second, products=18 * members * values[0].size * width),
        name="relayed",
    )(member, *values, *first, *second)


def finished(terms, last, mixes, row_chunk):
    members, _, _, rows, width = last.shape
    channels = mixes[0].shape[0]
    piece = min(width, 128)
    count = len(terms) + 1

    def body(*refs):
        fields, one, two, out = refs[:count], refs[count][...], refs[count + 1][...], refs[count + 2]

        def by_row(pick):
            parts = [pick(j, k) for j in range(members) for k in range(count)]
            return jnp.swapaxes(jnp.concatenate(parts, axis=0), 0, 1)

        p, q, r = [by_row(lambda j, k: fields[k][j, term]) for term in range(3)]
        over_rows = (((0,), (0,)), ((), ()))
        for l in range(rows):
            both = jnp.concatenate([p[l], r[l]], axis=1)
            got = lax.dot_general(one, both, over_rows, preferred_element_type=jnp.float32)
            more = (q[l].astype(jnp.float32) + got[:, piece:]).astype(jnp.bfloat16)
            total = got[:, :piece] + lax.dot_general(two, more, over_rows, preferred_element_type=jnp.float32)
            out[l] = total.astype(jnp.bfloat16).T

    def term_block(a, at):
        return pl.BlockSpec((members, 3, a.shape[2], rows, piece), lambda i: (0, 0, 0, at, i))

    return pl.pallas_call(
        body,
        grid=(width // piece,),
        in_specs=[term_block(a, row_chunk) for a in terms]
        + [term_block(last, 0)]
        + [whole((channels, channels))] * 2,
        out_specs=pl.BlockSpec((rows, piece, channels), lambda i: (0, i, 0)),
        out_shape=jax.ShapeDtypeStruct((rows, width, channels), jnp.bfloat16),
        compiler_params=VMEM,
        cost_estimate=cost(last, last, last),
        name="finished",
    )(*terms, last, *mixes)


def placed(rows_in, old, target, row_chunk, shape):
    rows, width, channels = rows_in.shape
    piece = min(width, 128)

    def body(source, before, *refs):
        refs[-1][...] = before[...].astype(jnp.float32) + source[...].astype(jnp.float32)

    given = [] if target is None else [target]
    block = pl.BlockSpec((rows, piece, channels), lambda i: (0, i, 0))
    return pl.pallas_call(
        body,
        grid=(width // piece,),
        in_specs=[block, block] + [pl.BlockSpec(memory_space=pl.ANY)] * len(given),
        out_specs=pl.BlockSpec((rows, piece, channels), lambda i: (row_chunk, i, 0)),
        out_shape=jax.ShapeDtypeStruct(shape, jnp.float32),
        input_output_aliases={2: 0} if given else {},
        compiler_params=VMEM,
        cost_estimate=cost(*[rows_in] * 5),
        name="placed",
    )(rows_in, old, *given)


def exchanged(values):
    return lax.all_to_all(values, GROUP, split_axis=0, concat_axis=0, tiled=True)


def solution(mesh):
    sections = mesh.shape["pipe"]
    bands = mesh.shape["band"]
    lanes, rest = sections // 2, bands // 2
    fine = Mesh(mesh.devices.reshape(lanes, 2, 2, rest), AXES)

    def flat(pipe, half, place):
        return (pipe * 2 + half) * rest + place

    places = [(pipe, band) for pipe in range(sections) for band in range(bands)]

    def at(pipe, band):
        return pipe * bands + band

    def hosts(section, member):
        return at(section // 2 * 2 + member // rest, section % 2 * rest + member % rest)

    spread_routes = [[(at(p, b), hosts(p, b ^ k)) for p, b in places] for k in range(bands)]
    shift_route = [(at(p, b), at((p + TICKS) % sections, b)) for p, b in places]
    return_route = [(hosts(p, b), at((p + TICKS) % sections, b)) for p, b in places]

    def on_device(memory, shear_blocks, shear_offsets, block_lists, mix_weight):
        line_count = shear_blocks.shape[2]
        source = (
            jnp.arange(line_count, dtype=jnp.int32)[None, None, :, None]
            + shear_offsets[0][:, :, None, None]
            + block_lists[0][:, None]
        ) % line_count
        pipe = ("lane", "core")
        own = lax.axis_index("lane") * 2 + lax.axis_index("half")
        all_blocks = lax.all_gather(shear_blocks[0], pipe)
        packs = lax.all_gather(packed(source, mix_weight[0]), pipe)

        members, (_, height, width, channels) = bands, memory.shape
        row_chunks = height // ROW_TILE
        out_shape = memory.shape[1:]
        mix_rows = mix_weight.shape[1]
        weights, mixes = [], []
        for tick in range(TICKS):
            which = ((own + tick) % sections).astype(jnp.int32)[None]
            tail = lax.dynamic_index_in_dim(packs, which[0], keepdims=False)
            table = tail[mix_rows:].reshape(-1)[: source.size].astype(jnp.int32)
            weights.append([dense(all_blocks, table, which, k, k != 1) for k in range(3)])
            mixes.append(tail[:mix_rows])

        band = (lax.axis_index("half") * rest + lax.axis_index("rest")).astype(jnp.int32)[None]
        member = (lax.axis_index("core") * rest + lax.axis_index("rest")).astype(jnp.int32)[None]
        sent = spread(memory[0], cut(channels // members, ENDS), members, band)
        last = len(sent) - 1

        def shifted(r, *waits):
            rows = memory[0, r * ROW_TILE : (r + 1) * ROW_TILE].astype(jnp.bfloat16)
            return lax.ppermute(tied(rows, *waits), AXES, shift_route)

        def delivered(k, *waits):
            pieces = sent[k]
            if waits:
                pieces = lax.optimization_barrier((*pieces, *waits))[:members]
            return [lax.ppermute(piece, AXES, route) for piece, route in zip(pieces, spread_routes)]

        def later(values, *waits):
            return lax.optimization_barrier((*values, *waits))[: len(values)]

        full = delivered(0, packs)
        terms, olds = [], []
        for k in range(last):
            (solved,) = relayed(full, member, *weights, 1)
            waits = [solved] if k else []
            if terms:
                terms[-1], solved = later([terms[-1], solved])
            full = delivered(k + 1, *full, *waits)
            if k:
                olds += [shifted(r, *olds[-1:], *waits) for r in range(len(olds), -(-row_chunks * k // last))]
            (solved,) = later([solved], *full, *olds)
            terms.append(exchanged(solved.reshape(members, -1, height, width)).reshape(solved.shape))
        solved = relayed(full, member, *weights, row_chunks)
        olds += [shifted(r, *olds[-1:], solved[0]) for r in range(len(olds), row_chunks)]
        terms[-1], *solved = later([terms[-1], *solved])
        solved = later(solved, *olds)

        out, rows = None, None
        moved = []
        for r in range(row_chunks):
            waits = ([rows] if r else []) + (moved[r - 2 : r - 1] if r > 1 else [])
            field = solved[r].reshape(members, -1, ROW_TILE, width)
            field = exchanged(tied(field, *waits) if waits else field)
            if r > 1 and r == row_chunks - 1:
                field = tied(field, moved[-1])
            rows = finished(terms, field.reshape(solved[r].shape), mixes, r)
            moved.append(lax.ppermute(rows, AXES, return_route))
        for r in range(row_chunks):
            out = placed(moved[r], olds[r], out, r, out_shape)
        return out[None]

    return jax.shard_map(
        on_device,
        mesh=fine,
        in_specs=(
            P(("lane", "core"), ("half", "rest"), None, None),
            P(("lane", "core"), None, None, None, None, None, None),
            P(("lane", "core"), None, None),
            P(("lane", "core"), None, None, None),
            P(("lane", "core"), None, None),
        ),
        out_specs=P(("lane", "core"), ("half", "rest"), None, None),
        check_vma=False,
    )
```

time: 781 us -> 743 us (0.951); the launches traced: 771 us -> 742 us
  blocking collectives: 107 us -> 6.69 us
  starting transfers between devices: 70.7 us -> 112 us
  Pallas kernels: 150 us -> 183 us
  waiting for transfers between devices: 413 us -> 402 us
    all_to_all x2 -> x0, blocking collectives: 83.5 us -> none  [exchanged(): lax.all_to_all(values, GROUP, split_axis=0, concat_axis=0, tiled=True)]
    ppermute x5 -> x36, starting transfers between devices: 16.9 us -> 74.4 us  [the longest x32 71.7 us: delivered(): lax.ppermute(piece, AXES, route)]
    all_to_all x10 -> x7, waiting for transfers between devices: 200 us -> 143 us  [exchanged(): lax.all_to_all(values, GROUP, split_axis=0, concat_axis=0, tiled=True)]
    pallas_call x17 -> x13, Pallas kernels: 124 us -> 156 us  [the longest x4 69.8 us: relayed(): pl.pallas_call(body, grid_spec=pltpu.PrefetchScalarGridSpec(num_scalar_pr...]
    ppermute x5 -> x36, waiting for transfers between devices: 137 us -> 167 us  [the longest x32 157 us: delivered(): lax.ppermute(piece, AXES, route)]
    all_gather x2 -> x1, blocking collectives: 23.7 us -> 6.69 us  [on_device(): packs = lax.all_gather(packed(source, mix_weight[0]), pipe)]
    ppermute x4, starting transfers between devices: 12.8 us -> 1.94 us  [on_device(): moved.append(lax.ppermute(rows, AXES, return_route))]
    all_gather x1, waiting for transfers between devices: 0.01 us -> 8.8 us  [on_device(): all_blocks = lax.all_gather(shear_blocks[0], pipe)]
  transfers between devices with their start and end apart: 20 -> 48, of which waited for: 13 -> 29; matrix products, arithmetic and copies ran while one was open for 1% -> 2% of each run, Pallas kernels for 15% -> 20%
where the time goes in v3:
time: 743 us; the launch traced here: 742 us
  waiting for transfers between devices  402 us (54%)
  Pallas kernels  183 us (25%)
  starting transfers between devices  112 us (15%)
  local copies, waits for them, and re-layouts  15.9 us (2%)
  between operations  13.9 us (2%)
  other arithmetic  7.43 us (1%)
    ppermute x32, waiting for transfers between devices, delivered(): lax.ppermute(piece, AXES, route)  157 us
    all_to_all x7, waiting for transfers between devices, exchanged(): lax.all_to_all(values, GROUP, split_axis=0, concat_axis=0, tiled=True)  143 us
    ppermute x4, waiting for transfers between devices, on_device(): moved.append(lax.ppermute(rows, AXES, return_route))  83.3 us
    ppermute x32, starting transfers between devices, delivered(): lax.ppermute(piece, AXES, route)  71.7 us
    pallas_call x4, Pallas kernels, relayed(): pl.pallas_call(body, grid_spec=pltpu.PrefetchScalarGridSpec(num_scalar_pr...  69.8 us
    pallas_call x4, Pallas kernels, finished(): pl.pallas_call(body, grid=(width // piece,), in_specs=[term_block(a, row_...  56.4 us
    all_to_all x7, starting transfers between devices, exchanged(): lax.all_to_all(values, GROUP, split_axis=0, concat_axis=0, tiled=True)  35.7 us
    pallas_call x6, Pallas kernels, dense(): pl.pallas_call(body, grid_spec=pltpu.PrefetchScalarGridSpec(num_scalar_pr...  26.9 us
  transfers between devices with their start and end apart: 48, of which 29 were waited for; matrix products, arithmetic and copies ran while one was open for 2% of the time, Pallas kernels for 20%

profile of v3, /device:TPU:1, one launch (start us, length us, event | category | flops | bytes accessed | tf_op | source)
XLA Modules:
  0.0 741.6 jit_solution(10723169080701051288)
XLA Ops:
  7.7 11.0 %spread.1 = (bf16[4,64,512]{2,1,0:T(8,128)(2,1)}, bf16[4,64,512]{2,1,0:T(8,128)(2,1)}, bf16[4,64,512]{2,1,0:T(8,128)(2,1)}, bf16[4,64,512]{2,1,0:T(8,128)(2,1)},...) custom-call(s32[1]{0:T(128)} %bitcast.1.band_ref, ...), custom_call_target="tpu_custom_call" | custom-call | bytes 33554432 | tf_op jit(solution)/shard_map/spread/pallas_call | solution.py:52
  18.8 6.7 all-gather
  25.5 5.0 collective-permute-start
  31.8 3.3 collective-permute-start.2
  36.9 6.7 collective-permute-done.1.refs_1_
  43.5 3.8 collective-permute-done.2.refs_2_
  47.3 5.2 collective-permute-done.3.refs_3_
  53.7 3.8 collective-permute-done.5.refs_5_
  57.5 4.7 collective-permute-done.6.refs_6_
  62.1 2.8 collective-permute-done.7.refs_7_
  65.0 13.9 %collective-permute-start.8 = (bf16[4,64,512]{2,1,0:T(8,128)(2,1)}, bf16[4,64,512]{2,1,0:T(8,128)(2,1)S(1)}, u32[]{:S(2)}, u32[]{:S(2)}) collective-permute-start(bf16[4,64,512]{2,1,0:T(8,128)(2,1)} %get-tuple-element.121), channel_id=1, source_target_pairs={{0,0},{1,1},{2,2},{3,3},{4,8},{5,9},{6,10},{7,11},{8,4},{9,5},{10,... | collective-permute-start | bytes 786440 | tf_op jit(solution)/shard_map/ppermute | solution.py:310
  80.3 2.7 collective-permute-start.10
  85.0 8.8 %all-gather.3.cloned.1.call-done.source = bf16[4,3,4,4,2,128,128]{6,5,4,3,2,1,0:T(8,128)(2,1)} async-done(((bf16[1,3,4,4,2,128,128]{6,5,4,3,2,1,0:T(8,128)(2,1)}), bf16[4,3,4,4,2,128,128]{6,5,4,3,2,1,0:T(8,128)(2,1)}) %all-gather.3.cloned.1.call-update) | async-done | bytes 12582928 | tf_op jit(solution)/shard_map/all_gather | solution.py:282
  93.8 4.5 dense.11.refs_13_
  98.3 4.4 dense.10.refs_12_
  102.7 4.5 dense.9.refs_11_
  107.2 4.5 dense.8.refs_10_
  111.7 4.4 dense.7.refs_9_
  116.1 4.6 dense.6.refs_8_
  120.7 3.3 collective-permute-start.13
  125.8 17.4 %relayed.4 = bf16[8,3,4,64,512]{4,3,2,1,0:T(8,128)(2,1)} custom-call(s32[1]{0:T(128)} %bitcast.member_ref, bf16[4,64,512]{2,1,0:T(8,128)(2,1)} %copy-done.30, bf16[4,64,512]{2,1,0:T(8,128)(2,1)} %copy-done.31, bf16[4,64,512]{2,1,0:T(8,128)(2,1)} %copy-done.32, bf16[4,64,512]{2,1,0:T(8,128)(2,1)} %copy-done.33, bf16[4,64,512]{2,1,0:T(8,128)(2,1)} %copy-done.34, ...), custom_call_target="tpu_custom_call" | custom-call | flops 19327352832 | bytes 20971520 | tf_op jit(solution)/shard_map/relayed/pallas_call | solution.py:166
  144.2 4.9 all-to-all-start
  149.1 6.7 convert.6
  155.7 3.4 slice_bitcast_fusion
  159.2 17.5 %relayed.5 = bf16[8,3,4,64,512]{4,3,2,1,0:T(8,128)(2,1)} custom-call(s32[1]{0:T(128)} %bitcast.member_ref, bf16[4,64,512]{2,1,0:T(8,128)(2,1)} %copy-done.38, bf16[4,64,512]{2,1,0:T(8,128)(2,1)} %copy-done.39, bf16[4,64,512]{2,1,0:T(8,128)(2,1)} %copy-done.40, bf16[4,64,512]{2,1,0:T(8,128)(2,1)} %copy-done.41, ...), custom_call_target="tpu_custom_call" | custom-call | flops 19327352832 | bytes 20971520 | tf_op jit(solution)/shard_map/relayed/pallas_call | solution.py:166
  178.2 4.1 collective-permute-start.16
  183.9 3.9 collective-permute-start.18
  187.8 34.7 %collective-permute-done.16.refs_0_ = bf16[4,64,512]{2,1,0:T(8,128)(2,1)S(1)} collective-permute-done((bf16[4,64,512]{2,1,0:T(8,128)(2,1)S(1)}, bf16[4,64,512]{2,1,0:T(8,128)(2,1)S(1)}, u32[]{:S(2)}, u32[]{:S(2)}) %collective-permute-start.16) | collective-permute-done | bytes 262176 | tf_op jit(solution)/shard_map/ppermute | solution.py:310
  222.5 5.3 collective-permute-start.19
  228.1 6.3 collective-permute-done.18.refs_2_
  234.4 3.9 collective-permute-done.19.refs_3_
  239.7 13.5 %collective-permute-start.23 = (bf16[4,64,512]{2,1,0:T(8,128)(2,1)S(1)}, bf16[4,64,512]{2,1,0:T(8,128)(2,1)}, u32[]{:S(2)}, u32[]{:S(2)}) collective-permute-start(bf16[4,64,512]{2,1,0:T(8,128)(2,1)S(1)} %copy-done.19), channel_id=1, source_target_pairs={{0,11},{1,10},{2,9},{3,8},{4,3},{5,2},{6,1},{7,0},{8,15},{9,14},{1... | collective-permute-start | bytes 786440 | tf_op jit(solution)/shard_map/ppermute | solution.py:310
  253.2 5.9 collective-permute-done.23.refs_7_
  259.1 9.9 %collective-permute-done.25.before = bf16[16,512,128]{2,1,0:T(8,128)(2,1)} collective-permute-done((bf16[16,512,128]{2,1,0:T(8,128)(2,1)}, bf16[16,512,128]{2,1,0:T(8,128)(2,1)}, u32[]{:S(2)}, u32[]{:S(2)}) %collective-permute-start.25) | collective-permute-done | bytes 2097184 | tf_op jit(solution)/shard_map/ppermute | solution.py:304
  269.1 5.7 all-to-all-start.1
  274.8 17.5 %relayed.6 = bf16[8,3,4,64,512]{4,3,2,1,0:T(8,128)(2,1)} custom-call(s32[1]{0:T(128)} %bitcast.member_ref, bf16[4,64,512]{2,1,0:T(8,128)(2,1)} %copy-done.45, bf16[4,64,512]{2,1,0:T(8,128)(2,1)} %copy-done.47, bf16[4,64,512]{2,1,0:T(8,128)(2,1)} %copy-done.48, bf16[4,64,512]{2,1,0:T(8,128)(2,1)} %copy-done.49, bf16[4,64,512]{2,1,0:T(8,128)(2,1)} %copy-done.51, ...), custom_call_target="tpu_custom_call" | custom-call | flops 19327352832 | bytes 20971520 | tf_op jit(solution)/shard_map/relayed/pallas_call | solution.py:166
  293.0 3.6 collective-permute-start.26
  298.7 2.9 collective-permute-start.28
  302.1 48.4 %collective-permute-done.26.refs_0_ = bf16[4,64,512]{2,1,0:T(8,128)(2,1)S(1)} collective-permute-done((bf16[4,64,512]{2,1,0:T(8,128)(2,1)S(1)}, bf16[4,64,512]{2,1,0:T(8,128)(2,1)S(1)}, u32[]{:S(2)}, u32[]{:S(2)}) %collective-permute-start.26) | collective-permute-done | bytes 262176 | tf_op jit(solution)/shard_map/ppermute | solution.py:310
  350.5 5.6 collective-permute-done.27.refs_1_
  356.1 7.9 %collective-permute-done.28.refs_2_ = bf16[4,64,512]{2,1,0:T(8,128)(2,1)S(1)} collective-permute-done((bf16[4,64,512]{2,1,0:T(8,128)(2,1)S(1)}, bf16[4,64,512]{2,1,0:T(8,128)(2,1)S(1)}, u32[]{:S(2)}, u32[]{:S(2)}) %collective-permute-start.28) | collective-permute-done | bytes 262176 | tf_op jit(solution)/shard_map/ppermute | solution.py:310
  367.6 4.7 collective-permute-done.31.refs_5_
  372.3 3.7 collective-permute-done.32.refs_6_
  376.0 2.8 collective-permute-done.33.refs_7_
  380.1 10.4 %all-to-all-start.2 = ((bf16[8,12,64,512]{3,2,1,0:T(8,128)(2,1)}), bf16[8,12,64,512]{3,2,1,0:T(8,128)(2,1)}, u32[]{:S(2)}, u32[]{:S(2)}) async-start(bf16[8,12,64,512]{3,2,1,0:T(8,128)(2,1)} %bitcast.46), calls=%async_computation.2 | async-start | bytes 12582912 | tf_op jit(solution)/shard_map/all_to_all | solution.py:249
  390.5 17.5 %relayed.7 = (bf16[8,3,4,16,512]{4,3,2,1,0:T(8,128)(2,1)}, bf16[8,3,4,16,512]{4,3,2,1,0:T(8,128)(2,1)}, bf16[8,3,4,16,512]{4,3,2,1,0:T(8,128)(2,1)}, bf16[8,3,4,16,512]{4,3,2,1,0:T(8,128)(2,1)}) custom-call(s32[1]{0:T(128)} %bitcast.member_ref, bf16[4,64,512]{2,1,0:T(8,128)(2,1)} %copy-done.42, bf16[4,64,512]{2,1,0:T(8,128)(2,1)} %copy-done.43, ...), custom_call_target="tpu_custom_call" | custom-call | flops 19327352832 | bytes 20971520 | tf_op jit(solution)/shard_map/relayed/pallas_call | solution.py:166
  408.4 53.0 %all-to-all-done.2 = bf16[8,12,64,512]{3,2,1,0:T(8,128)(2,1)} async-done(((bf16[8,12,64,512]{3,2,1,0:T(8,128)(2,1)}), bf16[8,12,64,512]{3,2,1,0:T(8,128)(2,1)}, u32[]{:S(2)}, u32[]{:S(2)}) %all-to-all-start.2) | async-done | bytes 6291488 | tf_op jit(solution)/shard_map/all_to_all | solution.py:249
  462.8 3.5 all-to-all-start.3
  467.0 19.3 %all-to-all-done.3 = bf16[8,12,16,512]{3,2,1,0:T(8,128)(2,1)S(1)} async-done(((bf16[8,12,16,512]{3,2,1,0:T(8,128)(2,1)}), bf16[8,12,16,512]{3,2,1,0:T(8,128)(2,1)S(1)}, u32[]{:S(2)}, u32[]{:S(2)}) %all-to-all-start.3) | async-done | bytes 1572896 | tf_op jit(solution)/shard_map/all_to_all | solution.py:249
  487.4 14.1 %finished.4 = bf16[16,512,128]{2,1,0:T(8,128)(2,1)} custom-call(bf16[8,3,4,64,512]{4,3,2,1,0:T(8,128)(2,1)} %bitcast.12.refs_0_, bf16[8,3,4,64,512]{4,3,2,1,0:T(8,128)(2,1)} %bitcast.16.refs_1_, bf16[8,3,4,64,512]{4,3,2,1,0:T(8,128)(2,1)} %bitcast.19.refs_2_, bf16[8,3,4,16,512]{4,3,2,1,0:T(8,128)(2,1)} %bitcast.49, ...), custom_call_target="tpu_custom_call" | custom-call | bytes 4718592 | tf_op jit(solution)/shard_map/finished/pallas_call | solution.py:212
  501.5 3.7 all-to-all-start.4
  507.0 34.9 %all-to-all-done.4 = bf16[8,12,16,512]{3,2,1,0:T(8,128)(2,1)S(1)} async-done(((bf16[8,12,16,512]{3,2,1,0:T(8,128)(2,1)}), bf16[8,12,16,512]{3,2,1,0:T(8,128)(2,1)S(1)}, u32[]{:S(2)}, u32[]{:S(2)}) %all-to-all-start.4) | async-done | bytes 1572896 | tf_op jit(solution)/shard_map/all_to_all | solution.py:249
  543.1 14.1 %finished.5 = bf16[16,512,128]{2,1,0:T(8,128)(2,1)} custom-call(bf16[8,3,4,64,512]{4,3,2,1,0:T(8,128)(2,1)} %bitcast.12.refs_0_, bf16[8,3,4,64,512]{4,3,2,1,0:T(8,128)(2,1)} %bitcast.16.refs_1_, bf16[8,3,4,64,512]{4,3,2,1,0:T(8,128)(2,1)} %bitcast.19.refs_2_, bf16[8,3,4,16,512]{4,3,2,1,0:T(8,128)(2,1)} %bitcast.50, ...), custom_call_target="tpu_custom_call" | custom-call | bytes 4718592 | tf_op jit(solution)/shard_map/finished/pallas_call | solution.py:212
  557.2 3.7 all-to-all-start.5
  561.1 35.8 %all-to-all-done.5 = bf16[8,12,16,512]{3,2,1,0:T(8,128)(2,1)S(1)} async-done(((bf16[8,12,16,512]{3,2,1,0:T(8,128)(2,1)}), bf16[8,12,16,512]{3,2,1,0:T(8,128)(2,1)S(1)}, u32[]{:S(2)}, u32[]{:S(2)}) %all-to-all-start.5) | async-done | bytes 1572896 | tf_op jit(solution)/shard_map/all_to_all | solution.py:249
  598.0 14.1 %finished.6 = bf16[16,512,128]{2,1,0:T(8,128)(2,1)} custom-call(bf16[8,3,4,64,512]{4,3,2,1,0:T(8,128)(2,1)} %bitcast.12.refs_0_, bf16[8,3,4,64,512]{4,3,2,1,0:T(8,128)(2,1)} %bitcast.16.refs_1_, bf16[8,3,4,64,512]{4,3,2,1,0:T(8,128)(2,1)} %bitcast.19.refs_2_, bf16[8,3,4,16,512]{4,3,2,1,0:T(8,128)(2,1)} %bitcast.51, ...), custom_call_target="tpu_custom_call" | custom-call | bytes 4718592 | tf_op jit(solution)/shard_map/finished/pallas_call | solution.py:212
  612.1 3.7 all-to-all-start.6
  615.8 50.1 %collective-permute-done.38.source = bf16[16,512,128]{2,1,0:T(8,128)(2,1)} collective-permute-done((bf16[16,512,128]{2,1,0:T(8,128)(2,1)}, bf16[16,512,128]{2,1,0:T(8,128)(2,1)}, u32[]{:S(2)}, u32[]{:S(2)}) %collective-permute-start.38) | collective-permute-done | bytes 2097184 | tf_op jit(solution)/shard_map/ppermute | solution.py:341
  667.1 14.1 %finished.7 = bf16[16,512,128]{2,1,0:T(8,128)(2,1)} custom-call(bf16[8,3,4,64,512]{4,3,2,1,0:T(8,128)(2,1)} %bitcast.12.refs_0_, bf16[8,3,4,64,512]{4,3,2,1,0:T(8,128)(2,1)} %bitcast.16.refs_1_, bf16[8,3,4,64,512]{4,3,2,1,0:T(8,128)(2,1)} %bitcast.19.refs_2_, bf16[8,3,4,16,512]{4,3,2,1,0:T(8,128)(2,1)} %bitcast.48, ...), custom_call_target="tpu_custom_call" | custom-call | bytes 4718592 | tf_op jit(solution)/shard_map/finished/pallas_call | solution.py:212
  681.2 4.8 placed.4.refs_0_
  685.9 4.8 placed.5.refs_0_
  690.7 4.8 placed.6.refs_0_
  695.4 33.3 %collective-permute-done.39.source = bf16[16,512,128]{2,1,0:T(8,128)(2,1)S(1)} collective-permute-done((bf16[16,512,128]{2,1,0:T(8,128)(2,1)}, bf16[16,512,128]{2,1,0:T(8,128)(2,1)S(1)}, u32[]{:S(2)}, u32[]{:S(2)}) %collective-permute-start.39) | collective-permute-done | bytes 2097184 | tf_op jit(solution)/shard_map/ppermute | solution.py:341
  730.0 4.8 placed.7
  (174 shorter events, 34.9 us)
Async XLA Ops:
  6.5 87.2 %all-gather.3.cloned.1.call-start = ((), (), s32[]{:S(2)}) async-start(), calls=%async_computation.7 | async-start | bytes 15728640 | tf_op jit(solution)/shard_map/all_gather | solution.py:282
  25.5 11.2 %collective-permute-start = (bf16[4,64,512]{2,1,0:T(8,128)(2,1)}, bf16[4,64,512]{2,1,0:T(8,128)(2,1)S(1)}, u32[]{:S(2)}, u32[]{:S(2)}) collective-permute-start(bf16[4,64,512]{2,1,0:T(8,128)(2,1)} %get-tuple-element.105), channel_id=1, source_target_pairs={{0,0},{1,1},{2,2},{3,3},{4,8},{5,9},{6,10},{7,11},{8,4},{9,5},{10,... | collective-permute-start | bytes 786440 | tf_op jit(solution)/shard_map/ppermute | solution.py:310
  30.4 13.1 %collective-permute-start.1 = (bf16[4,64,512]{2,1,0:T(8,128)(2,1)}, bf16[4,64,512]{2,1,0:T(8,128)(2,1)S(1)}, u32[]{:S(2)}, u32[]{:S(2)}) collective-permute-start(bf16[4,64,512]{2,1,0:T(8,128)(2,1)} %get-tuple-element.106), channel_id=1, source_target_pairs={{0,1},{1,0},{2,3},{3,2},{4,9},{5,8},{6,11},{7,10},{8,5},{9,4},{10,... | collective-permute-start | bytes 786440 | tf_op jit(solution)/shard_map/ppermute | solution.py:310
  31.8 15.5 %collective-permute-start.2 = (bf16[4,64,512]{2,1,0:T(8,128)(2,1)}, bf16[4,64,512]{2,1,0:T(8,128)(2,1)S(1)}, u32[]{:S(2)}, u32[]{:S(2)}) collective-permute-start(bf16[4,64,512]{2,1,0:T(8,128)(2,1)} %get-tuple-element.107), channel_id=1, source_target_pairs={{0,2},{1,3},{2,0},{3,1},{4,10},{5,11},{6,8},{7,9},{8,6},{9,7},{10,... | collective-permute-start | bytes 786440 | tf_op jit(solution)/shard_map/ppermute | solution.py:310
  35.1 17.4 %collective-permute-start.3 = (bf16[4,64,512]{2,1,0:T(8,128)(2,1)}, bf16[4,64,512]{2,1,0:T(8,128)(2,1)S(1)}, u32[]{:S(2)}, u32[]{:S(2)}) collective-permute-start(bf16[4,64,512]{2,1,0:T(8,128)(2,1)} %get-tuple-element.108), channel_id=1, source_target_pairs={{0,3},{1,2},{2,1},{3,0},{4,11},{5,10},{6,9},{7,8},{8,7},{9,6},{10,... | collective-permute-start | bytes 786440 | tf_op jit(solution)/shard_map/ppermute | solution.py:310
  35.1 18.6 %collective-permute-start.4 = (bf16[4,64,512]{2,1,0:T(8,128)(2,1)}, bf16[4,64,512]{2,1,0:T(8,128)(2,1)S(1)}, u32[]{:S(2)}, u32[]{:S(2)}) collective-permute-start(bf16[4,64,512]{2,1,0:T(8,128)(2,1)} %get-tuple-element.109), channel_id=1, source_target_pairs={{0,8},{1,9},{2,10},{3,11},{4,0},{5,1},{6,2},{7,3},{8,12},{9,13},{1... | collective-permute-start | bytes 786440 | tf_op jit(solution)/shard_map/ppermute | solution.py:310
  36.7 61.6 %copy-start.30 = (bf16[4,64,512]{2,1,0:T(8,128)(2,1)}, bf16[4,64,512]{2,1,0:T(8,128)(2,1)S(1)}, u32[]{:S(2)}) copy-start(bf16[4,64,512]{2,1,0:T(8,128)(2,1)S(1)} %collective-permute-done.refs_0_) | copy-start | bytes 786436
  36.7 20.8 %collective-permute-start.5 = (bf16[4,64,512]{2,1,0:T(8,128)(2,1)}, bf16[4,64,512]{2,1,0:T(8,128)(2,1)S(1)}, u32[]{:S(2)}, u32[]{:S(2)}) collective-permute-start(bf16[4,64,512]{2,1,0:T(8,128)(2,1)} %get-tuple-element.110), channel_id=1, source_target_pairs={{0,9},{1,8},{2,11},{3,10},{4,1},{5,0},{6,3},{7,2},{8,13},{9,12},{1... | collective-permute-start | bytes 786440 | tf_op jit(solution)/shard_map/ppermute | solution.py:310
  43.5 54.7 %copy-start.31 = (bf16[4,64,512]{2,1,0:T(8,128)(2,1)}, bf16[4,64,512]{2,1,0:T(8,128)(2,1)S(1)}, u32[]{:S(2)}) copy-start(bf16[4,64,512]{2,1,0:T(8,128)(2,1)S(1)} %collective-permute-done.1.refs_1_) | copy-start | bytes 786436
  43.5 18.6 %collective-permute-start.6 = (bf16[4,64,512]{2,1,0:T(8,128)(2,1)}, bf16[4,64,512]{2,1,0:T(8,128)(2,1)S(1)}, u32[]{:S(2)}, u32[]{:S(2)}) collective-permute-start(bf16[4,64,512]{2,1,0:T(8,128)(2,1)} %get-tuple-element.111), channel_id=1, source_target_pairs={{0,10},{1,11},{2,8},{3,9},{4,2},{5,3},{6,0},{7,1},{8,14},{9,15},{1... | collective-permute-start | bytes 786440 | tf_op jit(solution)/shard_map/ppermute | solution.py:310
  47.3 50.9 %copy-start.32 = (bf16[4,64,512]{2,1,0:T(8,128)(2,1)}, bf16[4,64,512]{2,1,0:T(8,128)(2,1)S(1)}, u32[]{:S(2)}) copy-start(bf16[4,64,512]{2,1,0:T(8,128)(2,1)S(1)} %collective-permute-done.2.refs_2_) | copy-start | bytes 786436
  47.3 17.6 %collective-permute-start.7 = (bf16[4,64,512]{2,1,0:T(8,128)(2,1)}, bf16[4,64,512]{2,1,0:T(8,128)(2,1)S(1)}, u32[]{:S(2)}, u32[]{:S(2)}) collective-permute-start(bf16[4,64,512]{2,1,0:T(8,128)(2,1)} %get-tuple-element.112), channel_id=1, source_target_pairs={{0,11},{1,10},{2,9},{3,8},{4,3},{5,2},{6,1},{7,0},{8,15},{9,14},{1... | collective-permute-start | bytes 786440 | tf_op jit(solution)/shard_map/ppermute | solution.py:310
  52.6 45.7 %copy-start.33 = (bf16[4,64,512]{2,1,0:T(8,128)(2,1)}, bf16[4,64,512]{2,1,0:T(8,128)(2,1)S(1)}, u32[]{:S(2)}) copy-start(bf16[4,64,512]{2,1,0:T(8,128)(2,1)S(1)} %collective-permute-done.3.refs_3_) | copy-start | bytes 786436
  53.7 44.6 %copy-start.34 = (bf16[4,64,512]{2,1,0:T(8,128)(2,1)}, bf16[4,64,512]{2,1,0:T(8,128)(2,1)S(1)}, u32[]{:S(2)}) copy-start(bf16[4,64,512]{2,1,0:T(8,128)(2,1)S(1)} %collective-permute-done.4.refs_4_) | copy-start | bytes 786436
  65.0 55.8 %collective-permute-start.8 = (bf16[4,64,512]{2,1,0:T(8,128)(2,1)}, bf16[4,64,512]{2,1,0:T(8,128)(2,1)S(1)}, u32[]{:S(2)}, u32[]{:S(2)}) collective-permute-start(bf16[4,64,512]{2,1,0:T(8,128)(2,1)} %get-tuple-element.121), channel_id=1, source_target_pairs={{0,0},{1,1},{2,2},{3,3},{4,8},{5,9},{6,10},{7,11},{8,4},{9,5},{10,... | collective-permute-start | bytes 786440 | tf_op jit(solution)/shard_map/ppermute | solution.py:310
  78.8 45.2 %collective-permute-start.9 = (bf16[4,64,512]{2,1,0:T(8,128)(2,1)}, bf16[4,64,512]{2,1,0:T(8,128)(2,1)S(1)}, u32[]{:S(2)}, u32[]{:S(2)}) collective-permute-start(bf16[4,64,512]{2,1,0:T(8,128)(2,1)} %get-tuple-element.122), channel_id=1, source_target_pairs={{0,1},{1,0},{2,3},{3,2},{4,9},{5,8},{6,11},{7,10},{8,5},{9,4},{10,... | collective-permute-start | bytes 786440 | tf_op jit(solution)/shard_map/ppermute | solution.py:310
  80.3 45.3 %collective-permute-start.10 = (bf16[4,64,512]{2,1,0:T(8,128)(2,1)}, bf16[4,64,512]{2,1,0:T(8,128)(2,1)S(1)}, u32[]{:S(2)}, u32[]{:S(2)}) collective-permute-start(bf16[4,64,512]{2,1,0:T(8,128)(2,1)} %get-tuple-element.123), channel_id=1, source_target_pairs={{0,2},{1,3},{2,0},{3,1},{4,10},{5,11},{6,8},{7,9},{8,6},{9,7},{10,... | collective-permute-start | bytes 786440 | tf_op jit(solution)/shard_map/ppermute | solution.py:310
  83.5 59.7 %collective-permute-start.11 = (bf16[4,64,512]{2,1,0:T(8,128)(2,1)}, bf16[4,64,512]{2,1,0:T(8,128)(2,1)S(1)}, u32[]{:S(2)}, u32[]{:S(2)}) collective-permute-start(bf16[4,64,512]{2,1,0:T(8,128)(2,1)} %get-tuple-element.124), channel_id=1, source_target_pairs={{0,3},{1,2},{2,1},{3,0},{4,11},{5,10},{6,9},{7,8},{8,7},{9,6},{10,... | collective-permute-start | bytes 786440 | tf_op jit(solution)/shard_map/ppermute | solution.py:310
  84.5 58.7 %collective-permute-start.12 = (bf16[4,64,512]{2,1,0:T(8,128)(2,1)}, bf16[4,64,512]{2,1,0:T(8,128)(2,1)}, u32[]{:S(2)}, u32[]{:S(2)}) collective-permute-start(bf16[4,64,512]{2,1,0:T(8,128)(2,1)} %get-tuple-element.125), channel_id=1, source_target_pairs={{0,8},{1,9},{2,10},{3,11},{4,0},{5,1},{6,2},{7,3},{8,12},{9,13},{1... | collective-permute-start | bytes 786440 | tf_op jit(solution)/shard_map/ppermute | solution.py:310
  120.7 22.5 %collective-permute-start.13 = (bf16[4,64,512]{2,1,0:T(8,128)(2,1)S(1)}, bf16[4,64,512]{2,1,0:T(8,128)(2,1)S(1)}, u32[]{:S(2)}, u32[]{:S(2)}) collective-permute-start(bf16[4,64,512]{2,1,0:T(8,128)(2,1)S(1)} %copy-done.29), channel_id=1, source_target_pairs={{0,9},{1,8},{2,11},{3,10},{4,1},{5,0},{6,3},{7,2},{8,13},{9,12},{1... | collective-permute-start | bytes 786440 | tf_op jit(solution)/shard_map/ppermute | solution.py:310
  124.0 19.2 %collective-permute-start.14 = (bf16[4,64,512]{2,1,0:T(8,128)(2,1)S(1)}, bf16[4,64,512]{2,1,0:T(8,128)(2,1)S(1)}, u32[]{:S(2)}, u32[]{:S(2)}) collective-permute-start(bf16[4,64,512]{2,1,0:T(8,128)(2,1)S(1)} %copy-done.28), channel_id=1, source_target_pairs={{0,10},{1,11},{2,8},{3,9},{4,2},{5,3},{6,0},{7,1},{8,14},{9,15},{1... | collective-permute-start | bytes 786440 | tf_op jit(solution)/shard_map/ppermute | solution.py:310
  125.5 17.7 %collective-permute-start.15 = (bf16[4,64,512]{2,1,0:T(8,128)(2,1)S(1)}, bf16[4,64,512]{2,1,0:T(8,128)(2,1)S(1)}, u32[]{:S(2)}, u32[]{:S(2)}) collective-permute-start(bf16[4,64,512]{2,1,0:T(8,128)(2,1)S(1)} %copy-done.27), channel_id=1, source_target_pairs={{0,11},{1,10},{2,9},{3,8},{4,3},{5,2},{6,1},{7,0},{8,15},{9,14},{1... | collective-permute-start | bytes 786440 | tf_op jit(solution)/shard_map/ppermute | solution.py:310
  144.2 109.0 %all-to-all-start = ((bf16[8,12,64,512]{3,2,1,0:T(8,128)(2,1)}), bf16[8,12,64,512]{3,2,1,0:T(8,128)(2,1)}, u32[]{:S(2)}, u32[]{:S(2)}) async-start(bf16[8,12,64,512]{3,2,1,0:T(8,128)(2,1)} %bitcast.47), calls=%async_computation | async-start | bytes 12582912 | tf_op jit(solution)/shard_map/all_to_all | solution.py:249
  159.1 63.4 %copy-start.23 = (bf16[4,64,512]{2,1,0:T(8,128)(2,1)S(1)}, bf16[4,64,512]{2,1,0:T(8,128)(2,1)}, u32[]{:S(2)}) copy-start(bf16[4,64,512]{2,1,0:T(8,128)(2,1)} %get-tuple-element.143) | copy-start | bytes 786436
  159.1 69.0 %copy-start.22 = (bf16[4,64,512]{2,1,0:T(8,128)(2,1)S(1)}, bf16[4,64,512]{2,1,0:T(8,128)(2,1)}, u32[]{:S(2)}) copy-start(bf16[4,64,512]{2,1,0:T(8,128)(2,1)} %get-tuple-element.144) | copy-start | bytes 786436
  159.1 75.2 %copy-start.21 = (bf16[4,64,512]{2,1,0:T(8,128)(2,1)S(1)}, bf16[4,64,512]{2,1,0:T(8,128)(2,1)}, u32[]{:S(2)}) copy-start(bf16[4,64,512]{2,1,0:T(8,128)(2,1)} %get-tuple-element.145) | copy-start | bytes 786436
  159.2 79.1 %copy-start.20 = (bf16[4,64,512]{2,1,0:T(8,128)(2,1)S(1)}, bf16[4,64,512]{2,1,0:T(8,128)(2,1)}, u32[]{:S(2)}) copy-start(bf16[4,64,512]{2,1,0:T(8,128)(2,1)} %get-tuple-element.146) | copy-start | bytes 786436
  159.2 80.5 %copy-start.19 = (bf16[4,64,512]{2,1,0:T(8,128)(2,1)S(1)}, bf16[4,64,512]{2,1,0:T(8,128)(2,1)}, u32[]{:S(2)}) copy-start(bf16[4,64,512]{2,1,0:T(8,128)(2,1)} %get-tuple-element.147) | copy-start | bytes 786436
  176.7 82.5 %collective-permute-start.24 = (bf16[16,512,128]{2,1,0:T(8,128)(2,1)}, bf16[16,512,128]{2,1,0:T(8,128)(2,1)S(1)}, u32[]{:S(2)}, u32[]{:S(2)}) collective-permute-start(bf16[16,512,128]{2,1,0:T(8,128)(2,1)} %get-tuple-element.148), channel_id=1, source_target_pairs={{0,16},{1,17},{2,18},{3,19},{4,20},{5,21},{6,22},{7,23},{8,24},{9,... | collective-permute-start | bytes 6291464 | tf_op jit(solution)/shard_map/ppermute | solution.py:304
  177.4 91.7 %collective-permute-start.25 = (bf16[16,512,128]{2,1,0:T(8,128)(2,1)}, bf16[16,512,128]{2,1,0:T(8,128)(2,1)}, u32[]{:S(2)}, u32[]{:S(2)}) collective-permute-start(bf16[16,512,128]{2,1,0:T(8,128)(2,1)} %get-tuple-element.149), channel_id=1, source_target_pairs={{0,16},{1,17},{2,18},{3,19},{4,20},{5,21},{6,22},{7,23},{8,24},{9,... | collective-permute-start | bytes 6291464 | tf_op jit(solution)/shard_map/ppermute | solution.py:304
  178.2 44.3 %collective-permute-start.16 = (bf16[4,64,512]{2,1,0:T(8,128)(2,1)S(1)}, bf16[4,64,512]{2,1,0:T(8,128)(2,1)S(1)}, u32[]{:S(2)}, u32[]{:S(2)}) collective-permute-start(bf16[4,64,512]{2,1,0:T(8,128)(2,1)S(1)} %copy-done.26), channel_id=1, source_target_pairs={{0,0},{1,1},{2,2},{3,3},{4,8},{5,9},{6,10},{7,11},{8,4},{9,5},{10,... | collective-permute-start | bytes 786440 | tf_op jit(solution)/shard_map/ppermute | solution.py:310
  182.3 45.8 %collective-permute-start.17 = (bf16[4,64,512]{2,1,0:T(8,128)(2,1)S(1)}, bf16[4,64,512]{2,1,0:T(8,128)(2,1)S(1)}, u32[]{:S(2)}, u32[]{:S(2)}) collective-permute-start(bf16[4,64,512]{2,1,0:T(8,128)(2,1)S(1)} %copy-done.25), channel_id=1, source_target_pairs={{0,1},{1,0},{2,3},{3,2},{4,9},{5,8},{6,11},{7,10},{8,5},{9,4},{10,... | collective-permute-start | bytes 786440 | tf_op jit(solution)/shard_map/ppermute | solution.py:310
  183.9 50.5 %collective-permute-start.18 = (bf16[4,64,512]{2,1,0:T(8,128)(2,1)S(1)}, bf16[4,64,512]{2,1,0:T(8,128)(2,1)S(1)}, u32[]{:S(2)}, u32[]{:S(2)}) collective-permute-start(bf16[4,64,512]{2,1,0:T(8,128)(2,1)S(1)} %copy-done.24), channel_id=1, source_target_pairs={{0,2},{1,3},{2,0},{3,1},{4,10},{5,11},{6,8},{7,9},{8,6},{9,7},{10,... | collective-permute-start | bytes 786440 | tf_op jit(solution)/shard_map/ppermute | solution.py:310
  222.5 46.6 %copy-start.45 = (bf16[4,64,512]{2,1,0:T(8,128)(2,1)}, bf16[4,64,512]{2,1,0:T(8,128)(2,1)S(1)}, u32[]{:S(2)}) copy-start(bf16[4,64,512]{2,1,0:T(8,128)(2,1)S(1)} %collective-permute-done.16.refs_0_) | copy-start | bytes 786436
  222.5 15.8 %collective-permute-start.19 = (bf16[4,64,512]{2,1,0:T(8,128)(2,1)S(1)}, bf16[4,64,512]{2,1,0:T(8,128)(2,1)S(1)}, u32[]{:S(2)}, u32[]{:S(2)}) collective-permute-start(bf16[4,64,512]{2,1,0:T(8,128)(2,1)S(1)} %copy-done.23), channel_id=1, source_target_pairs={{0,3},{1,2},{2,1},{3,0},{4,11},{5,10},{6,9},{7,8},{8,7},{9,6},{10,... | collective-permute-start | bytes 786440 | tf_op jit(solution)/shard_map/ppermute | solution.py:310
  228.1 41.0 %copy-start.47 = (bf16[4,64,512]{2,1,0:T(8,128)(2,1)}, bf16[4,64,512]{2,1,0:T(8,128)(2,1)S(1)}, u32[]{:S(2)}) copy-start(bf16[4,64,512]{2,1,0:T(8,128)(2,1)S(1)} %collective-permute-done.17.refs_1_) | copy-start | bytes 786436
  228.1 10.2 %collective-permute-start.20 = (bf16[4,64,512]{2,1,0:T(8,128)(2,1)S(1)}, bf16[4,64,512]{2,1,0:T(8,128)(2,1)S(1)}, u32[]{:S(2)}, u32[]{:S(2)}) collective-permute-start(bf16[4,64,512]{2,1,0:T(8,128)(2,1)S(1)} %copy-done.22), channel_id=1, source_target_pairs={{0,8},{1,9},{2,10},{3,11},{4,0},{5,1},{6,2},{7,3},{8,12},{9,13},{1... | collective-permute-start | bytes 786440 | tf_op jit(solution)/shard_map/ppermute | solution.py:310
  234.4 18.8 %collective-permute-start.21 = (bf16[4,64,512]{2,1,0:T(8,128)(2,1)S(1)}, bf16[4,64,512]{2,1,0:T(8,128)(2,1)}, u32[]{:S(2)}, u32[]{:S(2)}) collective-permute-start(bf16[4,64,512]{2,1,0:T(8,128)(2,1)S(1)} %copy-done.21), channel_id=1, source_target_pairs={{0,9},{1,8},{2,11},{3,10},{4,1},{5,0},{6,3},{7,2},{8,13},{9,12},{1... | collective-permute-start | bytes 786440 | tf_op jit(solution)/shard_map/ppermute | solution.py:310
  238.3 14.9 %collective-permute-start.22 = (bf16[4,64,512]{2,1,0:T(8,128)(2,1)S(1)}, bf16[4,64,512]{2,1,0:T(8,128)(2,1)}, u32[]{:S(2)}, u32[]{:S(2)}) collective-permute-start(bf16[4,64,512]{2,1,0:T(8,128)(2,1)S(1)} %copy-done.20), channel_id=1, source_target_pairs={{0,10},{1,11},{2,8},{3,9},{4,2},{5,3},{6,0},{7,1},{8,14},{9,15},{1... | collective-permute-start | bytes 786440 | tf_op jit(solution)/shard_map/ppermute | solution.py:310
  239.7 19.4 %collective-permute-start.23 = (bf16[4,64,512]{2,1,0:T(8,128)(2,1)S(1)}, bf16[4,64,512]{2,1,0:T(8,128)(2,1)}, u32[]{:S(2)}, u32[]{:S(2)}) collective-permute-start(bf16[4,64,512]{2,1,0:T(8,128)(2,1)S(1)} %copy-done.19), channel_id=1, source_target_pairs={{0,11},{1,10},{2,9},{3,8},{4,3},{5,2},{6,1},{7,0},{8,15},{9,14},{1... | collective-permute-start | bytes 786440 | tf_op jit(solution)/shard_map/ppermute | solution.py:310
  269.1 96.4 %all-to-all-start.1 = ((bf16[8,12,64,512]{3,2,1,0:T(8,128)(2,1)}), bf16[8,12,64,512]{3,2,1,0:T(8,128)(2,1)}, u32[]{:S(2)}, u32[]{:S(2)}) async-start(bf16[8,12,64,512]{3,2,1,0:T(8,128)(2,1)} %bitcast.45), calls=%async_computation.1 | async-start | bytes 12582912 | tf_op jit(solution)/shard_map/all_to_all | solution.py:249
  274.8 75.7 %copy-start.14 = (bf16[4,64,512]{2,1,0:T(8,128)(2,1)S(1)}, bf16[4,64,512]{2,1,0:T(8,128)(2,1)}, u32[]{:S(2)}) copy-start(bf16[4,64,512]{2,1,0:T(8,128)(2,1)} %get-tuple-element.165) | copy-start | bytes 786436
  274.8 81.3 %copy-start.13 = (bf16[4,64,512]{2,1,0:T(8,128)(2,1)S(1)}, bf16[4,64,512]{2,1,0:T(8,128)(2,1)}, u32[]{:S(2)}) copy-start(bf16[4,64,512]{2,1,0:T(8,128)(2,1)} %get-tuple-element.166) | copy-start | bytes 786436
  274.8 89.2 %copy-start.12 = (bf16[4,64,512]{2,1,0:T(8,128)(2,1)S(1)}, bf16[4,64,512]{2,1,0:T(8,128)(2,1)}, u32[]{:S(2)}) copy-start(bf16[4,64,512]{2,1,0:T(8,128)(2,1)} %get-tuple-element.167) | copy-start | bytes 786436
  274.8 90.7 %copy-start.11 = (bf16[4,64,512]{2,1,0:T(8,128)(2,1)S(1)}, bf16[4,64,512]{2,1,0:T(8,128)(2,1)}, u32[]{:S(2)}) copy-start(bf16[4,64,512]{2,1,0:T(8,128)(2,1)} %get-tuple-element.168) | copy-start | bytes 786436
  292.3 86.5 %collective-permute-start.34 = (bf16[16,512,128]{2,1,0:T(8,128)(2,1)}, bf16[16,512,128]{2,1,0:T(8,128)(2,1)S(1)}, u32[]{:S(2)}, u32[]{:S(2)}) collective-permute-start(bf16[16,512,128]{2,1,0:T(8,128)(2,1)} %get-tuple-element.169), channel_id=1, source_target_pairs={{0,16},{1,17},{2,18},{3,19},{4,20},{5,21},{6,22},{7,23},{8,24},{9,... | collective-permute-start | bytes 6291464 | tf_op jit(solution)/shard_map/ppermute | solution.py:304
  293.0 57.4 %collective-permute-start.26 = (bf16[4,64,512]{2,1,0:T(8,128)(2,1)S(1)}, bf16[4,64,512]{2,1,0:T(8,128)(2,1)S(1)}, u32[]{:S(2)}, u32[]{:S(2)}) collective-permute-start(bf16[4,64,512]{2,1,0:T(8,128)(2,1)S(1)} %copy-done.18), channel_id=1, source_target_pairs={{0,0},{1,1},{2,2},{3,3},{4,8},{5,9},{6,10},{7,11},{8,4},{9,5},{10,... | collective-permute-start | bytes 786440 | tf_op jit(solution)/shard_map/ppermute | solution.py:310
  296.7 59.4 %collective-permute-start.27 = (bf16[4,64,512]{2,1,0:T(8,128)(2,1)S(1)}, bf16[4,64,512]{2,1,0:T(8,128)(2,1)S(1)}, u32[]{:S(2)}, u32[]{:S(2)}) collective-permute-start(bf16[4,64,512]{2,1,0:T(8,128)(2,1)S(1)} %copy-done.17), channel_id=1, source_target_pairs={{0,1},{1,0},{2,3},{3,2},{4,9},{5,8},{6,11},{7,10},{8,5},{9,4},{10,... | collective-permute-start | bytes 786440 | tf_op jit(solution)/shard_map/ppermute | solution.py:310
  298.7 65.3 %collective-permute-start.28 = (bf16[4,64,512]{2,1,0:T(8,128)(2,1)S(1)}, bf16[4,64,512]{2,1,0:T(8,128)(2,1)S(1)}, u32[]{:S(2)}, u32[]{:S(2)}) collective-permute-start(bf16[4,64,512]{2,1,0:T(8,128)(2,1)S(1)} %copy-done.16), channel_id=1, source_target_pairs={{0,2},{1,3},{2,0},{3,1},{4,10},{5,11},{6,8},{7,9},{8,6},{9,7},{10,... | collective-permute-start | bytes 786440 | tf_op jit(solution)/shard_map/ppermute | solution.py:310
  301.6 63.2 %collective-permute-start.29 = (bf16[4,64,512]{2,1,0:T(8,128)(2,1)S(1)}, bf16[4,64,512]{2,1,0:T(8,128)(2,1)S(1)}, u32[]{:S(2)}, u32[]{:S(2)}) collective-permute-start(bf16[4,64,512]{2,1,0:T(8,128)(2,1)S(1)} %copy-done.15), channel_id=1, source_target_pairs={{0,3},{1,2},{2,1},{3,0},{4,11},{5,10},{6,9},{7,8},{8,7},{9,6},{10,... | collective-permute-start | bytes 786440 | tf_op jit(solution)/shard_map/ppermute | solution.py:310
  350.5 17.1 %collective-permute-start.30 = (bf16[4,64,512]{2,1,0:T(8,128)(2,1)S(1)}, bf16[4,64,512]{2,1,0:T(8,128)(2,1)}, u32[]{:S(2)}, u32[]{:S(2)}) collective-permute-start(bf16[4,64,512]{2,1,0:T(8,128)(2,1)S(1)} %copy-done.14), channel_id=1, source_target_pairs={{0,8},{1,9},{2,10},{3,11},{4,0},{5,1},{6,2},{7,3},{8,12},{9,13},{1... | collective-permute-start | bytes 786440 | tf_op jit(solution)/shard_map/ppermute | solution.py:310
  356.1 16.2 %collective-permute-start.31 = (bf16[4,64,512]{2,1,0:T(8,128)(2,1)S(1)}, bf16[4,64,512]{2,1,0:T(8,128)(2,1)}, u32[]{:S(2)}, u32[]{:S(2)}) collective-permute-start(bf16[4,64,512]{2,1,0:T(8,128)(2,1)S(1)} %copy-done.13), channel_id=1, source_target_pairs={{0,9},{1,8},{2,11},{3,10},{4,1},{5,0},{6,3},{7,2},{8,13},{9,12},{1... | collective-permute-start | bytes 786440 | tf_op jit(solution)/shard_map/ppermute | solution.py:310
  364.0 12.0 %collective-permute-start.32 = (bf16[4,64,512]{2,1,0:T(8,128)(2,1)S(1)}, bf16[4,64,512]{2,1,0:T(8,128)(2,1)}, u32[]{:S(2)}, u32[]{:S(2)}) collective-permute-start(bf16[4,64,512]{2,1,0:T(8,128)(2,1)S(1)} %copy-done.12), channel_id=1, source_target_pairs={{0,10},{1,11},{2,8},{3,9},{4,2},{5,3},{6,0},{7,1},{8,14},{9,15},{1... | collective-permute-start | bytes 786440 | tf_op jit(solution)/shard_map/ppermute | solution.py:310
  365.5 13.3 %collective-permute-start.33 = (bf16[4,64,512]{2,1,0:T(8,128)(2,1)S(1)}, bf16[4,64,512]{2,1,0:T(8,128)(2,1)}, u32[]{:S(2)}, u32[]{:S(2)}) collective-permute-start(bf16[4,64,512]{2,1,0:T(8,128)(2,1)S(1)} %copy-done.11), channel_id=1, source_target_pairs={{0,11},{1,10},{2,9},{3,8},{4,3},{5,2},{6,1},{7,0},{8,15},{9,14},{1... | collective-permute-start | bytes 786440 | tf_op jit(solution)/shard_map/ppermute | solution.py:310
  380.1 81.4 %all-to-all-start.2 = ((bf16[8,12,64,512]{3,2,1,0:T(8,128)(2,1)}), bf16[8,12,64,512]{3,2,1,0:T(8,128)(2,1)}, u32[]{:S(2)}, u32[]{:S(2)}) async-start(bf16[8,12,64,512]{3,2,1,0:T(8,128)(2,1)} %bitcast.46), calls=%async_computation.2 | async-start | bytes 12582912 | tf_op jit(solution)/shard_map/all_to_all | solution.py:249
  408.0 53.5 %collective-permute-start.35 = (bf16[16,512,128]{2,1,0:T(8,128)(2,1)}, bf16[16,512,128]{2,1,0:T(8,128)(2,1)S(1)}, u32[]{:S(2)}, u32[]{:S(2)}) collective-permute-start(bf16[16,512,128]{2,1,0:T(8,128)(2,1)} %get-tuple-element.180), channel_id=1, source_target_pairs={{0,16},{1,17},{2,18},{3,19},{4,20},{5,21},{6,22},{7,23},{8,24},{9,... | collective-permute-start | bytes 6291464 | tf_op jit(solution)/shard_map/ppermute | solution.py:304
  462.8 23.5 %all-to-all-start.3 = ((bf16[8,12,16,512]{3,2,1,0:T(8,128)(2,1)}), bf16[8,12,16,512]{3,2,1,0:T(8,128)(2,1)S(1)}, u32[]{:S(2)}, u32[]{:S(2)}) async-start(bf16[8,12,16,512]{3,2,1,0:T(8,128)(2,1)} %bitcast.52), calls=%async_computation.3 | async-start | bytes 3145728 | tf_op jit(solution)/shard_map/all_to_all | solution.py:249
  501.5 40.4 %all-to-all-start.4 = ((bf16[8,12,16,512]{3,2,1,0:T(8,128)(2,1)}), bf16[8,12,16,512]{3,2,1,0:T(8,128)(2,1)S(1)}, u32[]{:S(2)}, u32[]{:S(2)}) async-start(bf16[8,12,16,512]{3,2,1,0:T(8,128)(2,1)} %bitcast.23), calls=%async_computation.4 | async-start | bytes 3145728 | tf_op jit(solution)/shard_map/all_to_all | solution.py:249
  505.2 52.0 %collective-permute-start.36 = (bf16[16,512,128]{2,1,0:T(8,128)(2,1)}, bf16[16,512,128]{2,1,0:T(8,128)(2,1)}, u32[]{:S(2)}, u32[]{:S(2)}) collective-permute-start(bf16[16,512,128]{2,1,0:T(8,128)(2,1)} %finished.4), channel_id=1, source_target_pairs={{0,16},{1,17},{2,18},{3,19},{8,20},{9,21},{10,22},{11,23},{4,24},{... | collective-permute-start | bytes 6291464 | tf_op jit(solution)/shard_map/ppermute | solution.py:341
  557.2 39.7 %all-to-all-start.5 = ((bf16[8,12,16,512]{3,2,1,0:T(8,128)(2,1)}), bf16[8,12,16,512]{3,2,1,0:T(8,128)(2,1)S(1)}, u32[]{:S(2)}, u32[]{:S(2)}) async-start(bf16[8,12,16,512]{3,2,1,0:T(8,128)(2,1)} %bitcast.22), calls=%async_computation.5 | async-start | bytes 3145728 | tf_op jit(solution)/shard_map/all_to_all | solution.py:249
  560.9 51.1 %collective-permute-start.37 = (bf16[16,512,128]{2,1,0:T(8,128)(2,1)}, bf16[16,512,128]{2,1,0:T(8,128)(2,1)}, u32[]{:S(2)}, u32[]{:S(2)}) collective-permute-start(bf16[16,512,128]{2,1,0:T(8,128)(2,1)} %finished.5), channel_id=1, source_target_pairs={{0,16},{1,17},{2,18},{3,19},{8,20},{9,21},{10,22},{11,23},{4,24},{... | collective-permute-start | bytes 6291464 | tf_op jit(solution)/shard_map/ppermute | solution.py:341
  612.1 53.8 %all-to-all-start.6 = ((bf16[8,12,16,512]{3,2,1,0:T(8,128)(2,1)}), bf16[8,12,16,512]{3,2,1,0:T(8,128)(2,1)S(1)}, u32[]{:S(2)}, u32[]{:S(2)}) async-start(bf16[8,12,16,512]{3,2,1,0:T(8,128)(2,1)} %bitcast.21), calls=%async_computation.6 | async-start | bytes 3145728 | tf_op jit(solution)/shard_map/all_to_all | solution.py:249
  615.8 50.1 %collective-permute-start.38 = (bf16[16,512,128]{2,1,0:T(8,128)(2,1)}, bf16[16,512,128]{2,1,0:T(8,128)(2,1)}, u32[]{:S(2)}, u32[]{:S(2)}) collective-permute-start(bf16[16,512,128]{2,1,0:T(8,128)(2,1)} %finished.6), channel_id=1, source_target_pairs={{0,16},{1,17},{2,18},{3,19},{8,20},{9,21},{10,22},{11,23},{4,24},{... | collective-permute-start | bytes 6291464 | tf_op jit(solution)/shard_map/ppermute | solution.py:341
  681.2 47.5 %collective-permute-start.39 = (bf16[16,512,128]{2,1,0:T(8,128)(2,1)}, bf16[16,512,128]{2,1,0:T(8,128)(2,1)S(1)}, u32[]{:S(2)}, u32[]{:S(2)}) collective-permute-start(bf16[16,512,128]{2,1,0:T(8,128)(2,1)} %finished.7), channel_id=1, source_target_pairs={{0,16},{1,17},{2,18},{3,19},{8,20},{9,21},{10,22},{11,23},{4,24},{... | collective-permute-start | bytes 6291464 | tf_op jit(solution)/shard_map/ppermute | solution.py:341
  (38 other events, 427.7 us)
Sparse Core Ops, SparseCore 0:
  8.9 84.7 all-gather.2

commit v4 on v3

--- a/solution.py
+++ b/solution.py
@@ -8,6 +8,7 @@
 TICKS = 2
 ENDS = (4, 8, 12, 16)
 ROW_TILE = 16
+PIECE = 512
 AXES = ("lane", "core", "half", "rest")
 GROUP = ("core", "rest")
 VMEM = pltpu.CompilerParams(vmem_limit_bytes=58 << 20)
@@ -114,18 +115,21 @@
     )(table, which, blocks)
 
 
-def relayed(values, member, first, second, row_chunks):
+def relayed(values, member, first, second, targets, start):
+    row_chunks = len(targets)
     members = len(values)
     each, rows, width = values[0].shape
     lines = first[0].shape[0]
     wide = width // lines
     per = wide // rows
-    pair = 2 if each % 2 == 0 else 1
+    pair = 2 if each % 2 == 0 and start % 2 == 0 else 1
+    base = start // pair
+    given = targets if start else []
     height = rows // row_chunks
 
     def body(member_ref, *refs):
         pieces, mats = refs[:members], refs[members : members + 6]
-        outs, (source, kept, one, two) = refs[members + 6 : members + 6 + row_chunks], refs[members + 6 + row_chunks :]
+        outs, (source, kept, one, two) = refs[-4 - row_chunks : -4], refs[-4:]
         for k in range(members):
             source[member_ref[0] ^ k] = pieces[k][...]
 
@@ -151,15 +155,15 @@
                     for r in range(row_chunks):
                         outs[r][per * i : per * (i + 1), term, ch] = split[:, r]
 
-        def given(ch, i):
+        def fresh(ch, i):
             return source[per * i : per * (i + 1), ch].reshape(wide, width)
 
         def held(s, i):
             if s < pair:
-                return given(s, i)
+                return fresh(s, i)
             return kept[s - pair, i * wide : (i + 1) * wide]
 
-        shears(given, 0, [(0, ch) for ch in range(pair)])
+        shears(fresh, 0, [(0, ch) for ch in range(pair)])
         shears(held, 1, [(term, ch) for term in (1, 2) for ch in range(pair)])
 
     mat = pl.BlockSpec(first[0].shape, lambda c, _: (0, 0, 0), pipeline_mode=pl.Buffered(1))
@@ -168,8 +172,10 @@
         grid_spec=pltpu.PrefetchScalarGridSpec(
             num_scalar_prefetch=1,
             grid=(each // pair,),
-            in_specs=[pl.BlockSpec((pair, rows, width), lambda c, _: (c, 0, 0))] * members + [mat] * 6,
-            out_specs=[pl.BlockSpec((members, 3, pair, height, width), lambda c, _: (0, 0, c, 0, 0))] * row_chunks,
+            in_specs=[pl.BlockSpec((pair, rows, width), lambda c, _: (c, 0, 0))] * members
+            + [mat] * 6
+            + [pl.BlockSpec(memory_space=pl.ANY)] * len(given),
+            out_specs=[pl.BlockSpec((members, 3, pair, height, width), lambda c, _: (0, 0, base + c, 0, 0))] * row_chunks,
             scratch_shapes=[
                 pltpu.VMEM((members, pair, rows, width), jnp.bfloat16),
                 pltpu.VMEM((pair, width, width), jnp.bfloat16),
@@ -177,17 +183,18 @@
                 pltpu.VMEM((2 * pair, width, width), jnp.bfloat16),
             ],
         ),
-        out_shape=[jax.ShapeDtypeStruct((members, 3, each, height, width), jnp.bfloat16)] * row_chunks,
+        out_shape=[jax.ShapeDtypeStruct(target.shape, jnp.bfloat16) for target in targets],
+        input_output_aliases={1 + members + 6 + r: r for r in range(len(given))},
         compiler_params=VMEM,
         cost_estimate=cost(*values * 4, *first, *second, products=18 * members * values[0].size * width),
         name="relayed",
-    )(member, *values, *first, *second)
+    )(member, *values, *first, *second, *given)
 
 
 def finished(terms, last, mixes, row_chunk):
     members, _, _, rows, width = last.shape
     channels = mixes[0].shape[0]
-    piece = min(width, 128)
+    piece = min(width, PIECE)
     count = len(terms) + 1
 
     def body(*refs):
@@ -235,7 +242,7 @@
     return pl.pallas_call(
         body,
         grid=(width // piece,),
-        in_specs=[block, block] + [pl.BlockSpec(memory_space=pl.ANY)] * len(given),
+        in_specs=[block, pl.BlockSpec((rows, piece, channels), lambda i: (row_chunk, i, 0))] + [pl.BlockSpec(memory_space=pl.ANY)] * len(given),
         out_specs=pl.BlockSpec((rows, piece, channels), lambda i: (row_chunk, i, 0)),
         out_shape=jax.ShapeDtypeStruct(shape, jnp.float32),
         input_output_aliases={2: 0} if given else {},
@@ -299,10 +306,6 @@
         sent = spread(memory[0], cut(channels // members, ENDS), members, band)
         last = len(sent) - 1
 
-        def shifted(r, *waits):
-            rows = memory[0, r * ROW_TILE : (r + 1) * ROW_TILE].astype(jnp.bfloat16)
-            return lax.ppermute(tied(rows, *waits), AXES, shift_route)
-
         def delivered(k, *waits):
             pieces = sent[k]
             if waits:
@@ -312,22 +315,25 @@
         def later(values, *waits):
             return lax.optimization_barrier((*values, *waits))[: len(values)]
 
-        full = delivered(0, packs)
-        terms, olds = [], []
+        sizes = [pieces[0].shape[0] for pieces in sent]
+        starts = starts_of(sizes)
+
+        def room(each, rows):
+            return jax.ShapeDtypeStruct((members, 3, each, rows, width), jnp.bfloat16)
+
+        full = [delivered(0, packs)]
+        solved = [room(starts[last], height)]
         for k in range(last):
-            (solved,) = relayed(full, member, *weights, 1)
-            waits = [solved] if k else []
-            if terms:
-                terms[-1], solved = later([terms[-1], solved])
-            full = delivered(k + 1, *full, *waits)
-            if k:
-                olds += [shifted(r, *olds[-1:], *waits) for r in range(len(olds), -(-row_chunks * k // last))]
-            (solved,) = later([solved], *full, *olds)
-            terms.append(exchanged(solved.reshape(members, -1, height, width)).reshape(solved.shape))
-        solved = relayed(full, member, *weights, row_chunks)
-        olds += [shifted(r, *olds[-1:], solved[0]) for r in range(len(olds), row_chunks)]
-        terms[-1], *solved = later([terms[-1], *solved])
-        solved = later(solved, *olds)
+            waits = [*weights[0], *weights[1]] if k == 1 else earlier if k > 1 else []
+            full.append(delivered(k + 1, *full[k], *waits))
+            earlier = solved
+            solved = relayed(full[k], member, *weights, solved, starts[k])
+        ends = relayed(full[last], member, *weights, [room(sizes[last], ROW_TILE)] * row_chunks, 0)
+        (solved,) = later(solved, *full[last])
+        old = lax.ppermute(tied(memory[0].astype(jnp.bfloat16), *full[last]), AXES, shift_route)
+        terms = [exchanged(solved.reshape(members, -1, height, width)).reshape(solved.shape)]
+        terms[0], *solved = later([terms[0], *ends])
+        solved = later(solved, old)
 
         out, rows = None, None
         moved = []
@@ -335,12 +341,11 @@
             waits = ([rows] if r else []) + (moved[r - 2 : r - 1] if r > 1 else [])
             field = solved[r].reshape(members, -1, ROW_TILE, width)
             field = exchanged(tied(field, *waits) if waits else field)
-            if r > 1 and r == row_chunks - 1:
-                field = tied(field, moved[-1])
             rows = finished(terms, field.reshape(solved[r].shape), mixes, r)
-            moved.append(lax.ppermute(rows, AXES, return_route))
+            ending = r > 1 and r == row_chunks - 1
+            moved.append(lax.ppermute(tied(rows, moved[-1]) if ending else rows, AXES, return_route))
         for r in range(row_chunks):
-            out = placed(moved[r], olds[r], out, r, out_shape)
+            out = placed(moved[r], old, out, r, out_shape)
         return out[None]
 
     return jax.shard_map(

time: 743 us -> 707 us (0.952); the launches traced: 742 us -> 698 us
  Pallas kernels: 183 us -> 162 us
  starting transfers between devices: 112 us -> 101 us
  local copies, waits for them, and re-layouts: 15.9 us -> 8.05 us
    all_to_all x7 -> x5, waiting for transfers between devices: 143 us -> 297 us  [exchanged(): lax.all_to_all(values, GROUP, split_axis=0, concat_axis=0, tiled=True)]
    ppermute x32, waiting for transfers between devices: 157 us -> 53 us  [delivered(): lax.ppermute(piece, AXES, route)]
    ppermute x8 -> x5, waiting for transfers between devices: 93.3 us -> 44.6 us  [the longest x4 44.6 us: on_device(): lax.ppermute(tied(rows, moved[-1]) if ending else rows, AXES, return_route)]
    pallas_call x4, Pallas kernels: 56.4 us -> 35.4 us  [finished(): pl.pallas_call(body, grid=(width // piece,), in_specs=[term_block(a, row_...]
    all_to_all x7 -> x5, starting transfers between devices: 35.7 us -> 21.1 us  [exchanged(): lax.all_to_all(values, GROUP, split_axis=0, concat_axis=0, tiled=True)]
    convert_element_type x0 -> x1, other arithmetic: none -> 9.17 us  [on_device(): memory[0].astype(jnp.bfloat16)]
    all_gather x1, waiting for transfers between devices: 8.8 us -> 0.01 us  [on_device(): all_blocks = lax.all_gather(shear_blocks[0], pipe)]
    ppermute x8 -> x5, starting transfers between devices: 4.64 us -> 12.5 us  [the longest x4 11.8 us: on_device(): lax.ppermute(tied(rows, moved[-1]) if ending else rows, AXES, return_route)]
  transfers between devices with their start and end apart: 48 -> 43, of which waited for: 29 -> 22; matrix products, arithmetic and copies ran while one was open for 2% -> 2% of each run, Pallas kernels for 20% -> 21%
where the time goes in v4:
time: 707 us; the launch traced here: 698 us
  waiting for transfers between devices  395 us (56%)
  Pallas kernels  162 us (23%)
  starting transfers between devices  101 us (14%)
  between operations  14.6 us (2%)
  other arithmetic  9.93 us (1%)
  local copies, waits for them, and re-layouts  8.05 us (1%)
    all_to_all x5, waiting for transfers between devices, exchanged(): lax.all_to_all(values, GROUP, split_axis=0, concat_axis=0, tiled=True)  297 us
    pallas_call x4, Pallas kernels, relayed(): pl.pallas_call(body, grid_spec=pltpu.PrefetchScalarGridSpec(num_scalar_pr...  69.7 us
    ppermute x32, starting transfers between devices, delivered(): lax.ppermute(piece, AXES, route)  67.8 us
    ppermute x32, waiting for transfers between devices, delivered(): lax.ppermute(piece, AXES, route)  53 us
    ppermute x4, waiting for transfers between devices, on_device(): lax.ppermute(tied(rows, moved[-1]) if ending else rows, AXES, return_route)  44.6 us
    pallas_call x4, Pallas kernels, finished(): pl.pallas_call(body, grid=(width // piece,), in_specs=[term_block(a, row_...  35.4 us
    pallas_call x6, Pallas kernels, dense(): pl.pallas_call(body, grid_spec=pltpu.PrefetchScalarGridSpec(num_scalar_pr...  26.8 us
    all_to_all x5, starting transfers between devices, exchanged(): lax.all_to_all(values, GROUP, split_axis=0, concat_axis=0, tiled=True)  21.1 us
  transfers between devices with their start and end apart: 43, of which 22 were waited for; matrix products, arithmetic and copies ran while one was open for 2% of the time, Pallas kernels for 21%

profile of v4, /device:TPU:1, one launch (start us, length us, event | category | flops | bytes accessed | tf_op | source)
XLA Modules:
  0.0 697.6 jit_solution(15313215715032747024)
XLA Ops:
  7.7 11.0 %spread.1 = (bf16[4,64,512]{2,1,0:T(8,128)(2,1)}, bf16[4,64,512]{2,1,0:T(8,128)(2,1)}, bf16[4,64,512]{2,1,0:T(8,128)(2,1)}, bf16[4,64,512]{2,1,0:T(8,128)(2,1)},...) custom-call(s32[1]{0:T(128)} %bitcast.1.band_ref, ...), custom_call_target="tpu_custom_call" | custom-call | bytes 33554432 | tf_op jit(solution)/shard_map/spread/pallas_call | solution.py:53
  18.8 6.7 all-gather
  25.5 5.0 collective-permute-start
  30.4 1.3 collective-permute-start.1
  31.8 3.3 collective-permute-start.2
  35.1 1.5 collective-permute-done.refs_0_
  36.9 6.7 collective-permute-done.1.refs_1_
  43.5 3.8 collective-permute-done.2.refs_2_
  47.3 5.2 collective-permute-done.3.refs_3_
  53.7 3.9 collective-permute-done.5.refs_5_
  57.6 4.5 collective-permute-done.6.refs_6_
  62.1 2.8 collective-permute-done.7.refs_7_
  65.0 13.9 %collective-permute-start.8 = (bf16[4,64,512]{2,1,0:T(8,128)(2,1)}, bf16[4,64,512]{2,1,0:T(8,128)(2,1)S(1)}, u32[]{:S(2)}, u32[]{:S(2)}) collective-permute-start(bf16[4,64,512]{2,1,0:T(8,128)(2,1)} %get-tuple-element.120), channel_id=1, source_target_pairs={{0,0},{1,1},{2,2},{3,3},{4,8},{5,9},{6,10},{7,11},{8,4},{9,5},{10,... | collective-permute-start | bytes 786440 | tf_op jit(solution)/shard_map/ppermute | solution.py:313
  78.9 1.3 collective-permute-start.9
  80.3 2.7 collective-permute-start.10
  84.4 1.3 collective-permute-start.13
  85.7 5.5 collective-permute-done.9.refs_1_
  92.0 7.0 %collective-permute-done.10.refs_2_ = bf16[4,64,512]{2,1,0:T(8,128)(2,1)S(1)} collective-permute-done((bf16[4,64,512]{2,1,0:T(8,128)(2,1)}, bf16[4,64,512]{2,1,0:T(8,128)(2,1)S(1)}, u32[]{:S(2)}, u32[]{:S(2)}) %collective-permute-start.10) | collective-permute-done | bytes 262176 | tf_op jit(solution)/shard_map/ppermute | solution.py:313
  99.6 4.5 dense.6.refs_8_
  104.2 4.4 dense.7.refs_9_
  108.6 4.5 dense.8.refs_10_
  113.1 4.5 dense.9.refs_11_
  117.5 4.4 dense.10.refs_12_
  121.9 4.6 dense.11.refs_13_
  126.6 6.7 collective-permute-start.16
  133.6 4.3 collective-permute-start.19
  137.9 3.2 collective-permute-done.16.refs_0_
  141.2 5.1 collective-permute-done.17.refs_1_
  146.2 2.6 collective-permute-done.18.refs_2_
  148.8 1.3 collective-permute-start.23
  150.2 17.5 %relayed.4.refs_14_ = bf16[8,3,12,64,512]{4,3,2,1,0:T(8,128)(2,1)} custom-call(s32[1]{0:T(128)} %bitcast.member_ref, bf16[4,64,512]{2,1,0:T(8,128)(2,1)} %copy-done.24, bf16[4,64,512]{2,1,0:T(8,128)(2,1)} %copy-done.25, bf16[4,64,512]{2,1,0:T(8,128)(2,1)} %copy-done.26, bf16[4,64,512]{2,1,0:T(8,128)(2,1)} %copy-done.27, bf16[4,64,512]{2,1,0:T(8,128)(2,1)} %copy-done.28, ...), custom_call_target="tpu_custom_call" | custom-call | flops 19327352832 | bytes 20971520 | tf_op jit(solution)/shard_map/relayed/pallas_call | solution.py:170
  167.8 13.9 %collective-permute-start.24 = (bf16[4,64,512]{2,1,0:T(8,128)(2,1)S(1)}, bf16[4,64,512]{2,1,0:T(8,128)(2,1)S(1)}, u32[]{:S(2)}, u32[]{:S(2)}) collective-permute-start(bf16[4,64,512]{2,1,0:T(8,128)(2,1)S(1)} %copy-done.15), channel_id=1, source_target_pairs={{0,0},{1,1},{2,2},{3,3},{4,8},{5,9},{6,10},{7,11},{8,4},{9,5},{10,... | collective-permute-start | bytes 786440 | tf_op jit(solution)/shard_map/ppermute | solution.py:313
  182.3 3.9 collective-permute-start.27
  186.4 17.4 %relayed.5.refs_14_ = bf16[8,3,12,64,512]{4,3,2,1,0:T(8,128)(2,1)} custom-call(s32[1]{0:T(128)} %bitcast.member_ref, bf16[4,64,512]{2,1,0:T(8,128)(2,1)} %copy-done.29, bf16[4,64,512]{2,1,0:T(8,128)(2,1)} %copy-done.30, bf16[4,64,512]{2,1,0:T(8,128)(2,1)} %copy-done.32, ...), custom_call_target="tpu_custom_call", output_to_operand_aliasing={{}: (15, {})} | custom-call | flops 19327352832 | bytes 20971520 | tf_op jit(solution)/shard_map/relayed/pallas_call | solution.py:170
  204.1 2.2 collective-permute-start.30
  206.3 2.8 collective-permute-start.31
  209.1 17.4 %relayed.6 = bf16[8,3,12,64,512]{4,3,2,1,0:T(8,128)(2,1)} custom-call(s32[1]{0:T(128)} %bitcast.member_ref, bf16[4,64,512]{2,1,0:T(8,128)(2,1)} %copy-done.35, bf16[4,64,512]{2,1,0:T(8,128)(2,1)} %copy-done.36, bf16[4,64,512]{2,1,0:T(8,128)(2,1)} %copy-done.37, bf16[4,64,512]{2,1,0:T(8,128)(2,1)} %copy-done.38, ...), custom_call_target="tpu_custom_call", output_to_operand_aliasing={{}: (15, {})} | custom-call | flops 19327352832 | bytes 20971520 | tf_op jit(solution)/shard_map/relayed/pallas_call | solution.py:170
  227.7 6.2 all-to-all-start
  233.9 9.2 %bitcast_convert_fusion = bf16[64,512,128]{2,1,0:T(8,128)(2,1)} fusion(f32[1,64,512,128]{3,2,1,0:T(8,128)} %param.5), kind=kLoop, calls=%fused_computation.16 | loop fusion | flops 4194304 | bytes 25165824 | tf_op jit(solution)/shard_map/convert_element_type | solution.py:333
  243.8 17.4 %relayed.7 = (bf16[8,3,4,16,512]{4,3,2,1,0:T(8,128)(2,1)}, bf16[8,3,4,16,512]{4,3,2,1,0:T(8,128)(2,1)}, bf16[8,3,4,16,512]{4,3,2,1,0:T(8,128)(2,1)}, bf16[8,3,4,16,512]{4,3,2,1,0:T(8,128)(2,1)}) custom-call(s32[1]{0:T(128)} %bitcast.member_ref, bf16[4,64,512]{2,1,0:T(8,128)(2,1)} %copy-done.41, bf16[4,64,512]{2,1,0:T(8,128)(2,1)} %copy-done.43, ...), custom_call_target="tpu_custom_call" | custom-call | flops 19327352832 | bytes 20971520 | tf_op jit(solution)/shard_map/relayed/pallas_call | solution.py:170
  261.1 176.9 %all-to-all-done = bf16[8,36,64,512]{3,2,1,0:T(8,128)(2,1)} async-done(((bf16[8,36,64,512]{3,2,1,0:T(8,128)(2,1)}), bf16[8,36,64,512]{3,2,1,0:T(8,128)(2,1)}, u32[]{:S(2)}, u32[]{:S(2)}) %all-to-all-start) | async-done | bytes 18874400 | tf_op jit(solution)/shard_map/all_to_all | solution.py:256
  438.0 3.5 all-to-all-start.1
  442.2 19.1 %all-to-all-done.1 = bf16[8,12,16,512]{3,2,1,0:T(8,128)(2,1)S(1)} async-done(((bf16[8,12,16,512]{3,2,1,0:T(8,128)(2,1)}), bf16[8,12,16,512]{3,2,1,0:T(8,128)(2,1)S(1)}, u32[]{:S(2)}, u32[]{:S(2)}) %all-to-all-start.1) | async-done | bytes 1572896 | tf_op jit(solution)/shard_map/all_to_all | solution.py:256
  462.4 8.8 %finished.4 = bf16[16,512,128]{2,1,0:T(8,128)(2,1)} custom-call(bf16[8,3,12,64,512]{4,3,2,1,0:T(8,128)(2,1)} %bitcast.12.refs_0_, bf16[8,3,4,16,512]{4,3,2,1,0:T(8,128)(2,1)} %bitcast.35, bf16[128,128]{1,0:T(8,128)(2,1)} %get-tuple-element.172.refs_2_, bf16[128,128]{1,0:T(8,128)(2,1)} %get-tuple-element.171.refs_3_), custom_call_target="tpu_custom_call" | custom-call | bytes 4718592 | tf_op jit(solution)/shard_map/finished/pallas_call | solution.py:219
  471.3 4.0 all-to-all-start.2
  475.3 3.5 collective-permute-start.33
  478.8 33.9 %all-to-all-done.2 = bf16[8,12,16,512]{3,2,1,0:T(8,128)(2,1)S(1)} async-done(((bf16[8,12,16,512]{3,2,1,0:T(8,128)(2,1)}), bf16[8,12,16,512]{3,2,1,0:T(8,128)(2,1)S(1)}, u32[]{:S(2)}, u32[]{:S(2)}) %all-to-all-start.2) | async-done | bytes 1572896 | tf_op jit(solution)/shard_map/all_to_all | solution.py:256
  513.9 8.9 %finished.5 = bf16[16,512,128]{2,1,0:T(8,128)(2,1)} custom-call(bf16[8,3,12,64,512]{4,3,2,1,0:T(8,128)(2,1)} %bitcast.12.refs_0_, bf16[8,3,4,16,512]{4,3,2,1,0:T(8,128)(2,1)} %bitcast.37, bf16[128,128]{1,0:T(8,128)(2,1)} %get-tuple-element.172.refs_2_, bf16[128,128]{1,0:T(8,128)(2,1)} %get-tuple-element.171.refs_3_), custom_call_target="tpu_custom_call" | custom-call | bytes 4718592 | tf_op jit(solution)/shard_map/finished/pallas_call | solution.py:219
  522.8 2.7 collective-permute-done.33.source
  525.4 3.5 all-to-all-start.3
  529.0 4.0 collective-permute-start.34
  533.0 33.5 %all-to-all-done.3 = bf16[8,12,16,512]{3,2,1,0:T(8,128)(2,1)S(1)} async-done(((bf16[8,12,16,512]{3,2,1,0:T(8,128)(2,1)}), bf16[8,12,16,512]{3,2,1,0:T(8,128)(2,1)S(1)}, u32[]{:S(2)}, u32[]{:S(2)}) %all-to-all-start.3) | async-done | bytes 1572896 | tf_op jit(solution)/shard_map/all_to_all | solution.py:256
  567.7 8.8 %finished.6 = bf16[16,512,128]{2,1,0:T(8,128)(2,1)} custom-call(bf16[8,3,12,64,512]{4,3,2,1,0:T(8,128)(2,1)} %bitcast.12.refs_0_, bf16[8,3,4,16,512]{4,3,2,1,0:T(8,128)(2,1)} %bitcast.38, bf16[128,128]{1,0:T(8,128)(2,1)} %get-tuple-element.172.refs_2_, bf16[128,128]{1,0:T(8,128)(2,1)} %get-tuple-element.171.refs_3_), custom_call_target="tpu_custom_call" | custom-call | bytes 4718592 | tf_op jit(solution)/shard_map/finished/pallas_call | solution.py:219
  576.5 3.0 collective-permute-done.34.source
  579.6 3.9 all-to-all-start.4
  583.5 4.2 collective-permute-start.35
  587.7 33.3 %all-to-all-done.4 = bf16[8,12,16,512]{3,2,1,0:T(8,128)(2,1)S(1)} async-done(((bf16[8,12,16,512]{3,2,1,0:T(8,128)(2,1)}), bf16[8,12,16,512]{3,2,1,0:T(8,128)(2,1)S(1)}, u32[]{:S(2)}, u32[]{:S(2)}) %all-to-all-start.4) | async-done | bytes 1572896 | tf_op jit(solution)/shard_map/all_to_all | solution.py:256
  622.2 8.8 %finished.7 = bf16[16,512,128]{2,1,0:T(8,128)(2,1)} custom-call(bf16[8,3,12,64,512]{4,3,2,1,0:T(8,128)(2,1)} %bitcast.12.refs_0_, bf16[8,3,4,16,512]{4,3,2,1,0:T(8,128)(2,1)} %bitcast.36, bf16[128,128]{1,0:T(8,128)(2,1)} %get-tuple-element.172.refs_2_, bf16[128,128]{1,0:T(8,128)(2,1)} %get-tuple-element.171.refs_3_), custom_call_target="tpu_custom_call" | custom-call | bytes 4718592 | tf_op jit(solution)/shard_map/finished/pallas_call | solution.py:219
  631.1 3.2 collective-permute-done.35.source
  634.3 4.8 placed.4.refs_0_
  639.0 4.8 placed.5.refs_0_
  643.8 4.8 placed.6.refs_0_
  648.5 35.7 %collective-permute-done.36.source = bf16[16,512,128]{2,1,0:T(8,128)(2,1)S(1)} collective-permute-done((bf16[16,512,128]{2,1,0:T(8,128)(2,1)}, bf16[16,512,128]{2,1,0:T(8,128)(2,1)S(1)}, u32[]{:S(2)}, u32[]{:S(2)}) %collective-permute-start.36) | collective-permute-done | bytes 2097184 | tf_op jit(solution)/shard_map/ppermute | solution.py:346
  685.5 4.8 placed.7
  (157 shorter events, 15.2 us)
Async XLA Ops:
  6.5 93.1 %all-gather.3.cloned.1.call-start = ((), (), s32[]{:S(2)}) async-start(), calls=%async_computation.5 | async-start | bytes 15728640 | tf_op jit(solution)/shard_map/all_gather | solution.py:289
  25.5 11.2 %collective-permute-start = (bf16[4,64,512]{2,1,0:T(8,128)(2,1)}, bf16[4,64,512]{2,1,0:T(8,128)(2,1)S(1)}, u32[]{:S(2)}, u32[]{:S(2)}) collective-permute-start(bf16[4,64,512]{2,1,0:T(8,128)(2,1)} %get-tuple-element.112), channel_id=1, source_target_pairs={{0,0},{1,1},{2,2},{3,3},{4,8},{5,9},{6,10},{7,11},{8,4},{9,5},{10,... | collective-permute-start | bytes 786440 | tf_op jit(solution)/shard_map/ppermute | solution.py:313
  30.4 13.1 %collective-permute-start.1 = (bf16[4,64,512]{2,1,0:T(8,128)(2,1)}, bf16[4,64,512]{2,1,0:T(8,128)(2,1)S(1)}, u32[]{:S(2)}, u32[]{:S(2)}) collective-permute-start(bf16[4,64,512]{2,1,0:T(8,128)(2,1)} %get-tuple-element.113), channel_id=1, source_target_pairs={{0,1},{1,0},{2,3},{3,2},{4,9},{5,8},{6,11},{7,10},{8,5},{9,4},{10,... | collective-permute-start | bytes 786440 | tf_op jit(solution)/shard_map/ppermute | solution.py:313
  31.8 15.5 %collective-permute-start.2 = (bf16[4,64,512]{2,1,0:T(8,128)(2,1)}, bf16[4,64,512]{2,1,0:T(8,128)(2,1)S(1)}, u32[]{:S(2)}, u32[]{:S(2)}) collective-permute-start(bf16[4,64,512]{2,1,0:T(8,128)(2,1)} %get-tuple-element.114), channel_id=1, source_target_pairs={{0,2},{1,3},{2,0},{3,1},{4,10},{5,11},{6,8},{7,9},{8,6},{9,7},{10,... | collective-permute-start | bytes 786440 | tf_op jit(solution)/shard_map/ppermute | solution.py:313
  35.1 17.4 %collective-permute-start.3 = (bf16[4,64,512]{2,1,0:T(8,128)(2,1)}, bf16[4,64,512]{2,1,0:T(8,128)(2,1)S(1)}, u32[]{:S(2)}, u32[]{:S(2)}) collective-permute-start(bf16[4,64,512]{2,1,0:T(8,128)(2,1)} %get-tuple-element.115), channel_id=1, source_target_pairs={{0,3},{1,2},{2,1},{3,0},{4,11},{5,10},{6,9},{7,8},{8,7},{9,6},{10,... | collective-permute-start | bytes 786440 | tf_op jit(solution)/shard_map/ppermute | solution.py:313
  35.1 18.6 %collective-permute-start.4 = (bf16[4,64,512]{2,1,0:T(8,128)(2,1)}, bf16[4,64,512]{2,1,0:T(8,128)(2,1)S(1)}, u32[]{:S(2)}, u32[]{:S(2)}) collective-permute-start(bf16[4,64,512]{2,1,0:T(8,128)(2,1)} %get-tuple-element.116), channel_id=1, source_target_pairs={{0,8},{1,9},{2,10},{3,11},{4,0},{5,1},{6,2},{7,3},{8,12},{9,13},{1... | collective-permute-start | bytes 786440 | tf_op jit(solution)/shard_map/ppermute | solution.py:313
  36.6 67.5 %copy-start.24 = (bf16[4,64,512]{2,1,0:T(8,128)(2,1)}, bf16[4,64,512]{2,1,0:T(8,128)(2,1)S(1)}, u32[]{:S(2)}) copy-start(bf16[4,64,512]{2,1,0:T(8,128)(2,1)S(1)} %collective-permute-done.refs_0_) | copy-start | bytes 786436
  36.6 21.0 %collective-permute-start.5 = (bf16[4,64,512]{2,1,0:T(8,128)(2,1)}, bf16[4,64,512]{2,1,0:T(8,128)(2,1)S(1)}, u32[]{:S(2)}, u32[]{:S(2)}) collective-permute-start(bf16[4,64,512]{2,1,0:T(8,128)(2,1)} %get-tuple-element.117), channel_id=1, source_target_pairs={{0,9},{1,8},{2,11},{3,10},{4,1},{5,0},{6,3},{7,2},{8,13},{9,12},{1... | collective-permute-start | bytes 786440 | tf_op jit(solution)/shard_map/ppermute | solution.py:313
  43.5 60.6 %copy-start.25 = (bf16[4,64,512]{2,1,0:T(8,128)(2,1)}, bf16[4,64,512]{2,1,0:T(8,128)(2,1)S(1)}, u32[]{:S(2)}) copy-start(bf16[4,64,512]{2,1,0:T(8,128)(2,1)S(1)} %collective-permute-done.1.refs_1_) | copy-start | bytes 786436
  43.5 18.6 %collective-permute-start.6 = (bf16[4,64,512]{2,1,0:T(8,128)(2,1)}, bf16[4,64,512]{2,1,0:T(8,128)(2,1)S(1)}, u32[]{:S(2)}, u32[]{:S(2)}) collective-permute-start(bf16[4,64,512]{2,1,0:T(8,128)(2,1)} %get-tuple-element.118), channel_id=1, source_target_pairs={{0,10},{1,11},{2,8},{3,9},{4,2},{5,3},{6,0},{7,1},{8,14},{9,15},{1... | collective-permute-start | bytes 786440 | tf_op jit(solution)/shard_map/ppermute | solution.py:313
  47.3 56.8 %copy-start.26 = (bf16[4,64,512]{2,1,0:T(8,128)(2,1)}, bf16[4,64,512]{2,1,0:T(8,128)(2,1)S(1)}, u32[]{:S(2)}) copy-start(bf16[4,64,512]{2,1,0:T(8,128)(2,1)S(1)} %collective-permute-done.2.refs_2_) | copy-start | bytes 786436
  47.3 17.6 %collective-permute-start.7 = (bf16[4,64,512]{2,1,0:T(8,128)(2,1)}, bf16[4,64,512]{2,1,0:T(8,128)(2,1)S(1)}, u32[]{:S(2)}, u32[]{:S(2)}) collective-permute-start(bf16[4,64,512]{2,1,0:T(8,128)(2,1)} %get-tuple-element.119), channel_id=1, source_target_pairs={{0,11},{1,10},{2,9},{3,8},{4,3},{5,2},{6,1},{7,0},{8,15},{9,14},{1... | collective-permute-start | bytes 786440 | tf_op jit(solution)/shard_map/ppermute | solution.py:313
  52.6 51.6 %copy-start.27 = (bf16[4,64,512]{2,1,0:T(8,128)(2,1)}, bf16[4,64,512]{2,1,0:T(8,128)(2,1)S(1)}, u32[]{:S(2)}) copy-start(bf16[4,64,512]{2,1,0:T(8,128)(2,1)S(1)} %collective-permute-done.3.refs_3_) | copy-start | bytes 786436
  53.7 50.4 %copy-start.28 = (bf16[4,64,512]{2,1,0:T(8,128)(2,1)}, bf16[4,64,512]{2,1,0:T(8,128)(2,1)S(1)}, u32[]{:S(2)}) copy-start(bf16[4,64,512]{2,1,0:T(8,128)(2,1)S(1)} %collective-permute-done.4.refs_4_) | copy-start | bytes 786436
  65.0 19.4 %collective-permute-start.8 = (bf16[4,64,512]{2,1,0:T(8,128)(2,1)}, bf16[4,64,512]{2,1,0:T(8,128)(2,1)S(1)}, u32[]{:S(2)}, u32[]{:S(2)}) collective-permute-start(bf16[4,64,512]{2,1,0:T(8,128)(2,1)} %get-tuple-element.120), channel_id=1, source_target_pairs={{0,0},{1,1},{2,2},{3,3},{4,8},{5,9},{6,10},{7,11},{8,4},{9,5},{10,... | collective-permute-start | bytes 786440 | tf_op jit(solution)/shard_map/ppermute | solution.py:313
  78.9 12.2 %collective-permute-start.9 = (bf16[4,64,512]{2,1,0:T(8,128)(2,1)}, bf16[4,64,512]{2,1,0:T(8,128)(2,1)S(1)}, u32[]{:S(2)}, u32[]{:S(2)}) collective-permute-start(bf16[4,64,512]{2,1,0:T(8,128)(2,1)} %get-tuple-element.121), channel_id=1, source_target_pairs={{0,1},{1,0},{2,3},{3,2},{4,9},{5,8},{6,11},{7,10},{8,5},{9,4},{10,... | collective-permute-start | bytes 786440 | tf_op jit(solution)/shard_map/ppermute | solution.py:313
  80.3 18.8 %collective-permute-start.10 = (bf16[4,64,512]{2,1,0:T(8,128)(2,1)}, bf16[4,64,512]{2,1,0:T(8,128)(2,1)S(1)}, u32[]{:S(2)}, u32[]{:S(2)}) collective-permute-start(bf16[4,64,512]{2,1,0:T(8,128)(2,1)} %get-tuple-element.122), channel_id=1, source_target_pairs={{0,2},{1,3},{2,0},{3,1},{4,10},{5,11},{6,8},{7,9},{8,6},{9,7},{10,... | collective-permute-start | bytes 786440 | tf_op jit(solution)/shard_map/ppermute | solution.py:313
  82.9 43.6 %collective-permute-start.11 = (bf16[4,64,512]{2,1,0:T(8,128)(2,1)}, bf16[4,64,512]{2,1,0:T(8,128)(2,1)}, u32[]{:S(2)}, u32[]{:S(2)}) collective-permute-start(bf16[4,64,512]{2,1,0:T(8,128)(2,1)} %get-tuple-element.123), channel_id=1, source_target_pairs={{0,3},{1,2},{2,1},{3,0},{4,11},{5,10},{6,9},{7,8},{8,7},{9,6},{10,... | collective-permute-start | bytes 786440 | tf_op jit(solution)/shard_map/ppermute | solution.py:313
  83.9 42.7 %collective-permute-start.12 = (bf16[4,64,512]{2,1,0:T(8,128)(2,1)}, bf16[4,64,512]{2,1,0:T(8,128)(2,1)}, u32[]{:S(2)}, u32[]{:S(2)}) collective-permute-start(bf16[4,64,512]{2,1,0:T(8,128)(2,1)} %get-tuple-element.124), channel_id=1, source_target_pairs={{0,8},{1,9},{2,10},{3,11},{4,0},{5,1},{6,2},{7,3},{8,12},{9,13},{1... | collective-permute-start | bytes 786440 | tf_op jit(solution)/shard_map/ppermute | solution.py:313
  84.4 42.2 %collective-permute-start.13 = (bf16[4,64,512]{2,1,0:T(8,128)(2,1)}, bf16[4,64,512]{2,1,0:T(8,128)(2,1)}, u32[]{:S(2)}, u32[]{:S(2)}) collective-permute-start(bf16[4,64,512]{2,1,0:T(8,128)(2,1)} %get-tuple-element.125), channel_id=1, source_target_pairs={{0,9},{1,8},{2,11},{3,10},{4,1},{5,0},{6,3},{7,2},{8,13},{9,12},{1... | collective-permute-start | bytes 786440 | tf_op jit(solution)/shard_map/ppermute | solution.py:313
  91.2 35.4 %collective-permute-start.14 = (bf16[4,64,512]{2,1,0:T(8,128)(2,1)}, bf16[4,64,512]{2,1,0:T(8,128)(2,1)}, u32[]{:S(2)}, u32[]{:S(2)}) collective-permute-start(bf16[4,64,512]{2,1,0:T(8,128)(2,1)} %get-tuple-element.126), channel_id=1, source_target_pairs={{0,10},{1,11},{2,8},{3,9},{4,2},{5,3},{6,0},{7,1},{8,14},{9,15},{1... | collective-permute-start | bytes 786440 | tf_op jit(solution)/shard_map/ppermute | solution.py:313
  99.0 27.6 %collective-permute-start.15 = (bf16[4,64,512]{2,1,0:T(8,128)(2,1)}, bf16[4,64,512]{2,1,0:T(8,128)(2,1)}, u32[]{:S(2)}, u32[]{:S(2)}) collective-permute-start(bf16[4,64,512]{2,1,0:T(8,128)(2,1)} %get-tuple-element.127), channel_id=1, source_target_pairs={{0,11},{1,10},{2,9},{3,8},{4,3},{5,2},{6,1},{7,0},{8,15},{9,14},{1... | collective-permute-start | bytes 786440 | tf_op jit(solution)/shard_map/ppermute | solution.py:313
  121.9 24.3 %copy-start.17 = (bf16[4,64,512]{2,1,0:T(8,128)(2,1)S(1)}, bf16[4,64,512]{2,1,0:T(8,128)(2,1)}, u32[]{:S(2)}) copy-start(bf16[4,64,512]{2,1,0:T(8,128)(2,1)} %get-tuple-element.134) | copy-start | bytes 786436
  121.9 26.9 %copy-start.16 = (bf16[4,64,512]{2,1,0:T(8,128)(2,1)S(1)}, bf16[4,64,512]{2,1,0:T(8,128)(2,1)}, u32[]{:S(2)}) copy-start(bf16[4,64,512]{2,1,0:T(8,128)(2,1)} %get-tuple-element.135) | copy-start | bytes 786436
  126.6 14.5 %collective-permute-start.16 = (bf16[4,64,512]{2,1,0:T(8,128)(2,1)S(1)}, bf16[4,64,512]{2,1,0:T(8,128)(2,1)S(1)}, u32[]{:S(2)}, u32[]{:S(2)}) collective-permute-start(bf16[4,64,512]{2,1,0:T(8,128)(2,1)S(1)} %copy-done.23), channel_id=1, source_target_pairs={{0,0},{1,1},{2,2},{3,3},{4,8},{5,9},{6,10},{7,11},{8,4},{9,5},{10,... | collective-permute-start | bytes 786440 | tf_op jit(solution)/shard_map/ppermute | solution.py:313
  133.4 12.9 %collective-permute-start.17 = (bf16[4,64,512]{2,1,0:T(8,128)(2,1)S(1)}, bf16[4,64,512]{2,1,0:T(8,128)(2,1)S(1)}, u32[]{:S(2)}, u32[]{:S(2)}) collective-permute-start(bf16[4,64,512]{2,1,0:T(8,128)(2,1)S(1)} %copy-done.22), channel_id=1, source_target_pairs={{0,1},{1,0},{2,3},{3,2},{4,9},{5,8},{6,11},{7,10},{8,5},{9,4},{10,... | collective-permute-start | bytes 786440 | tf_op jit(solution)/shard_map/ppermute | solution.py:313
  133.5 15.3 %collective-permute-start.18 = (bf16[4,64,512]{2,1,0:T(8,128)(2,1)S(1)}, bf16[4,64,512]{2,1,0:T(8,128)(2,1)S(1)}, u32[]{:S(2)}, u32[]{:S(2)}) collective-permute-start(bf16[4,64,512]{2,1,0:T(8,128)(2,1)S(1)} %copy-done.21), channel_id=1, source_target_pairs={{0,2},{1,3},{2,0},{3,1},{4,10},{5,11},{6,8},{7,9},{8,6},{9,7},{10,... | collective-permute-start | bytes 786440 | tf_op jit(solution)/shard_map/ppermute | solution.py:313
  133.6 34.0 %collective-permute-start.19 = (bf16[4,64,512]{2,1,0:T(8,128)(2,1)S(1)}, bf16[4,64,512]{2,1,0:T(8,128)(2,1)S(1)}, u32[]{:S(2)}, u32[]{:S(2)}) collective-permute-start(bf16[4,64,512]{2,1,0:T(8,128)(2,1)S(1)} %copy-done.20), channel_id=1, source_target_pairs={{0,3},{1,2},{2,1},{3,0},{4,11},{5,10},{6,9},{7,8},{8,7},{9,6},{10,... | collective-permute-start | bytes 786440 | tf_op jit(solution)/shard_map/ppermute | solution.py:313
  137.9 29.8 %collective-permute-start.20 = (bf16[4,64,512]{2,1,0:T(8,128)(2,1)S(1)}, bf16[4,64,512]{2,1,0:T(8,128)(2,1)S(1)}, u32[]{:S(2)}, u32[]{:S(2)}) collective-permute-start(bf16[4,64,512]{2,1,0:T(8,128)(2,1)S(1)} %copy-done.19), channel_id=1, source_target_pairs={{0,8},{1,9},{2,10},{3,11},{4,0},{5,1},{6,2},{7,3},{8,12},{9,13},{1... | collective-permute-start | bytes 786440 | tf_op jit(solution)/shard_map/ppermute | solution.py:313
  141.2 26.5 %copy-start.35 = (bf16[4,64,512]{2,1,0:T(8,128)(2,1)}, bf16[4,64,512]{2,1,0:T(8,128)(2,1)S(1)}, u32[]{:S(2)}) copy-start(bf16[4,64,512]{2,1,0:T(8,128)(2,1)S(1)} %collective-permute-done.16.refs_0_) | copy-start | bytes 786436
  141.2 26.6 %collective-permute-start.21 = (bf16[4,64,512]{2,1,0:T(8,128)(2,1)S(1)}, bf16[4,64,512]{2,1,0:T(8,128)(2,1)S(1)}, u32[]{:S(2)}, u32[]{:S(2)}) collective-permute-start(bf16[4,64,512]{2,1,0:T(8,128)(2,1)S(1)} %copy-done.18), channel_id=1, source_target_pairs={{0,9},{1,8},{2,11},{3,10},{4,1},{5,0},{6,3},{7,2},{8,13},{9,12},{1... | collective-permute-start | bytes 786440 | tf_op jit(solution)/shard_map/ppermute | solution.py:313
  146.2 21.5 %collective-permute-start.22 = (bf16[4,64,512]{2,1,0:T(8,128)(2,1)S(1)}, bf16[4,64,512]{2,1,0:T(8,128)(2,1)S(1)}, u32[]{:S(2)}, u32[]{:S(2)}) collective-permute-start(bf16[4,64,512]{2,1,0:T(8,128)(2,1)S(1)} %copy-done.17), channel_id=1, source_target_pairs={{0,10},{1,11},{2,8},{3,9},{4,2},{5,3},{6,0},{7,1},{8,14},{9,15},{1... | collective-permute-start | bytes 786440 | tf_op jit(solution)/shard_map/ppermute | solution.py:313
  148.8 19.0 %collective-permute-start.23 = (bf16[4,64,512]{2,1,0:T(8,128)(2,1)S(1)}, bf16[4,64,512]{2,1,0:T(8,128)(2,1)S(1)}, u32[]{:S(2)}, u32[]{:S(2)}) collective-permute-start(bf16[4,64,512]{2,1,0:T(8,128)(2,1)S(1)} %copy-done.16), channel_id=1, source_target_pairs={{0,11},{1,10},{2,9},{3,8},{4,3},{5,2},{6,1},{7,0},{8,15},{9,14},{1... | collective-permute-start | bytes 786440 | tf_op jit(solution)/shard_map/ppermute | solution.py:313
  150.1 31.6 %copy-start.14 = (bf16[4,64,512]{2,1,0:T(8,128)(2,1)S(1)}, bf16[4,64,512]{2,1,0:T(8,128)(2,1)}, u32[]{:S(2)}) copy-start(bf16[4,64,512]{2,1,0:T(8,128)(2,1)} %get-tuple-element.145) | copy-start | bytes 786436
  150.1 31.6 %copy-start.13 = (bf16[4,64,512]{2,1,0:T(8,128)(2,1)S(1)}, bf16[4,64,512]{2,1,0:T(8,128)(2,1)}, u32[]{:S(2)}) copy-start(bf16[4,64,512]{2,1,0:T(8,128)(2,1)} %get-tuple-element.146) | copy-start | bytes 786436
  150.1 32.2 %copy-start.12 = (bf16[4,64,512]{2,1,0:T(8,128)(2,1)S(1)}, bf16[4,64,512]{2,1,0:T(8,128)(2,1)}, u32[]{:S(2)}) copy-start(bf16[4,64,512]{2,1,0:T(8,128)(2,1)} %get-tuple-element.147) | copy-start | bytes 786436
  150.2 36.1 %copy-start.11 = (bf16[4,64,512]{2,1,0:T(8,128)(2,1)S(1)}, bf16[4,64,512]{2,1,0:T(8,128)(2,1)}, u32[]{:S(2)}) copy-start(bf16[4,64,512]{2,1,0:T(8,128)(2,1)} %get-tuple-element.148) | copy-start | bytes 786436
  167.7 36.1 %copy-start.38 = (bf16[4,64,512]{2,1,0:T(8,128)(2,1)}, bf16[4,64,512]{2,1,0:T(8,128)(2,1)S(1)}, u32[]{:S(2)}) copy-start(bf16[4,64,512]{2,1,0:T(8,128)(2,1)S(1)} %collective-permute-done.19.refs_3_) | copy-start | bytes 786436
  167.7 36.1 %copy-start.39 = (bf16[4,64,512]{2,1,0:T(8,128)(2,1)}, bf16[4,64,512]{2,1,0:T(8,128)(2,1)S(1)}, u32[]{:S(2)}) copy-start(bf16[4,64,512]{2,1,0:T(8,128)(2,1)S(1)} %collective-permute-done.20.refs_4_) | copy-start | bytes 786436
  167.7 36.1 %copy-start.40 = (bf16[4,64,512]{2,1,0:T(8,128)(2,1)}, bf16[4,64,512]{2,1,0:T(8,128)(2,1)S(1)}, u32[]{:S(2)}) copy-start(bf16[4,64,512]{2,1,0:T(8,128)(2,1)S(1)} %collective-permute-done.21.refs_5_) | copy-start | bytes 786436
  167.8 36.0 %copy-start.42 = (bf16[4,64,512]{2,1,0:T(8,128)(2,1)}, bf16[4,64,512]{2,1,0:T(8,128)(2,1)S(1)}, u32[]{:S(2)}) copy-start(bf16[4,64,512]{2,1,0:T(8,128)(2,1)S(1)} %collective-permute-done.22.refs_6_) | copy-start | bytes 786436
  167.8 36.0 %copy-start.46 = (bf16[4,64,512]{2,1,0:T(8,128)(2,1)}, bf16[4,64,512]{2,1,0:T(8,128)(2,1)S(1)}, u32[]{:S(2)}) copy-start(bf16[4,64,512]{2,1,0:T(8,128)(2,1)S(1)} %collective-permute-done.23.refs_7_) | copy-start | bytes 786436
  167.8 36.0 %copy-start.10 = (bf16[4,64,512]{2,1,0:T(8,128)(2,1)S(1)}, bf16[4,64,512]{2,1,0:T(8,128)(2,1)}, u32[]{:S(2)}) copy-start(bf16[4,64,512]{2,1,0:T(8,128)(2,1)} %get-tuple-element.149) | copy-start | bytes 786436
  167.8 36.3 %copy-start.9 = (bf16[4,64,512]{2,1,0:T(8,128)(2,1)S(1)}, bf16[4,64,512]{2,1,0:T(8,128)(2,1)}, u32[]{:S(2)}) copy-start(bf16[4,64,512]{2,1,0:T(8,128)(2,1)} %get-tuple-element.150) | copy-start | bytes 786436
  167.8 38.5 %copy-start.8 = (bf16[4,64,512]{2,1,0:T(8,128)(2,1)S(1)}, bf16[4,64,512]{2,1,0:T(8,128)(2,1)}, u32[]{:S(2)}) copy-start(bf16[4,64,512]{2,1,0:T(8,128)(2,1)} %get-tuple-element.151) | copy-start | bytes 786436
  167.8 36.0 %collective-permute-start.24 = (bf16[4,64,512]{2,1,0:T(8,128)(2,1)S(1)}, bf16[4,64,512]{2,1,0:T(8,128)(2,1)S(1)}, u32[]{:S(2)}, u32[]{:S(2)}) collective-permute-start(bf16[4,64,512]{2,1,0:T(8,128)(2,1)S(1)} %copy-done.15), channel_id=1, source_target_pairs={{0,0},{1,1},{2,2},{3,3},{4,8},{5,9},{6,10},{7,11},{8,4},{9,5},{10,... | collective-permute-start | bytes 786440 | tf_op jit(solution)/shard_map/ppermute | solution.py:313
  181.7 22.4 %collective-permute-start.25 = (bf16[4,64,512]{2,1,0:T(8,128)(2,1)S(1)}, bf16[4,64,512]{2,1,0:T(8,128)(2,1)S(1)}, u32[]{:S(2)}, u32[]{:S(2)}) collective-permute-start(bf16[4,64,512]{2,1,0:T(8,128)(2,1)S(1)} %copy-done.14), channel_id=1, source_target_pairs={{0,1},{1,0},{2,3},{3,2},{4,9},{5,8},{6,11},{7,10},{8,5},{9,4},{10,... | collective-permute-start | bytes 786440 | tf_op jit(solution)/shard_map/ppermute | solution.py:313
  181.8 24.5 %collective-permute-start.26 = (bf16[4,64,512]{2,1,0:T(8,128)(2,1)S(1)}, bf16[4,64,512]{2,1,0:T(8,128)(2,1)S(1)}, u32[]{:S(2)}, u32[]{:S(2)}) collective-permute-start(bf16[4,64,512]{2,1,0:T(8,128)(2,1)S(1)} %copy-done.13), channel_id=1, source_target_pairs={{0,2},{1,3},{2,0},{3,1},{4,10},{5,11},{6,8},{7,9},{8,6},{9,7},{10,... | collective-permute-start | bytes 786440 | tf_op jit(solution)/shard_map/ppermute | solution.py:313
  182.3 44.3 %collective-permute-start.27 = (bf16[4,64,512]{2,1,0:T(8,128)(2,1)S(1)}, bf16[4,64,512]{2,1,0:T(8,128)(2,1)S(1)}, u32[]{:S(2)}, u32[]{:S(2)}) collective-permute-start(bf16[4,64,512]{2,1,0:T(8,128)(2,1)S(1)} %copy-done.12), channel_id=1, source_target_pairs={{0,3},{1,2},{2,1},{3,0},{4,11},{5,10},{6,9},{7,8},{8,7},{9,6},{10,... | collective-permute-start | bytes 786440 | tf_op jit(solution)/shard_map/ppermute | solution.py:313
  186.2 40.4 %collective-permute-start.28 = (bf16[4,64,512]{2,1,0:T(8,128)(2,1)S(1)}, bf16[4,64,512]{2,1,0:T(8,128)(2,1)S(1)}, u32[]{:S(2)}, u32[]{:S(2)}) collective-permute-start(bf16[4,64,512]{2,1,0:T(8,128)(2,1)S(1)} %copy-done.11), channel_id=1, source_target_pairs={{0,8},{1,9},{2,10},{3,11},{4,0},{5,1},{6,2},{7,3},{8,12},{9,13},{1... | collective-permute-start | bytes 786440 | tf_op jit(solution)/shard_map/ppermute | solution.py:313
  203.8 22.7 %copy-start.41 = (bf16[4,64,512]{2,1,0:T(8,128)(2,1)}, bf16[4,64,512]{2,1,0:T(8,128)(2,1)S(1)}, u32[]{:S(2)}) copy-start(bf16[4,64,512]{2,1,0:T(8,128)(2,1)S(1)} %collective-permute-done.24.refs_0_) | copy-start | bytes 786436
  203.8 22.8 %collective-permute-start.29 = (bf16[4,64,512]{2,1,0:T(8,128)(2,1)S(1)}, bf16[4,64,512]{2,1,0:T(8,128)(2,1)S(1)}, u32[]{:S(2)}, u32[]{:S(2)}) collective-permute-start(bf16[4,64,512]{2,1,0:T(8,128)(2,1)S(1)} %copy-done.10), channel_id=1, source_target_pairs={{0,9},{1,8},{2,11},{3,10},{4,1},{5,0},{6,3},{7,2},{8,13},{9,12},{1... | collective-permute-start | bytes 786440 | tf_op jit(solution)/shard_map/ppermute | solution.py:313
  204.1 22.5 %collective-permute-start.30 = (bf16[4,64,512]{2,1,0:T(8,128)(2,1)S(1)}, bf16[4,64,512]{2,1,0:T(8,128)(2,1)S(1)}, u32[]{:S(2)}, u32[]{:S(2)}) collective-permute-start(bf16[4,64,512]{2,1,0:T(8,128)(2,1)S(1)} %copy-done.9), channel_id=1, source_target_pairs={{0,10},{1,11},{2,8},{3,9},{4,2},{5,3},{6,0},{7,1},{8,14},{9,15},{1... | collective-permute-start | bytes 786440 | tf_op jit(solution)/shard_map/ppermute | solution.py:313
  206.3 20.4 %collective-permute-start.31 = (bf16[4,64,512]{2,1,0:T(8,128)(2,1)S(1)}, bf16[4,64,512]{2,1,0:T(8,128)(2,1)S(1)}, u32[]{:S(2)}, u32[]{:S(2)}) collective-permute-start(bf16[4,64,512]{2,1,0:T(8,128)(2,1)S(1)} %copy-done.8), channel_id=1, source_target_pairs={{0,11},{1,10},{2,9},{3,8},{4,3},{5,2},{6,1},{7,0},{8,15},{9,14},{1... | collective-permute-start | bytes 786440 | tf_op jit(solution)/shard_map/ppermute | solution.py:313
  227.7 210.3 %all-to-all-start = ((bf16[8,36,64,512]{3,2,1,0:T(8,128)(2,1)}), bf16[8,36,64,512]{3,2,1,0:T(8,128)(2,1)}, u32[]{:S(2)}, u32[]{:S(2)}) async-start(bf16[8,36,64,512]{3,2,1,0:T(8,128)(2,1)} %bitcast.34), calls=%async_computation | async-start | bytes 37748736 | tf_op jit(solution)/shard_map/all_to_all | solution.py:256
  243.1 194.9 %collective-permute-start.32 = (bf16[64,512,128]{2,1,0:T(8,128)(2,1)}, bf16[64,512,128]{2,1,0:T(8,128)(2,1)}, u32[]{:S(2)}, u32[]{:S(2)}) collective-permute-start(bf16[64,512,128]{2,1,0:T(8,128)(2,1)} %bitcast_convert_fusion), channel_id=1, source_target_pairs={{0,16},{1,17},{2,18},{3,19},{4,20},{5,21},{6,22},{7,23},{8,24},{9,... | collective-permute-start | bytes 25165832 | tf_op jit(solution)/shard_map/ppermute | solution.py:333
  438.0 23.3 %all-to-all-start.1 = ((bf16[8,12,16,512]{3,2,1,0:T(8,128)(2,1)}), bf16[8,12,16,512]{3,2,1,0:T(8,128)(2,1)S(1)}, u32[]{:S(2)}, u32[]{:S(2)}) async-start(bf16[8,12,16,512]{3,2,1,0:T(8,128)(2,1)} %bitcast.39), calls=%async_computation.1 | async-start | bytes 3145728 | tf_op jit(solution)/shard_map/all_to_all | solution.py:256
  471.3 41.4 %all-to-all-start.2 = ((bf16[8,12,16,512]{3,2,1,0:T(8,128)(2,1)}), bf16[8,12,16,512]{3,2,1,0:T(8,128)(2,1)S(1)}, u32[]{:S(2)}, u32[]{:S(2)}) async-start(bf16[8,12,16,512]{3,2,1,0:T(8,128)(2,1)} %bitcast.15), calls=%async_computation.2 | async-start | bytes 3145728 | tf_op jit(solution)/shard_map/all_to_all | solution.py:256
  475.3 50.2 %collective-permute-start.33 = (bf16[16,512,128]{2,1,0:T(8,128)(2,1)}, bf16[16,512,128]{2,1,0:T(8,128)(2,1)}, u32[]{:S(2)}, u32[]{:S(2)}) collective-permute-start(bf16[16,512,128]{2,1,0:T(8,128)(2,1)} %finished.4), channel_id=1, source_target_pairs={{0,16},{1,17},{2,18},{3,19},{8,20},{9,21},{10,22},{11,23},{4,24},{... | collective-permute-start | bytes 6291464 | tf_op jit(solution)/shard_map/ppermute | solution.py:346
  525.4 41.1 %all-to-all-start.3 = ((bf16[8,12,16,512]{3,2,1,0:T(8,128)(2,1)}), bf16[8,12,16,512]{3,2,1,0:T(8,128)(2,1)S(1)}, u32[]{:S(2)}, u32[]{:S(2)}) async-start(bf16[8,12,16,512]{3,2,1,0:T(8,128)(2,1)} %bitcast.14), calls=%async_computation.3 | async-start | bytes 3145728 | tf_op jit(solution)/shard_map/all_to_all | solution.py:256
  529.0 50.6 %collective-permute-start.34 = (bf16[16,512,128]{2,1,0:T(8,128)(2,1)}, bf16[16,512,128]{2,1,0:T(8,128)(2,1)}, u32[]{:S(2)}, u32[]{:S(2)}) collective-permute-start(bf16[16,512,128]{2,1,0:T(8,128)(2,1)} %finished.5), channel_id=1, source_target_pairs={{0,16},{1,17},{2,18},{3,19},{8,20},{9,21},{10,22},{11,23},{4,24},{... | collective-permute-start | bytes 6291464 | tf_op jit(solution)/shard_map/ppermute | solution.py:346
  579.6 41.4 %all-to-all-start.4 = ((bf16[8,12,16,512]{3,2,1,0:T(8,128)(2,1)}), bf16[8,12,16,512]{3,2,1,0:T(8,128)(2,1)S(1)}, u32[]{:S(2)}, u32[]{:S(2)}) async-start(bf16[8,12,16,512]{3,2,1,0:T(8,128)(2,1)} %bitcast.13), calls=%async_computation.4 | async-start | bytes 3145728 | tf_op jit(solution)/shard_map/all_to_all | solution.py:256
  583.5 50.8 %collective-permute-start.35 = (bf16[16,512,128]{2,1,0:T(8,128)(2,1)}, bf16[16,512,128]{2,1,0:T(8,128)(2,1)}, u32[]{:S(2)}, u32[]{:S(2)}) collective-permute-start(bf16[16,512,128]{2,1,0:T(8,128)(2,1)} %finished.6), channel_id=1, source_target_pairs={{0,16},{1,17},{2,18},{3,19},{8,20},{9,21},{10,22},{11,23},{4,24},{... | collective-permute-start | bytes 6291464 | tf_op jit(solution)/shard_map/ppermute | solution.py:346
  634.3 49.9 %collective-permute-start.36 = (bf16[16,512,128]{2,1,0:T(8,128)(2,1)}, bf16[16,512,128]{2,1,0:T(8,128)(2,1)S(1)}, u32[]{:S(2)}, u32[]{:S(2)}) collective-permute-start(bf16[16,512,128]{2,1,0:T(8,128)(2,1)} %finished.7), channel_id=1, source_target_pairs={{0,16},{1,17},{2,18},{3,19},{8,20},{9,21},{10,22},{11,23},{4,24},{... | collective-permute-start | bytes 6291464 | tf_op jit(solution)/shard_map/ppermute | solution.py:346
  (30 other events, 260.5 us)
Sparse Core Ops, SparseCore 0:
  8.9 84.7 all-gather.2

commit v5 on v4

--- a/solution.py
+++ b/solution.py
@@ -6,7 +6,7 @@
 from jax.sharding import Mesh, PartitionSpec as P
 
 TICKS = 2
-ENDS = (4, 8, 12, 16)
+ENDS = (6, 12, 16)
 ROW_TILE = 16
 PIECE = 512
 AXES = ("lane", "core", "half", "rest")
@@ -274,6 +274,7 @@
         return at(section // 2 * 2 + member // rest, section % 2 * rest + member % rest)
 
     spread_routes = [[(at(p, b), hosts(p, b ^ k)) for p, b in places] for k in range(bands)]
+    pack_routes = [[(at((p + tick) % sections, b), hosts(p, b)) for p, b in places] for tick in range(TICKS)]
     shift_route = [(at(p, b), at((p + TICKS) % sections, b)) for p, b in places]
     return_route = [(hosts(p, b), at((p + TICKS) % sections, b)) for p, b in places]
 
@@ -287,7 +288,8 @@
         pipe = ("lane", "core")
         own = lax.axis_index("lane") * 2 + lax.axis_index("half")
         all_blocks = lax.all_gather(shear_blocks[0], pipe)
-        packs = lax.all_gather(packed(source, mix_weight[0]), pipe)
+        pack = packed(source, mix_weight[0])
+        packs = [lax.ppermute(pack, AXES, route) for route in pack_routes]
 
         members, (_, height, width, channels) = bands, memory.shape
         row_chunks = height // ROW_TILE
@@ -296,7 +298,7 @@
         weights, mixes = [], []
         for tick in range(TICKS):
             which = ((own + tick) % sections).astype(jnp.int32)[None]
-            tail = lax.dynamic_index_in_dim(packs, which[0], keepdims=False)
+            tail = packs[tick]
             table = tail[mix_rows:].reshape(-1)[: source.size].astype(jnp.int32)
             weights.append([dense(all_blocks, table, which, k, k != 1) for k in range(3)])
             mixes.append(tail[:mix_rows])
@@ -321,12 +323,10 @@
         def room(each, rows):
             return jax.ShapeDtypeStruct((members, 3, each, rows, width), jnp.bfloat16)
 
-        full = [delivered(0, packs)]
+        full = [delivered(0, *packs)]
         solved = [room(starts[last], height)]
         for k in range(last):
-            waits = [*weights[0], *weights[1]] if k == 1 else earlier if k > 1 else []
-            full.append(delivered(k + 1, *full[k], *waits))
-            earlier = solved
+            full.append(delivered(k + 1, *full[k], *(solved if k else [])))
             solved = relayed(full[k], member, *weights, solved, starts[k])
         ends = relayed(full[last], member, *weights, [room(sizes[last], ROW_TILE)] * row_chunks, 0)
         (solved,) = later(solved, *full[last])

time: 707 us -> 701 us (level)
  waiting for transfers between devices: 395 us -> 405 us
    ppermute x32 -> x24, starting transfers between devices: 67.8 us -> 55.9 us  [delivered(): lax.ppermute(piece, AXES, route)]
    ppermute x4, waiting for transfers between devices: 44.6 us -> 52.3 us  [on_device(): lax.ppermute(tied(rows, moved[-1]) if ending else rows, AXES, return_route)]
    all_to_all x5, starting transfers between devices: 21.1 us -> 28.3 us  [exchanged(): lax.all_to_all(values, GROUP, split_axis=0, concat_axis=0, tiled=True)]
    pallas_call x4 -> x3, Pallas kernels: 69.7 us -> 63 us  [relayed(): pl.pallas_call(body, grid_spec=pltpu.PrefetchScalarGridSpec(num_scalar_pr...]
    ppermute x32 -> x24, waiting for transfers between devices: 53 us -> 56.7 us  [delivered(): lax.ppermute(piece, AXES, route)]
  transfers between devices with their start and end apart: 43 -> 37, of which waited for: 22 -> 20; matrix products, arithmetic and copies ran while one was open for 2% -> 2% of each run, Pallas kernels for 21% -> 21%
where the time goes in v5:
time: 701 us; the launch traced here: 692 us
  waiting for transfers between devices  405 us (58%)
  Pallas kernels  156 us (22%)
  starting transfers between devices  96.8 us (14%)
  between operations  14.3 us (2%)
  other arithmetic  10.4 us (1%)
  local copies, waits for them, and re-layouts  9.09 us (1%)
    all_to_all x5, waiting for transfers between devices, exchanged(): lax.all_to_all(values, GROUP, split_axis=0, concat_axis=0, tiled=True)  295 us
    pallas_call x3, Pallas kernels, relayed(): pl.pallas_call(body, grid_spec=pltpu.PrefetchScalarGridSpec(num_scalar_pr...  63 us
    ppermute x24, waiting for transfers between devices, delivered(): lax.ppermute(piece, AXES, route)  56.7 us
    ppermute x24, starting transfers between devices, delivered(): lax.ppermute(piece, AXES, route)  55.9 us
    ppermute x4, waiting for transfers between devices, on_device(): lax.ppermute(tied(rows, moved[-1]) if ending else rows, AXES, return_route)  52.3 us
    pallas_call x4, Pallas kernels, finished(): pl.pallas_call(body, grid=(width // piece,), in_specs=[term_block(a, row_...  35.4 us
    all_to_all x5, starting transfers between devices, exchanged(): lax.all_to_all(values, GROUP, split_axis=0, concat_axis=0, tiled=True)  28.3 us
    pallas_call x6, Pallas kernels, dense(): pl.pallas_call(body, grid_spec=pltpu.PrefetchScalarGridSpec(num_scalar_pr...  26.9 us
  transfers between devices with their start and end apart: 37, of which 20 were waited for; matrix products, arithmetic and copies ran while one was open for 2% of the time, Pallas kernels for 21%

profile of v5, /device:TPU:1, one launch (start us, length us, event | category | flops | bytes accessed | tf_op | source)
XLA Modules:
  0.0 691.8 jit_solution(13930466174916890239)
XLA Ops:
  7.7 5.6 collective-permute-start
  13.4 12.2 %spread.1 = (bf16[6,64,512]{2,1,0:T(8,128)(2,1)}, bf16[6,64,512]{2,1,0:T(8,128)(2,1)}, bf16[6,64,512]{2,1,0:T(8,128)(2,1)}, bf16[6,64,512]{2,1,0:T(8,128)(2,1)},...) custom-call(s32[1]{0:T(128)} %bitcast.1.band_ref, ...), custom_call_target="tpu_custom_call" | custom-call | bytes 33554432 | tf_op jit(solution)/shard_map/spread/pallas_call | solution.py:53
  25.7 1.9 collective-permute-start.2
  27.6 3.6 collective-permute-start.3
  32.2 2.6 collective-permute-start.5
  34.7 5.0 collective-permute-done.2.refs_0_
  39.7 8.7 %collective-permute-done.3.refs_1_ = bf16[6,64,512]{2,1,0:T(8,128)(2,1)S(1)} collective-permute-done((bf16[6,64,512]{2,1,0:T(8,128)(2,1)}, bf16[6,64,512]{2,1,0:T(8,128)(2,1)S(1)}, u32[]{:S(2)}, u32[]{:S(2)}) %collective-permute-start.3) | collective-permute-done | bytes 393248 | tf_op jit(solution)/shard_map/ppermute | solution.py:315
  48.4 8.6 %collective-permute-done.4.refs_2_ = bf16[6,64,512]{2,1,0:T(8,128)(2,1)S(1)} collective-permute-done((bf16[6,64,512]{2,1,0:T(8,128)(2,1)}, bf16[6,64,512]{2,1,0:T(8,128)(2,1)S(1)}, u32[]{:S(2)}, u32[]{:S(2)}) %collective-permute-start.4) | collective-permute-done | bytes 393248 | tf_op jit(solution)/shard_map/ppermute | solution.py:315
  57.0 5.8 collective-permute-done.5.refs_3_
  62.8 7.0 %collective-permute-done.7.refs_5_ = bf16[6,64,512]{2,1,0:T(8,128)(2,1)S(1)} collective-permute-done((bf16[6,64,512]{2,1,0:T(8,128)(2,1)}, bf16[6,64,512]{2,1,0:T(8,128)(2,1)S(1)}, u32[]{:S(2)}, u32[]{:S(2)}) %collective-permute-start.7) | collective-permute-done | bytes 393248 | tf_op jit(solution)/shard_map/ppermute | solution.py:315
  69.8 5.0 collective-permute-done.8.refs_6_
  74.8 4.2 collective-permute-done.9.refs_7_
  79.0 25.0 %collective-permute-start.10 = (bf16[6,64,512]{2,1,0:T(8,128)(2,1)}, bf16[6,64,512]{2,1,0:T(8,128)(2,1)S(1)}, u32[]{:S(2)}, u32[]{:S(2)}) collective-permute-start(bf16[6,64,512]{2,1,0:T(8,128)(2,1)} %get-tuple-element.96), channel_id=1, source_target_pairs={{0,0},{1,1},{2,2},{3,3},{4,8},{5,9},{6,10},{7,11},{8,4},{9,5},{10,... | collective-permute-start | bytes 1179656 | tf_op jit(solution)/shard_map/ppermute | solution.py:315
  106.1 3.6 collective-permute-start.13
  109.8 4.5 dense.6.refs_8_
  114.3 4.5 dense.7.refs_9_
  118.7 4.5 dense.8.refs_10_
  123.2 4.5 dense.9.refs_11_
  127.7 4.4 dense.10.refs_12_
  132.1 4.6 dense.11.refs_13_
  136.7 1.8 collective-permute-start.15
  138.5 1.4 collective-permute-start.16
  140.0 2.0 collective-permute-start.17
  142.0 22.8 %relayed.3.refs_14_ = bf16[8,3,12,64,512]{4,3,2,1,0:T(8,128)(2,1)} custom-call(s32[1]{0:T(128)} %bitcast.member_ref, bf16[6,64,512]{2,1,0:T(8,128)(2,1)} %copy-done.11, bf16[6,64,512]{2,1,0:T(8,128)(2,1)} %copy-done.12, bf16[6,64,512]{2,1,0:T(8,128)(2,1)} %copy-done.13, bf16[6,64,512]{2,1,0:T(8,128)(2,1)} %copy-done.19, bf16[6,64,512]{2,1,0:T(8,128)(2,1)} %copy-done.20, ...), custom_call_target="tpu_custom_call" | custom-call | flops 28991029248 | bytes 25165824 | tf_op jit(solution)/shard_map/relayed/pallas_call | solution.py:170
  164.9 2.0 collective-permute-done.17.refs_7_
  166.9 7.2 %collective-permute-start.18 = (bf16[4,64,512]{2,1,0:T(8,128)(2,1)}, bf16[4,64,512]{2,1,0:T(8,128)(2,1)S(1)}, u32[]{:S(2)}, u32[]{:S(2)}) collective-permute-start(bf16[4,64,512]{2,1,0:T(8,128)(2,1)} %get-tuple-element.112), channel_id=1, source_target_pairs={{0,0},{1,1},{2,2},{3,3},{4,8},{5,9},{6,10},{7,11},{8,4},{9,5},{10,... | collective-permute-start | bytes 786440 | tf_op jit(solution)/shard_map/ppermute | solution.py:315
  175.0 3.7 collective-permute-start.21
  178.7 2.7 collective-permute-done.18.refs_0_
  181.4 6.4 collective-permute-done.19.refs_1_
  187.8 1.4 collective-permute-done.20.refs_2_
  189.4 22.7 %relayed.4 = bf16[8,3,12,64,512]{4,3,2,1,0:T(8,128)(2,1)} custom-call(s32[1]{0:T(128)} %bitcast.member_ref, bf16[6,64,512]{2,1,0:T(8,128)(2,1)} %copy-done.14, bf16[6,64,512]{2,1,0:T(8,128)(2,1)} %copy-done.15, bf16[6,64,512]{2,1,0:T(8,128)(2,1)} %copy-done.16, bf16[6,64,512]{2,1,0:T(8,128)(2,1)} %copy-done.17, ...), custom_call_target="tpu_custom_call", output_to_operand_aliasing={{}: (15, {})} | custom-call | flops 28991029248 | bytes 25165824 | tf_op jit(solution)/shard_map/relayed/pallas_call | solution.py:170
  213.7 13.3 %all-to-all-start = ((bf16[8,36,64,512]{3,2,1,0:T(8,128)(2,1)}), bf16[8,36,64,512]{3,2,1,0:T(8,128)(2,1)}, u32[]{:S(2)}, u32[]{:S(2)}) async-start(bf16[8,36,64,512]{3,2,1,0:T(8,128)(2,1)} %bitcast.29), calls=%async_computation | async-start | bytes 37748736 | tf_op jit(solution)/shard_map/all_to_all | solution.py:256
  227.0 9.2 %bitcast_convert_fusion = bf16[64,512,128]{2,1,0:T(8,128)(2,1)} fusion(f32[1,64,512,128]{3,2,1,0:T(8,128)} %param.5), kind=kLoop, calls=%fused_computation.14 | loop fusion | flops 4194304 | bytes 25165824 | tf_op jit(solution)/shard_map/convert_element_type | solution.py:333
  236.2 1.4 collective-permute-start.26
  237.5 17.5 %relayed.5 = (bf16[8,3,4,16,512]{4,3,2,1,0:T(8,128)(2,1)}, bf16[8,3,4,16,512]{4,3,2,1,0:T(8,128)(2,1)}, bf16[8,3,4,16,512]{4,3,2,1,0:T(8,128)(2,1)}, bf16[8,3,4,16,512]{4,3,2,1,0:T(8,128)(2,1)}) custom-call(s32[1]{0:T(128)} %bitcast.member_ref, bf16[4,64,512]{2,1,0:T(8,128)(2,1)} %copy-done.33, bf16[4,64,512]{2,1,0:T(8,128)(2,1)} %copy-done.34, ...), custom_call_target="tpu_custom_call" | custom-call | flops 19327352832 | bytes 20971520 | tf_op jit(solution)/shard_map/relayed/pallas_call | solution.py:170
  255.0 177.8 %all-to-all-done = bf16[8,36,64,512]{3,2,1,0:T(8,128)(2,1)} async-done(((bf16[8,36,64,512]{3,2,1,0:T(8,128)(2,1)}), bf16[8,36,64,512]{3,2,1,0:T(8,128)(2,1)}, u32[]{:S(2)}, u32[]{:S(2)}) %all-to-all-start) | async-done | bytes 18874400 | tf_op jit(solution)/shard_map/all_to_all | solution.py:256
  432.8 4.0 all-to-all-start.1
  438.0 19.0 %all-to-all-done.1 = bf16[8,12,16,512]{3,2,1,0:T(8,128)(2,1)S(1)} async-done(((bf16[8,12,16,512]{3,2,1,0:T(8,128)(2,1)}), bf16[8,12,16,512]{3,2,1,0:T(8,128)(2,1)S(1)}, u32[]{:S(2)}, u32[]{:S(2)}) %all-to-all-start.1) | async-done | bytes 1572896 | tf_op jit(solution)/shard_map/all_to_all | solution.py:256
  457.0 1.1 copy-done.1
  458.2 8.8 %finished.4 = bf16[16,512,128]{2,1,0:T(8,128)(2,1)} custom-call(bf16[8,3,12,64,512]{4,3,2,1,0:T(8,128)(2,1)} %bitcast.11.refs_0_, bf16[8,3,4,16,512]{4,3,2,1,0:T(8,128)(2,1)} %bitcast.31, bf16[128,128]{1,0:T(8,128)(2,1)} %slice.28.refs_2_, bf16[128,128]{1,0:T(8,128)(2,1)} %slice.29.refs_3_), custom_call_target="tpu_custom_call" | custom-call | bytes 4718592 | tf_op jit(solution)/shard_map/finished/pallas_call | solution.py:219
  467.0 3.7 all-to-all-start.2
  470.7 1.3 collective-permute-start.27
  472.0 33.0 %all-to-all-done.2 = bf16[8,12,16,512]{3,2,1,0:T(8,128)(2,1)S(1)} async-done(((bf16[8,12,16,512]{3,2,1,0:T(8,128)(2,1)}), bf16[8,12,16,512]{3,2,1,0:T(8,128)(2,1)S(1)}, u32[]{:S(2)}, u32[]{:S(2)}) %all-to-all-start.2) | async-done | bytes 1572896 | tf_op jit(solution)/shard_map/all_to_all | solution.py:256
  505.0 1.2 copy-done.2
  506.2 8.9 %finished.5 = bf16[16,512,128]{2,1,0:T(8,128)(2,1)} custom-call(bf16[8,3,12,64,512]{4,3,2,1,0:T(8,128)(2,1)} %bitcast.11.refs_0_, bf16[8,3,4,16,512]{4,3,2,1,0:T(8,128)(2,1)} %bitcast.32, bf16[128,128]{1,0:T(8,128)(2,1)} %slice.28.refs_2_, bf16[128,128]{1,0:T(8,128)(2,1)} %slice.29.refs_3_), custom_call_target="tpu_custom_call" | custom-call | bytes 4718592 | tf_op jit(solution)/shard_map/finished/pallas_call | solution.py:219
  515.1 5.7 collective-permute-done.27.source
  520.8 3.5 all-to-all-start.3
  524.4 1.8 collective-permute-start.28
  526.2 32.6 %all-to-all-done.3 = bf16[8,12,16,512]{3,2,1,0:T(8,128)(2,1)S(1)} async-done(((bf16[8,12,16,512]{3,2,1,0:T(8,128)(2,1)}), bf16[8,12,16,512]{3,2,1,0:T(8,128)(2,1)S(1)}, u32[]{:S(2)}, u32[]{:S(2)}) %all-to-all-start.3) | async-done | bytes 1572896 | tf_op jit(solution)/shard_map/all_to_all | solution.py:256
  558.8 1.1 copy-done.3
  559.9 8.8 %finished.6 = bf16[16,512,128]{2,1,0:T(8,128)(2,1)} custom-call(bf16[8,3,12,64,512]{4,3,2,1,0:T(8,128)(2,1)} %bitcast.11.refs_0_, bf16[8,3,4,16,512]{4,3,2,1,0:T(8,128)(2,1)} %bitcast.33, bf16[128,128]{1,0:T(8,128)(2,1)} %slice.28.refs_2_, bf16[128,128]{1,0:T(8,128)(2,1)} %slice.29.refs_3_), custom_call_target="tpu_custom_call" | custom-call | bytes 4718592 | tf_op jit(solution)/shard_map/finished/pallas_call | solution.py:219
  568.7 5.8 collective-permute-done.28.source
  574.5 3.8 all-to-all-start.4
  578.3 2.5 collective-permute-start.29
  580.8 32.5 %all-to-all-done.4 = bf16[8,12,16,512]{3,2,1,0:T(8,128)(2,1)S(1)} async-done(((bf16[8,12,16,512]{3,2,1,0:T(8,128)(2,1)}), bf16[8,12,16,512]{3,2,1,0:T(8,128)(2,1)S(1)}, u32[]{:S(2)}, u32[]{:S(2)}) %all-to-all-start.4) | async-done | bytes 1572896 | tf_op jit(solution)/shard_map/all_to_all | solution.py:256
  613.3 1.2 copy-done
  614.5 8.8 %finished.7 = bf16[16,512,128]{2,1,0:T(8,128)(2,1)} custom-call(bf16[8,3,12,64,512]{4,3,2,1,0:T(8,128)(2,1)} %bitcast.11.refs_0_, bf16[8,3,4,16,512]{4,3,2,1,0:T(8,128)(2,1)} %bitcast.30, bf16[128,128]{1,0:T(8,128)(2,1)} %slice.28.refs_2_, bf16[128,128]{1,0:T(8,128)(2,1)} %slice.29.refs_3_), custom_call_target="tpu_custom_call" | custom-call | bytes 4718592 | tf_op jit(solution)/shard_map/finished/pallas_call | solution.py:219
  623.4 5.2 collective-permute-done.29.source
  628.6 4.8 placed.4.refs_0_
  633.3 4.8 placed.5.refs_0_
  638.1 4.8 placed.6.refs_0_
  642.8 35.7 %collective-permute-done.30.source = bf16[16,512,128]{2,1,0:T(8,128)(2,1)S(1)} collective-permute-done((bf16[16,512,128]{2,1,0:T(8,128)(2,1)}, bf16[16,512,128]{2,1,0:T(8,128)(2,1)S(1)}, u32[]{:S(2)}, u32[]{:S(2)}) %collective-permute-start.30) | collective-permute-done | bytes 2097184 | tf_op jit(solution)/shard_map/ppermute | solution.py:346
  678.5 1.3 copy-done.4
  679.8 4.8 placed.7
  (126 shorter events, 8.2 us)
Async XLA Ops:
  6.5 103.2 %all-gather.2.cloned.1.call-start = ((), (), s32[]{:S(2)}) async-start(), calls=%async_computation.5 | async-start | bytes 15728640 | tf_op jit(solution)/shard_map/all_gather | solution.py:290
  7.7 17.9 %collective-permute-start = (bf16[144,128]{1,0:T(8,128)(2,1)S(1)}, bf16[144,128]{1,0:T(8,128)(2,1)S(1)}, u32[]{:S(2)}, u32[]{:S(2)}) collective-permute-start(bf16[144,128]{1,0:T(8,128)(2,1)S(1)} %pad_maximum_fusion), channel_id=1, source_target_pairs={{0,0},{1,1},{2,2},{3,3},{4,8},{5,9},{6,10},{7,11},{8,4},{9,5},{10,... | collective-permute-start | bytes 110600 | tf_op jit(solution)/shard_map/ppermute | solution.py:292
  13.4 12.3 %collective-permute-start.1 = (bf16[144,128]{1,0:T(8,128)(2,1)S(1)}, bf16[144,128]{1,0:T(8,128)(2,1)S(1)}, u32[]{:S(2)}, u32[]{:S(2)}) collective-permute-start(bf16[144,128]{1,0:T(8,128)(2,1)S(1)} %pad_maximum_fusion), channel_id=1, source_target_pairs={{8,0},{9,1},{10,2},{11,3},{12,8},{13,9},{14,10},{15,11},{16,4},{17... | collective-permute-start | bytes 110600 | tf_op jit(solution)/shard_map/ppermute | solution.py:292
  25.7 14.0 %collective-permute-start.2 = (bf16[6,64,512]{2,1,0:T(8,128)(2,1)}, bf16[6,64,512]{2,1,0:T(8,128)(2,1)S(1)}, u32[]{:S(2)}, u32[]{:S(2)}) collective-permute-start(bf16[6,64,512]{2,1,0:T(8,128)(2,1)} %get-tuple-element.88), channel_id=1, source_target_pairs={{0,0},{1,1},{2,2},{3,3},{4,8},{5,9},{6,10},{7,11},{8,4},{9,5},{10,... | collective-permute-start | bytes 1179656 | tf_op jit(solution)/shard_map/ppermute | solution.py:315
  27.6 20.8 %collective-permute-start.3 = (bf16[6,64,512]{2,1,0:T(8,128)(2,1)}, bf16[6,64,512]{2,1,0:T(8,128)(2,1)S(1)}, u32[]{:S(2)}, u32[]{:S(2)}) collective-permute-start(bf16[6,64,512]{2,1,0:T(8,128)(2,1)} %get-tuple-element.89), channel_id=1, source_target_pairs={{0,1},{1,0},{2,3},{3,2},{4,9},{5,8},{6,11},{7,10},{8,5},{9,4},{10,... | collective-permute-start | bytes 1179656 | tf_op jit(solution)/shard_map/ppermute | solution.py:315
  31.2 25.8 %collective-permute-start.4 = (bf16[6,64,512]{2,1,0:T(8,128)(2,1)}, bf16[6,64,512]{2,1,0:T(8,128)(2,1)S(1)}, u32[]{:S(2)}, u32[]{:S(2)}) collective-permute-start(bf16[6,64,512]{2,1,0:T(8,128)(2,1)} %get-tuple-element.90), channel_id=1, source_target_pairs={{0,2},{1,3},{2,0},{3,1},{4,10},{5,11},{6,8},{7,9},{8,6},{9,7},{10,... | collective-permute-start | bytes 1179656 | tf_op jit(solution)/shard_map/ppermute | solution.py:315
  32.2 30.6 %collective-permute-start.5 = (bf16[6,64,512]{2,1,0:T(8,128)(2,1)}, bf16[6,64,512]{2,1,0:T(8,128)(2,1)S(1)}, u32[]{:S(2)}, u32[]{:S(2)}) collective-permute-start(bf16[6,64,512]{2,1,0:T(8,128)(2,1)} %get-tuple-element.91), channel_id=1, source_target_pairs={{0,3},{1,2},{2,1},{3,0},{4,11},{5,10},{6,9},{7,8},{8,7},{9,6},{10,... | collective-permute-start | bytes 1179656 | tf_op jit(solution)/shard_map/ppermute | solution.py:315
  34.7 28.1 %collective-permute-start.6 = (bf16[6,64,512]{2,1,0:T(8,128)(2,1)}, bf16[6,64,512]{2,1,0:T(8,128)(2,1)S(1)}, u32[]{:S(2)}, u32[]{:S(2)}) collective-permute-start(bf16[6,64,512]{2,1,0:T(8,128)(2,1)} %get-tuple-element.92), channel_id=1, source_target_pairs={{0,8},{1,9},{2,10},{3,11},{4,0},{5,1},{6,2},{7,3},{8,12},{9,13},{1... | collective-permute-start | bytes 1179656 | tf_op jit(solution)/shard_map/ppermute | solution.py:315
  39.7 74.6 %copy-start.11 = (bf16[6,64,512]{2,1,0:T(8,128)(2,1)}, bf16[6,64,512]{2,1,0:T(8,128)(2,1)S(1)}, u32[]{:S(2)}) copy-start(bf16[6,64,512]{2,1,0:T(8,128)(2,1)S(1)} %collective-permute-done.2.refs_0_) | copy-start | bytes 1179652
  39.7 30.1 %collective-permute-start.7 = (bf16[6,64,512]{2,1,0:T(8,128)(2,1)}, bf16[6,64,512]{2,1,0:T(8,128)(2,1)S(1)}, u32[]{:S(2)}, u32[]{:S(2)}) collective-permute-start(bf16[6,64,512]{2,1,0:T(8,128)(2,1)} %get-tuple-element.93), channel_id=1, source_target_pairs={{0,9},{1,8},{2,11},{3,10},{4,1},{5,0},{6,3},{7,2},{8,13},{9,12},{1... | collective-permute-start | bytes 1179656 | tf_op jit(solution)/shard_map/ppermute | solution.py:315
  48.4 65.9 %copy-start.12 = (bf16[6,64,512]{2,1,0:T(8,128)(2,1)}, bf16[6,64,512]{2,1,0:T(8,128)(2,1)S(1)}, u32[]{:S(2)}) copy-start(bf16[6,64,512]{2,1,0:T(8,128)(2,1)S(1)} %collective-permute-done.3.refs_1_) | copy-start | bytes 1179652
  48.4 26.4 %collective-permute-start.8 = (bf16[6,64,512]{2,1,0:T(8,128)(2,1)}, bf16[6,64,512]{2,1,0:T(8,128)(2,1)S(1)}, u32[]{:S(2)}, u32[]{:S(2)}) collective-permute-start(bf16[6,64,512]{2,1,0:T(8,128)(2,1)} %get-tuple-element.94), channel_id=1, source_target_pairs={{0,10},{1,11},{2,8},{3,9},{4,2},{5,3},{6,0},{7,1},{8,14},{9,15},{1... | collective-permute-start | bytes 1179656 | tf_op jit(solution)/shard_map/ppermute | solution.py:315
  57.0 57.3 %copy-start.13 = (bf16[6,64,512]{2,1,0:T(8,128)(2,1)}, bf16[6,64,512]{2,1,0:T(8,128)(2,1)S(1)}, u32[]{:S(2)}) copy-start(bf16[6,64,512]{2,1,0:T(8,128)(2,1)S(1)} %collective-permute-done.4.refs_2_) | copy-start | bytes 1179652
  57.0 22.0 %collective-permute-start.9 = (bf16[6,64,512]{2,1,0:T(8,128)(2,1)}, bf16[6,64,512]{2,1,0:T(8,128)(2,1)S(1)}, u32[]{:S(2)}, u32[]{:S(2)}) collective-permute-start(bf16[6,64,512]{2,1,0:T(8,128)(2,1)} %get-tuple-element.95), channel_id=1, source_target_pairs={{0,11},{1,10},{2,9},{3,8},{4,3},{5,2},{6,1},{7,0},{8,15},{9,14},{1... | collective-permute-start | bytes 1179656 | tf_op jit(solution)/shard_map/ppermute | solution.py:315
  62.8 16.2 %copy-start.19 = (bf16[6,64,512]{2,1,0:T(8,128)(2,1)}, bf16[6,64,512]{2,1,0:T(8,128)(2,1)S(1)}, u32[]{:S(2)}) copy-start(bf16[6,64,512]{2,1,0:T(8,128)(2,1)S(1)} %collective-permute-done.5.refs_3_) | copy-start | bytes 1179652
  62.8 43.3 %copy-start.20 = (bf16[6,64,512]{2,1,0:T(8,128)(2,1)}, bf16[6,64,512]{2,1,0:T(8,128)(2,1)S(1)}, u32[]{:S(2)}) copy-start(bf16[6,64,512]{2,1,0:T(8,128)(2,1)S(1)} %collective-permute-done.6.refs_4_) | copy-start | bytes 1179652
  69.8 39.9 %copy-start.21 = (bf16[6,64,512]{2,1,0:T(8,128)(2,1)}, bf16[6,64,512]{2,1,0:T(8,128)(2,1)S(1)}, u32[]{:S(2)}) copy-start(bf16[6,64,512]{2,1,0:T(8,128)(2,1)S(1)} %collective-permute-done.7.refs_5_) | copy-start | bytes 1179652
  74.8 34.9 %copy-start.22 = (bf16[6,64,512]{2,1,0:T(8,128)(2,1)}, bf16[6,64,512]{2,1,0:T(8,128)(2,1)S(1)}, u32[]{:S(2)}) copy-start(bf16[6,64,512]{2,1,0:T(8,128)(2,1)S(1)} %collective-permute-done.8.refs_6_) | copy-start | bytes 1179652
  79.0 30.7 %copy-start.24 = (bf16[6,64,512]{2,1,0:T(8,128)(2,1)}, bf16[6,64,512]{2,1,0:T(8,128)(2,1)S(1)}, u32[]{:S(2)}) copy-start(bf16[6,64,512]{2,1,0:T(8,128)(2,1)S(1)} %collective-permute-done.9.refs_7_) | copy-start | bytes 1179652
  79.0 57.7 %collective-permute-start.10 = (bf16[6,64,512]{2,1,0:T(8,128)(2,1)}, bf16[6,64,512]{2,1,0:T(8,128)(2,1)S(1)}, u32[]{:S(2)}, u32[]{:S(2)}) collective-permute-start(bf16[6,64,512]{2,1,0:T(8,128)(2,1)} %get-tuple-element.96), channel_id=1, source_target_pairs={{0,0},{1,1},{2,2},{3,3},{4,8},{5,9},{6,10},{7,11},{8,4},{9,5},{10,... | collective-permute-start | bytes 1179656 | tf_op jit(solution)/shard_map/ppermute | solution.py:315
  104.1 34.4 %collective-permute-start.11 = (bf16[6,64,512]{2,1,0:T(8,128)(2,1)}, bf16[6,64,512]{2,1,0:T(8,128)(2,1)S(1)}, u32[]{:S(2)}, u32[]{:S(2)}) collective-permute-start(bf16[6,64,512]{2,1,0:T(8,128)(2,1)} %get-tuple-element.97), channel_id=1, source_target_pairs={{0,1},{1,0},{2,3},{3,2},{4,9},{5,8},{6,11},{7,10},{8,5},{9,4},{10,... | collective-permute-start | bytes 1179656 | tf_op jit(solution)/shard_map/ppermute | solution.py:315
  105.0 35.0 %collective-permute-start.12 = (bf16[6,64,512]{2,1,0:T(8,128)(2,1)}, bf16[6,64,512]{2,1,0:T(8,128)(2,1)S(1)}, u32[]{:S(2)}, u32[]{:S(2)}) collective-permute-start(bf16[6,64,512]{2,1,0:T(8,128)(2,1)} %get-tuple-element.98), channel_id=1, source_target_pairs={{0,2},{1,3},{2,0},{3,1},{4,10},{5,11},{6,8},{7,9},{8,6},{9,7},{10,... | collective-permute-start | bytes 1179656 | tf_op jit(solution)/shard_map/ppermute | solution.py:315
  106.1 58.7 %collective-permute-start.13 = (bf16[6,64,512]{2,1,0:T(8,128)(2,1)}, bf16[6,64,512]{2,1,0:T(8,128)(2,1)S(1)}, u32[]{:S(2)}, u32[]{:S(2)}) collective-permute-start(bf16[6,64,512]{2,1,0:T(8,128)(2,1)} %get-tuple-element.99), channel_id=1, source_target_pairs={{0,3},{1,2},{2,1},{3,0},{4,11},{5,10},{6,9},{7,8},{8,7},{9,6},{10,... | collective-permute-start | bytes 1179656 | tf_op jit(solution)/shard_map/ppermute | solution.py:315
  109.7 55.1 %collective-permute-start.14 = (bf16[6,64,512]{2,1,0:T(8,128)(2,1)}, bf16[6,64,512]{2,1,0:T(8,128)(2,1)S(1)}, u32[]{:S(2)}, u32[]{:S(2)}) collective-permute-start(bf16[6,64,512]{2,1,0:T(8,128)(2,1)} %get-tuple-element.100), channel_id=1, source_target_pairs={{0,8},{1,9},{2,10},{3,11},{4,0},{5,1},{6,2},{7,3},{8,12},{9,13},{1... | collective-permute-start | bytes 1179656 | tf_op jit(solution)/shard_map/ppermute | solution.py:315
  132.1 6.4 copy-start.9
  132.1 7.9 %copy-start.8 = (bf16[6,64,512]{2,1,0:T(8,128)(2,1)S(1)}, bf16[6,64,512]{2,1,0:T(8,128)(2,1)}, u32[]{:S(2)}) copy-start(bf16[6,64,512]{2,1,0:T(8,128)(2,1)} %get-tuple-element.103) | copy-start | bytes 1179652
  136.7 28.1 %copy-start.14 = (bf16[6,64,512]{2,1,0:T(8,128)(2,1)}, bf16[6,64,512]{2,1,0:T(8,128)(2,1)S(1)}, u32[]{:S(2)}) copy-start(bf16[6,64,512]{2,1,0:T(8,128)(2,1)S(1)} %collective-permute-done.10.refs_0_) | copy-start | bytes 1179652
  136.7 28.1 %collective-permute-start.15 = (bf16[6,64,512]{2,1,0:T(8,128)(2,1)S(1)}, bf16[6,64,512]{2,1,0:T(8,128)(2,1)S(1)}, u32[]{:S(2)}, u32[]{:S(2)}) collective-permute-start(bf16[6,64,512]{2,1,0:T(8,128)(2,1)S(1)} %copy-done.10), channel_id=1, source_target_pairs={{0,9},{1,8},{2,11},{3,10},{4,1},{5,0},{6,3},{7,2},{8,13},{9,12},{1... | collective-permute-start | bytes 1179656 | tf_op jit(solution)/shard_map/ppermute | solution.py:315
  138.5 26.3 %copy-start.15 = (bf16[6,64,512]{2,1,0:T(8,128)(2,1)}, bf16[6,64,512]{2,1,0:T(8,128)(2,1)S(1)}, u32[]{:S(2)}) copy-start(bf16[6,64,512]{2,1,0:T(8,128)(2,1)S(1)} %collective-permute-done.11.refs_1_) | copy-start | bytes 1179652
  138.5 26.4 %collective-permute-start.16 = (bf16[6,64,512]{2,1,0:T(8,128)(2,1)S(1)}, bf16[6,64,512]{2,1,0:T(8,128)(2,1)S(1)}, u32[]{:S(2)}, u32[]{:S(2)}) collective-permute-start(bf16[6,64,512]{2,1,0:T(8,128)(2,1)S(1)} %copy-done.9), channel_id=1, source_target_pairs={{0,10},{1,11},{2,8},{3,9},{4,2},{5,3},{6,0},{7,1},{8,14},{9,15},{1... | collective-permute-start | bytes 1179656 | tf_op jit(solution)/shard_map/ppermute | solution.py:315
  140.0 24.8 %copy-start.16 = (bf16[6,64,512]{2,1,0:T(8,128)(2,1)}, bf16[6,64,512]{2,1,0:T(8,128)(2,1)S(1)}, u32[]{:S(2)}) copy-start(bf16[6,64,512]{2,1,0:T(8,128)(2,1)S(1)} %collective-permute-done.12.refs_2_) | copy-start | bytes 1179652
  140.0 26.9 %collective-permute-start.17 = (bf16[6,64,512]{2,1,0:T(8,128)(2,1)S(1)}, bf16[6,64,512]{2,1,0:T(8,128)(2,1)S(1)}, u32[]{:S(2)}, u32[]{:S(2)}) collective-permute-start(bf16[6,64,512]{2,1,0:T(8,128)(2,1)S(1)} %copy-done.8), channel_id=1, source_target_pairs={{0,11},{1,10},{2,9},{3,8},{4,3},{5,2},{6,1},{7,0},{8,15},{9,14},{1... | collective-permute-start | bytes 1179656 | tf_op jit(solution)/shard_map/ppermute | solution.py:315
  142.0 33.0 %copy-start.32 = (bf16[4,64,512]{2,1,0:T(8,128)(2,1)S(1)}, bf16[4,64,512]{2,1,0:T(8,128)(2,1)}, u32[]{:S(2)}) copy-start(bf16[4,64,512]{2,1,0:T(8,128)(2,1)} %get-tuple-element.114) | copy-start | bytes 786436
  142.0 33.0 %copy-start.31 = (bf16[4,64,512]{2,1,0:T(8,128)(2,1)S(1)}, bf16[4,64,512]{2,1,0:T(8,128)(2,1)}, u32[]{:S(2)}) copy-start(bf16[4,64,512]{2,1,0:T(8,128)(2,1)} %get-tuple-element.115) | copy-start | bytes 786436
  142.0 36.7 %copy-start.30 = (bf16[4,64,512]{2,1,0:T(8,128)(2,1)S(1)}, bf16[4,64,512]{2,1,0:T(8,128)(2,1)}, u32[]{:S(2)}) copy-start(bf16[4,64,512]{2,1,0:T(8,128)(2,1)} %get-tuple-element.116) | copy-start | bytes 786436
  142.0 39.4 %copy-start.29 = (bf16[4,64,512]{2,1,0:T(8,128)(2,1)S(1)}, bf16[4,64,512]{2,1,0:T(8,128)(2,1)}, u32[]{:S(2)}) copy-start(bf16[4,64,512]{2,1,0:T(8,128)(2,1)} %get-tuple-element.117) | copy-start | bytes 786436
  142.0 45.8 %copy-start.28 = (bf16[4,64,512]{2,1,0:T(8,128)(2,1)S(1)}, bf16[4,64,512]{2,1,0:T(8,128)(2,1)}, u32[]{:S(2)}) copy-start(bf16[4,64,512]{2,1,0:T(8,128)(2,1)} %get-tuple-element.118) | copy-start | bytes 786436
  142.0 47.2 %copy-start.27 = (bf16[4,64,512]{2,1,0:T(8,128)(2,1)S(1)}, bf16[4,64,512]{2,1,0:T(8,128)(2,1)}, u32[]{:S(2)}) copy-start(bf16[4,64,512]{2,1,0:T(8,128)(2,1)} %get-tuple-element.119) | copy-start | bytes 786436
  164.8 24.5 %copy-start.17 = (bf16[6,64,512]{2,1,0:T(8,128)(2,1)}, bf16[6,64,512]{2,1,0:T(8,128)(2,1)S(1)}, u32[]{:S(2)}) copy-start(bf16[6,64,512]{2,1,0:T(8,128)(2,1)S(1)} %collective-permute-done.13.refs_3_) | copy-start | bytes 1179652
  164.8 24.5 %copy-start.18 = (bf16[6,64,512]{2,1,0:T(8,128)(2,1)}, bf16[6,64,512]{2,1,0:T(8,128)(2,1)S(1)}, u32[]{:S(2)}) copy-start(bf16[6,64,512]{2,1,0:T(8,128)(2,1)S(1)} %collective-permute-done.14.refs_4_) | copy-start | bytes 1179652
  164.8 24.5 %copy-start.23 = (bf16[6,64,512]{2,1,0:T(8,128)(2,1)}, bf16[6,64,512]{2,1,0:T(8,128)(2,1)S(1)}, u32[]{:S(2)}) copy-start(bf16[6,64,512]{2,1,0:T(8,128)(2,1)S(1)} %collective-permute-done.15.refs_5_) | copy-start | bytes 1179652
  164.9 24.5 %copy-start.25 = (bf16[6,64,512]{2,1,0:T(8,128)(2,1)}, bf16[6,64,512]{2,1,0:T(8,128)(2,1)S(1)}, u32[]{:S(2)}) copy-start(bf16[6,64,512]{2,1,0:T(8,128)(2,1)S(1)} %collective-permute-done.16.refs_6_) | copy-start | bytes 1179652
  166.9 22.5 %copy-start.26 = (bf16[6,64,512]{2,1,0:T(8,128)(2,1)}, bf16[6,64,512]{2,1,0:T(8,128)(2,1)S(1)}, u32[]{:S(2)}) copy-start(bf16[6,64,512]{2,1,0:T(8,128)(2,1)S(1)} %collective-permute-done.17.refs_7_) | copy-start | bytes 1179652
  166.9 14.4 %collective-permute-start.18 = (bf16[4,64,512]{2,1,0:T(8,128)(2,1)}, bf16[4,64,512]{2,1,0:T(8,128)(2,1)S(1)}, u32[]{:S(2)}, u32[]{:S(2)}) collective-permute-start(bf16[4,64,512]{2,1,0:T(8,128)(2,1)} %get-tuple-element.112), channel_id=1, source_target_pairs={{0,0},{1,1},{2,2},{3,3},{4,8},{5,9},{6,10},{7,11},{8,4},{9,5},{10,... | collective-permute-start | bytes 786440 | tf_op jit(solution)/shard_map/ppermute | solution.py:315
  174.1 13.6 %collective-permute-start.19 = (bf16[4,64,512]{2,1,0:T(8,128)(2,1)}, bf16[4,64,512]{2,1,0:T(8,128)(2,1)S(1)}, u32[]{:S(2)}, u32[]{:S(2)}) collective-permute-start(bf16[4,64,512]{2,1,0:T(8,128)(2,1)} %get-tuple-element.113), channel_id=1, source_target_pairs={{0,1},{1,0},{2,3},{3,2},{4,9},{5,8},{6,11},{7,10},{8,5},{9,4},{10,... | collective-permute-start | bytes 786440 | tf_op jit(solution)/shard_map/ppermute | solution.py:315
  174.9 14.2 %collective-permute-start.20 = (bf16[4,64,512]{2,1,0:T(8,128)(2,1)S(1)}, bf16[4,64,512]{2,1,0:T(8,128)(2,1)S(1)}, u32[]{:S(2)}, u32[]{:S(2)}) collective-permute-start(bf16[4,64,512]{2,1,0:T(8,128)(2,1)S(1)} %copy-done.32), channel_id=1, source_target_pairs={{0,2},{1,3},{2,0},{3,1},{4,10},{5,11},{6,8},{7,9},{8,6},{9,7},{10,... | collective-permute-start | bytes 786440 | tf_op jit(solution)/shard_map/ppermute | solution.py:315
  175.0 37.2 %collective-permute-start.21 = (bf16[4,64,512]{2,1,0:T(8,128)(2,1)S(1)}, bf16[4,64,512]{2,1,0:T(8,128)(2,1)S(1)}, u32[]{:S(2)}, u32[]{:S(2)}) collective-permute-start(bf16[4,64,512]{2,1,0:T(8,128)(2,1)S(1)} %copy-done.31), channel_id=1, source_target_pairs={{0,3},{1,2},{2,1},{3,0},{4,11},{5,10},{6,9},{7,8},{8,7},{9,6},{10,... | collective-permute-start | bytes 786440 | tf_op jit(solution)/shard_map/ppermute | solution.py:315
  178.7 33.5 %collective-permute-start.22 = (bf16[4,64,512]{2,1,0:T(8,128)(2,1)S(1)}, bf16[4,64,512]{2,1,0:T(8,128)(2,1)S(1)}, u32[]{:S(2)}, u32[]{:S(2)}) collective-permute-start(bf16[4,64,512]{2,1,0:T(8,128)(2,1)S(1)} %copy-done.30), channel_id=1, source_target_pairs={{0,8},{1,9},{2,10},{3,11},{4,0},{5,1},{6,2},{7,3},{8,12},{9,13},{1... | collective-permute-start | bytes 786440 | tf_op jit(solution)/shard_map/ppermute | solution.py:315
  181.4 30.7 %copy-start.33 = (bf16[4,64,512]{2,1,0:T(8,128)(2,1)}, bf16[4,64,512]{2,1,0:T(8,128)(2,1)S(1)}, u32[]{:S(2)}) copy-start(bf16[4,64,512]{2,1,0:T(8,128)(2,1)S(1)} %collective-permute-done.18.refs_0_) | copy-start | bytes 786436
  181.4 30.8 %collective-permute-start.23 = (bf16[4,64,512]{2,1,0:T(8,128)(2,1)S(1)}, bf16[4,64,512]{2,1,0:T(8,128)(2,1)S(1)}, u32[]{:S(2)}, u32[]{:S(2)}) collective-permute-start(bf16[4,64,512]{2,1,0:T(8,128)(2,1)S(1)} %copy-done.29), channel_id=1, source_target_pairs={{0,9},{1,8},{2,11},{3,10},{4,1},{5,0},{6,3},{7,2},{8,13},{9,12},{1... | collective-permute-start | bytes 786440 | tf_op jit(solution)/shard_map/ppermute | solution.py:315
  187.8 24.3 %copy-start.34 = (bf16[4,64,512]{2,1,0:T(8,128)(2,1)}, bf16[4,64,512]{2,1,0:T(8,128)(2,1)S(1)}, u32[]{:S(2)}) copy-start(bf16[4,64,512]{2,1,0:T(8,128)(2,1)S(1)} %collective-permute-done.19.refs_1_) | copy-start | bytes 786436
  187.8 24.4 %collective-permute-start.24 = (bf16[4,64,512]{2,1,0:T(8,128)(2,1)S(1)}, bf16[4,64,512]{2,1,0:T(8,128)(2,1)S(1)}, u32[]{:S(2)}, u32[]{:S(2)}) collective-permute-start(bf16[4,64,512]{2,1,0:T(8,128)(2,1)S(1)} %copy-done.28), channel_id=1, source_target_pairs={{0,10},{1,11},{2,8},{3,9},{4,2},{5,3},{6,0},{7,1},{8,14},{9,15},{1... | collective-permute-start | bytes 786440 | tf_op jit(solution)/shard_map/ppermute | solution.py:315
  189.2 23.0 %copy-start.35 = (bf16[4,64,512]{2,1,0:T(8,128)(2,1)}, bf16[4,64,512]{2,1,0:T(8,128)(2,1)S(1)}, u32[]{:S(2)}) copy-start(bf16[4,64,512]{2,1,0:T(8,128)(2,1)S(1)} %collective-permute-done.20.refs_2_) | copy-start | bytes 786436
  189.2 23.0 %collective-permute-start.25 = (bf16[4,64,512]{2,1,0:T(8,128)(2,1)S(1)}, bf16[4,64,512]{2,1,0:T(8,128)(2,1)S(1)}, u32[]{:S(2)}, u32[]{:S(2)}) collective-permute-start(bf16[4,64,512]{2,1,0:T(8,128)(2,1)S(1)} %copy-done.27), channel_id=1, source_target_pairs={{0,11},{1,10},{2,9},{3,8},{4,3},{5,2},{6,1},{7,0},{8,15},{9,14},{1... | collective-permute-start | bytes 786440 | tf_op jit(solution)/shard_map/ppermute | solution.py:315
  213.7 219.1 %all-to-all-start = ((bf16[8,36,64,512]{3,2,1,0:T(8,128)(2,1)}), bf16[8,36,64,512]{3,2,1,0:T(8,128)(2,1)}, u32[]{:S(2)}, u32[]{:S(2)}) async-start(bf16[8,36,64,512]{3,2,1,0:T(8,128)(2,1)} %bitcast.29), calls=%async_computation | async-start | bytes 37748736 | tf_op jit(solution)/shard_map/all_to_all | solution.py:256
  236.2 196.6 %collective-permute-start.26 = (bf16[64,512,128]{2,1,0:T(8,128)(2,1)}, bf16[64,512,128]{2,1,0:T(8,128)(2,1)}, u32[]{:S(2)}, u32[]{:S(2)}) collective-permute-start(bf16[64,512,128]{2,1,0:T(8,128)(2,1)} %bitcast_convert_fusion), channel_id=1, source_target_pairs={{0,16},{1,17},{2,18},{3,19},{4,20},{5,21},{6,22},{7,23},{8,24},{9,... | collective-permute-start | bytes 25165832 | tf_op jit(solution)/shard_map/ppermute | solution.py:333
  432.8 24.2 %all-to-all-start.1 = ((bf16[8,12,16,512]{3,2,1,0:T(8,128)(2,1)}), bf16[8,12,16,512]{3,2,1,0:T(8,128)(2,1)S(1)}, u32[]{:S(2)}, u32[]{:S(2)}) async-start(bf16[8,12,16,512]{3,2,1,0:T(8,128)(2,1)} %bitcast.34), calls=%async_computation.1 | async-start | bytes 3145728 | tf_op jit(solution)/shard_map/all_to_all | solution.py:256
  467.0 38.0 %all-to-all-start.2 = ((bf16[8,12,16,512]{3,2,1,0:T(8,128)(2,1)}), bf16[8,12,16,512]{3,2,1,0:T(8,128)(2,1)S(1)}, u32[]{:S(2)}, u32[]{:S(2)}) async-start(bf16[8,12,16,512]{3,2,1,0:T(8,128)(2,1)} %bitcast.14), calls=%async_computation.2 | async-start | bytes 3145728 | tf_op jit(solution)/shard_map/all_to_all | solution.py:256
  470.7 50.1 %collective-permute-start.27 = (bf16[16,512,128]{2,1,0:T(8,128)(2,1)}, bf16[16,512,128]{2,1,0:T(8,128)(2,1)}, u32[]{:S(2)}, u32[]{:S(2)}) collective-permute-start(bf16[16,512,128]{2,1,0:T(8,128)(2,1)} %finished.4), channel_id=1, source_target_pairs={{0,16},{1,17},{2,18},{3,19},{8,20},{9,21},{10,22},{11,23},{4,24},{... | collective-permute-start | bytes 6291464 | tf_op jit(solution)/shard_map/ppermute | solution.py:346
  520.8 37.9 %all-to-all-start.3 = ((bf16[8,12,16,512]{3,2,1,0:T(8,128)(2,1)}), bf16[8,12,16,512]{3,2,1,0:T(8,128)(2,1)S(1)}, u32[]{:S(2)}, u32[]{:S(2)}) async-start(bf16[8,12,16,512]{3,2,1,0:T(8,128)(2,1)} %bitcast.13), calls=%async_computation.3 | async-start | bytes 3145728 | tf_op jit(solution)/shard_map/all_to_all | solution.py:256
  524.4 50.2 %collective-permute-start.28 = (bf16[16,512,128]{2,1,0:T(8,128)(2,1)}, bf16[16,512,128]{2,1,0:T(8,128)(2,1)}, u32[]{:S(2)}, u32[]{:S(2)}) collective-permute-start(bf16[16,512,128]{2,1,0:T(8,128)(2,1)} %finished.5), channel_id=1, source_target_pairs={{0,16},{1,17},{2,18},{3,19},{8,20},{9,21},{10,22},{11,23},{4,24},{... | collective-permute-start | bytes 6291464 | tf_op jit(solution)/shard_map/ppermute | solution.py:346
  574.5 38.8 %all-to-all-start.4 = ((bf16[8,12,16,512]{3,2,1,0:T(8,128)(2,1)}), bf16[8,12,16,512]{3,2,1,0:T(8,128)(2,1)S(1)}, u32[]{:S(2)}, u32[]{:S(2)}) async-start(bf16[8,12,16,512]{3,2,1,0:T(8,128)(2,1)} %bitcast.12), calls=%async_computation.4 | async-start | bytes 3145728 | tf_op jit(solution)/shard_map/all_to_all | solution.py:256
  578.3 50.2 %collective-permute-start.29 = (bf16[16,512,128]{2,1,0:T(8,128)(2,1)}, bf16[16,512,128]{2,1,0:T(8,128)(2,1)}, u32[]{:S(2)}, u32[]{:S(2)}) collective-permute-start(bf16[16,512,128]{2,1,0:T(8,128)(2,1)} %finished.6), channel_id=1, source_target_pairs={{0,16},{1,17},{2,18},{3,19},{8,20},{9,21},{10,22},{11,23},{4,24},{... | collective-permute-start | bytes 6291464 | tf_op jit(solution)/shard_map/ppermute | solution.py:346
  628.5 49.9 %collective-permute-start.30 = (bf16[16,512,128]{2,1,0:T(8,128)(2,1)}, bf16[16,512,128]{2,1,0:T(8,128)(2,1)S(1)}, u32[]{:S(2)}, u32[]{:S(2)}) collective-permute-start(bf16[16,512,128]{2,1,0:T(8,128)(2,1)} %finished.7), channel_id=1, source_target_pairs={{0,16},{1,17},{2,18},{3,19},{8,20},{9,21},{10,22},{11,23},{4,24},{... | collective-permute-start | bytes 6291464 | tf_op jit(solution)/shard_map/ppermute | solution.py:346
  (14 other events, 17.5 us)
Sparse Core Ops, SparseCore 0:
  8.9 84.6 all-gather.1

commit v6 on v5

--- a/solution.py
+++ b/solution.py
@@ -8,7 +8,7 @@
 TICKS = 2
 ENDS = (6, 12, 16)
 ROW_TILE = 16
-PIECE = 512
+PIECE = 256
 AXES = ("lane", "core", "half", "rest")
 GROUP = ("core", "rest")
 VMEM = pltpu.CompilerParams(vmem_limit_bytes=58 << 20)
@@ -83,13 +83,14 @@
     def body(table_ref, _, source, out):
         line = pl.program_id(0)
         out[...] = jnp.zeros(out.shape, out.dtype)
-        for q in range(outs_count):
+
+        @pl.loop(0, outs_count)
+        def _(q):
+            fixed = pl.ds(pl.multiple_of(q * wide, wide), wide)
             for t in range(slots):
                 place = table_ref[((shear * lines + line) * outs_count + q) * slots + t]
-                start = pl.multiple_of(place * wide, wide)
+                moved = pl.ds(pl.multiple_of(place * wide, wide), wide)
                 block = source[0, 0, 0, q, t]
-                fixed = pl.ds(q * wide, wide)
-                moved = pl.ds(start, wide)
                 if transposed:
                     out[0, moved, fixed] += block.T
                 else:
@@ -115,7 +116,7 @@
     )(table, which, blocks)
 
 
-def relayed(values, member, first, second, targets, start):
+def relayed(values, member, first, second, targets, start, compact=False):
     row_chunks = len(targets)
     members = len(values)
     each, rows, width = values[0].shape
@@ -133,12 +134,26 @@
         for k in range(members):
             source[member_ref[0] ^ k] = pieces[k][...]
 
+        def rows_of(i):
+            return pl.ds(pl.multiple_of(i * wide, wide) if compact else i * wide, wide)
+
+        def over_lines(step):
+            if compact:
+                pl.loop(0, lines)(step)
+            else:
+                for i in range(lines):
+                    step(i)
+
         def shears(load, k, slots):
             for s in range(len(slots)):
-                for i in range(lines):
+
+                @over_lines
+                def _(i):
                     got = jnp.dot(load(s, i), mats[3 * k][i], preferred_element_type=jnp.float32).astype(jnp.bfloat16)
+                    at_rows = rows_of(i)
                     for j in range(lines):
-                        one[j, i * wide : (i + 1) * wide, s * wide : (s + 1) * wide] = got[:, j * wide : (j + 1) * wide]
+                        one[j, at_rows, s * wide : (s + 1) * wide] = got[:, j * wide : (j + 1) * wide]
+
             span = len(slots) * wide
             for j in range(lines):
                 got = jnp.dot(mats[3 * k + 1][j], one[j, :, :span], preferred_element_type=jnp.float32)
@@ -146,22 +161,25 @@
                 for s in range(len(slots)):
                     two[s, :, j * wide : (j + 1) * wide] = got[:, s * wide : (s + 1) * wide]
             for s, (term, ch) in enumerate(slots):
-                for i in range(lines):
-                    lhs = two[s, i * wide : (i + 1) * wide]
+
+                @over_lines
+                def _(i):
+                    at_rows = rows_of(i)
+                    lhs = two[s, at_rows]
                     got = jnp.dot(lhs, mats[3 * k + 2][i], preferred_element_type=jnp.float32).astype(jnp.bfloat16)
                     if term == 0:
-                        kept[ch, i * wide : (i + 1) * wide] = got
+                        kept[ch, at_rows] = got
                     split = got.reshape(per, row_chunks, height, width)
                     for r in range(row_chunks):
-                        outs[r][per * i : per * (i + 1), term, ch] = split[:, r]
+                        outs[r][pl.ds(per * i, per), term, ch] = split[:, r]
 
         def fresh(ch, i):
-            return source[per * i : per * (i + 1), ch].reshape(wide, width)
+            return source[pl.ds(per * i, per), ch].reshape(wide, width)
 
         def held(s, i):
             if s < pair:
                 return fresh(s, i)
-            return kept[s - pair, i * wide : (i + 1) * wide]
+            return kept[s - pair, rows_of(i)]
 
         shears(fresh, 0, [(0, ch) for ch in range(pair)])
         shears(held, 1, [(term, ch) for term in (1, 2) for ch in range(pair)])
@@ -328,7 +346,7 @@
         for k in range(last):
             full.append(delivered(k + 1, *full[k], *(solved if k else [])))
             solved = relayed(full[k], member, *weights, solved, starts[k])
-        ends = relayed(full[last], member, *weights, [room(sizes[last], ROW_TILE)] * row_chunks, 0)
+        ends = relayed(full[last], member, *weights, [room(sizes[last], ROW_TILE)] * row_chunks, 0, compact=True)
         (solved,) = later(solved, *full[last])
         old = lax.ppermute(tied(memory[0].astype(jnp.bfloat16), *full[last]), AXES, shift_route)
         terms = [exchanged(solved.reshape(members, -1, height, width)).reshape(solved.shape)]

time: 701 us -> 693 us (0.989); the launches traced: 692 us -> 691 us
  Pallas kernels: 156 us -> 177 us
  waiting for transfers between devices: 405 us -> 386 us
    all_to_all x5, waiting for transfers between devices: 295 us -> 278 us  [exchanged(): lax.all_to_all(values, GROUP, split_axis=0, concat_axis=0, tiled=True)]
    pallas_call x3, Pallas kernels: 63 us -> 79.3 us  [relayed(): pl.pallas_call(body, grid_spec=pltpu.PrefetchScalarGridSpec(num_scalar_pr...]
  transfers between devices with their start and end apart: 37 -> 37, of which waited for: 20 -> 20; matrix products, arithmetic and copies ran while one was open for 2% -> 2% of each run, Pallas kernels for 21% -> 24%
where the time goes in v6:
time: 693 us; the launch traced here: 691 us
  waiting for transfers between devices  386 us (56%)
  Pallas kernels  177 us (26%)
  starting transfers between devices  95.2 us (14%)
  between operations  13.8 us (2%)
  other arithmetic  10.4 us (2%)
  local copies, waits for them, and re-layouts  9.09 us (1%)
    all_to_all x5, waiting for transfers between devices, exchanged(): lax.all_to_all(values, GROUP, split_axis=0, concat_axis=0, tiled=True)  278 us
    pallas_call x3, Pallas kernels, relayed(): pl.pallas_call(body, grid_spec=pltpu.PrefetchScalarGridSpec(num_scalar_pr...  79.3 us
    ppermute x24, waiting for transfers between devices, delivered(): lax.ppermute(piece, AXES, route)  56.7 us
    ppermute x24, starting transfers between devices, delivered(): lax.ppermute(piece, AXES, route)  54.1 us
    ppermute x4, waiting for transfers between devices, on_device(): lax.ppermute(tied(rows, moved[-1]) if ending else rows, AXES, return_route)  49.9 us
    pallas_call x4, Pallas kernels, finished(): pl.pallas_call(body, grid=(width // piece,), in_specs=[term_block(a, row_...  38.1 us
    pallas_call x6, Pallas kernels, dense(): pl.pallas_call(body, grid_spec=pltpu.PrefetchScalarGridSpec(num_scalar_pr...  28.6 us
    all_to_all x5, starting transfers between devices, exchanged(): lax.all_to_all(values, GROUP, split_axis=0, concat_axis=0, tiled=True)  27.7 us
  transfers between devices with their start and end apart: 37, of which 20 were waited for; matrix products, arithmetic and copies ran while one was open for 2% of the time, Pallas kernels for 24%

profile of v6, /device:TPU:1, one launch (start us, length us, event | category | flops | bytes accessed | tf_op | source)
XLA Modules:
  0.0 691.4 jit_solution(8849884913755158548)
XLA Ops:
  7.7 5.6 collective-permute-start
  13.4 12.2 %spread.1 = (bf16[6,64,512]{2,1,0:T(8,128)(2,1)}, bf16[6,64,512]{2,1,0:T(8,128)(2,1)}, bf16[6,64,512]{2,1,0:T(8,128)(2,1)}, bf16[6,64,512]{2,1,0:T(8,128)(2,1)},...) custom-call(s32[1]{0:T(128)} %bitcast.1.band_ref, ...), custom_call_target="tpu_custom_call" | custom-call | bytes 33554432 | tf_op jit(solution)/shard_map/spread/pallas_call | solution.py:53
  25.7 1.9 collective-permute-start.2
  27.6 3.6 collective-permute-start.3
  32.2 2.6 collective-permute-start.5
  34.7 5.0 collective-permute-done.2.refs_0_
  39.7 8.7 %collective-permute-done.3.refs_1_ = bf16[6,64,512]{2,1,0:T(8,128)(2,1)S(1)} collective-permute-done((bf16[6,64,512]{2,1,0:T(8,128)(2,1)}, bf16[6,64,512]{2,1,0:T(8,128)(2,1)S(1)}, u32[]{:S(2)}, u32[]{:S(2)}) %collective-permute-start.3) | collective-permute-done | bytes 393248 | tf_op jit(solution)/shard_map/ppermute | solution.py:333
  48.4 8.6 %collective-permute-done.4.refs_2_ = bf16[6,64,512]{2,1,0:T(8,128)(2,1)S(1)} collective-permute-done((bf16[6,64,512]{2,1,0:T(8,128)(2,1)}, bf16[6,64,512]{2,1,0:T(8,128)(2,1)S(1)}, u32[]{:S(2)}, u32[]{:S(2)}) %collective-permute-start.4) | collective-permute-done | bytes 393248 | tf_op jit(solution)/shard_map/ppermute | solution.py:333
  57.0 5.8 collective-permute-done.5.refs_3_
  62.8 7.0 %collective-permute-done.7.refs_5_ = bf16[6,64,512]{2,1,0:T(8,128)(2,1)S(1)} collective-permute-done((bf16[6,64,512]{2,1,0:T(8,128)(2,1)}, bf16[6,64,512]{2,1,0:T(8,128)(2,1)S(1)}, u32[]{:S(2)}, u32[]{:S(2)}) %collective-permute-start.7) | collective-permute-done | bytes 393248 | tf_op jit(solution)/shard_map/ppermute | solution.py:333
  69.8 5.0 collective-permute-done.8.refs_6_
  74.8 4.2 collective-permute-done.9.refs_7_
  79.0 25.0 %collective-permute-start.10 = (bf16[6,64,512]{2,1,0:T(8,128)(2,1)}, bf16[6,64,512]{2,1,0:T(8,128)(2,1)S(1)}, u32[]{:S(2)}, u32[]{:S(2)}) collective-permute-start(bf16[6,64,512]{2,1,0:T(8,128)(2,1)} %get-tuple-element.96), channel_id=1, source_target_pairs={{0,0},{1,1},{2,2},{3,3},{4,8},{5,9},{6,10},{7,11},{8,4},{9,5},{10,... | collective-permute-start | bytes 1179656 | tf_op jit(solution)/shard_map/ppermute | solution.py:333
  106.1 3.6 collective-permute-start.13
  109.8 4.9 dense.6.refs_8_
  114.7 4.5 dense.7.refs_9_
  119.2 4.9 dense.8.refs_10_
  124.1 4.9 dense.9.refs_11_
  129.0 4.4 dense.10.refs_12_
  133.4 5.0 dense.11.refs_13_
  138.5 1.8 collective-permute-start.15
  140.3 1.4 collective-permute-start.16
  141.7 2.0 collective-permute-start.17
  143.8 22.8 %relayed.3.refs_14_ = bf16[8,3,12,64,512]{4,3,2,1,0:T(8,128)(2,1)} custom-call(s32[1]{0:T(128)} %bitcast.member_ref, bf16[6,64,512]{2,1,0:T(8,128)(2,1)} %copy-done.11, bf16[6,64,512]{2,1,0:T(8,128)(2,1)} %copy-done.12, bf16[6,64,512]{2,1,0:T(8,128)(2,1)} %copy-done.13, bf16[6,64,512]{2,1,0:T(8,128)(2,1)} %copy-done.19, bf16[6,64,512]{2,1,0:T(8,128)(2,1)} %copy-done.20, ...), custom_call_target="tpu_custom_call" | custom-call | flops 28991029248 | bytes 25165824 | tf_op jit(solution)/shard_map/relayed/pallas_call | solution.py:188
  166.6 2.0 collective-permute-done.17.refs_7_
  168.7 5.5 collective-permute-start.18
  175.0 3.7 collective-permute-start.21
  178.7 2.7 collective-permute-done.18.refs_0_
  181.4 6.4 collective-permute-done.19.refs_1_
  187.7 1.4 collective-permute-done.20.refs_2_
  189.4 22.7 %relayed.4 = bf16[8,3,12,64,512]{4,3,2,1,0:T(8,128)(2,1)} custom-call(s32[1]{0:T(128)} %bitcast.member_ref, bf16[6,64,512]{2,1,0:T(8,128)(2,1)} %copy-done.14, bf16[6,64,512]{2,1,0:T(8,128)(2,1)} %copy-done.15, bf16[6,64,512]{2,1,0:T(8,128)(2,1)} %copy-done.16, bf16[6,64,512]{2,1,0:T(8,128)(2,1)} %copy-done.17, ...), custom_call_target="tpu_custom_call", output_to_operand_aliasing={{}: (15, {})} | custom-call | flops 28991029248 | bytes 25165824 | tf_op jit(solution)/shard_map/relayed/pallas_call | solution.py:188
  213.7 13.2 %all-to-all-start = ((bf16[8,36,64,512]{3,2,1,0:T(8,128)(2,1)}), bf16[8,36,64,512]{3,2,1,0:T(8,128)(2,1)}, u32[]{:S(2)}, u32[]{:S(2)}) async-start(bf16[8,36,64,512]{3,2,1,0:T(8,128)(2,1)} %bitcast.29), calls=%async_computation | async-start | bytes 37748736 | tf_op jit(solution)/shard_map/all_to_all | solution.py:274
  226.9 9.2 %bitcast_convert_fusion = bf16[64,512,128]{2,1,0:T(8,128)(2,1)} fusion(f32[1,64,512,128]{3,2,1,0:T(8,128)} %param.5), kind=kLoop, calls=%fused_computation.14 | loop fusion | flops 4194304 | bytes 25165824 | tf_op jit(solution)/shard_map/convert_element_type | solution.py:351
  236.0 1.4 collective-permute-start.26
  237.4 33.8 %relayed.5 = (bf16[8,3,4,16,512]{4,3,2,1,0:T(8,128)(2,1)}, bf16[8,3,4,16,512]{4,3,2,1,0:T(8,128)(2,1)}, bf16[8,3,4,16,512]{4,3,2,1,0:T(8,128)(2,1)}, bf16[8,3,4,16,512]{4,3,2,1,0:T(8,128)(2,1)}) custom-call(s32[1]{0:T(128)} %bitcast.member_ref, bf16[4,64,512]{2,1,0:T(8,128)(2,1)} %copy-done.33, bf16[4,64,512]{2,1,0:T(8,128)(2,1)} %copy-done.34, ...), custom_call_target="tpu_custom_call" | custom-call | flops 19327352832 | bytes 20971520 | tf_op jit(solution)/shard_map/relayed/pallas_call | solution.py:188
  271.2 161.4 %all-to-all-done = bf16[8,36,64,512]{3,2,1,0:T(8,128)(2,1)} async-done(((bf16[8,36,64,512]{3,2,1,0:T(8,128)(2,1)}), bf16[8,36,64,512]{3,2,1,0:T(8,128)(2,1)}, u32[]{:S(2)}, u32[]{:S(2)}) %all-to-all-start) | async-done | bytes 18874400 | tf_op jit(solution)/shard_map/all_to_all | solution.py:274
  432.7 3.7 all-to-all-start.1
  437.6 19.1 %all-to-all-done.1 = bf16[8,12,16,512]{3,2,1,0:T(8,128)(2,1)S(1)} async-done(((bf16[8,12,16,512]{3,2,1,0:T(8,128)(2,1)}), bf16[8,12,16,512]{3,2,1,0:T(8,128)(2,1)S(1)}, u32[]{:S(2)}, u32[]{:S(2)}) %all-to-all-start.1) | async-done | bytes 1572896 | tf_op jit(solution)/shard_map/all_to_all | solution.py:274
  456.7 1.1 copy-done.1
  457.8 9.5 %finished.4 = bf16[16,512,128]{2,1,0:T(8,128)(2,1)} custom-call(bf16[8,3,12,64,512]{4,3,2,1,0:T(8,128)(2,1)} %bitcast.11.refs_0_, bf16[8,3,4,16,512]{4,3,2,1,0:T(8,128)(2,1)} %bitcast.31, bf16[128,128]{1,0:T(8,128)(2,1)} %slice.28.refs_2_, bf16[128,128]{1,0:T(8,128)(2,1)} %slice.29.refs_3_), custom_call_target="tpu_custom_call" | custom-call | bytes 4718592 | tf_op jit(solution)/shard_map/finished/pallas_call | solution.py:237
  467.3 3.8 all-to-all-start.2
  471.0 1.7 collective-permute-start.27
  472.8 32.7 %all-to-all-done.2 = bf16[8,12,16,512]{3,2,1,0:T(8,128)(2,1)S(1)} async-done(((bf16[8,12,16,512]{3,2,1,0:T(8,128)(2,1)}), bf16[8,12,16,512]{3,2,1,0:T(8,128)(2,1)S(1)}, u32[]{:S(2)}, u32[]{:S(2)}) %all-to-all-start.2) | async-done | bytes 1572896 | tf_op jit(solution)/shard_map/all_to_all | solution.py:274
  505.5 1.2 copy-done.2
  506.7 9.6 %finished.5 = bf16[16,512,128]{2,1,0:T(8,128)(2,1)} custom-call(bf16[8,3,12,64,512]{4,3,2,1,0:T(8,128)(2,1)} %bitcast.11.refs_0_, bf16[8,3,4,16,512]{4,3,2,1,0:T(8,128)(2,1)} %bitcast.32, bf16[128,128]{1,0:T(8,128)(2,1)} %slice.28.refs_2_, bf16[128,128]{1,0:T(8,128)(2,1)} %slice.29.refs_3_), custom_call_target="tpu_custom_call" | custom-call | bytes 4718592 | tf_op jit(solution)/shard_map/finished/pallas_call | solution.py:237
  516.3 4.9 collective-permute-done.27.source
  521.2 3.5 all-to-all-start.3
  524.7 2.0 collective-permute-start.28
  526.7 32.5 %all-to-all-done.3 = bf16[8,12,16,512]{3,2,1,0:T(8,128)(2,1)S(1)} async-done(((bf16[8,12,16,512]{3,2,1,0:T(8,128)(2,1)}), bf16[8,12,16,512]{3,2,1,0:T(8,128)(2,1)S(1)}, u32[]{:S(2)}, u32[]{:S(2)}) %all-to-all-start.3) | async-done | bytes 1572896 | tf_op jit(solution)/shard_map/all_to_all | solution.py:274
  559.2 1.1 copy-done.3
  560.4 9.5 %finished.6 = bf16[16,512,128]{2,1,0:T(8,128)(2,1)} custom-call(bf16[8,3,12,64,512]{4,3,2,1,0:T(8,128)(2,1)} %bitcast.11.refs_0_, bf16[8,3,4,16,512]{4,3,2,1,0:T(8,128)(2,1)} %bitcast.33, bf16[128,128]{1,0:T(8,128)(2,1)} %slice.28.refs_2_, bf16[128,128]{1,0:T(8,128)(2,1)} %slice.29.refs_3_), custom_call_target="tpu_custom_call" | custom-call | bytes 4718592 | tf_op jit(solution)/shard_map/finished/pallas_call | solution.py:237
  569.9 5.0 collective-permute-done.28.source
  574.9 3.5 all-to-all-start.4
  578.4 2.6 collective-permute-start.29
  581.0 32.5 %all-to-all-done.4 = bf16[8,12,16,512]{3,2,1,0:T(8,128)(2,1)S(1)} async-done(((bf16[8,12,16,512]{3,2,1,0:T(8,128)(2,1)}), bf16[8,12,16,512]{3,2,1,0:T(8,128)(2,1)S(1)}, u32[]{:S(2)}, u32[]{:S(2)}) %all-to-all-start.4) | async-done | bytes 1572896 | tf_op jit(solution)/shard_map/all_to_all | solution.py:274
  613.5 1.2 copy-done
  614.8 9.5 %finished.7 = bf16[16,512,128]{2,1,0:T(8,128)(2,1)} custom-call(bf16[8,3,12,64,512]{4,3,2,1,0:T(8,128)(2,1)} %bitcast.11.refs_0_, bf16[8,3,4,16,512]{4,3,2,1,0:T(8,128)(2,1)} %bitcast.30, bf16[128,128]{1,0:T(8,128)(2,1)} %slice.28.refs_2_, bf16[128,128]{1,0:T(8,128)(2,1)} %slice.29.refs_3_), custom_call_target="tpu_custom_call" | custom-call | bytes 4718592 | tf_op jit(solution)/shard_map/finished/pallas_call | solution.py:237
  624.3 4.3 collective-permute-done.29.source
  628.6 4.8 placed.4.refs_0_
  633.3 4.8 placed.5.refs_0_
  638.1 4.8 placed.6.refs_0_
  642.8 35.7 %collective-permute-done.30.source = bf16[16,512,128]{2,1,0:T(8,128)(2,1)S(1)} collective-permute-done((bf16[16,512,128]{2,1,0:T(8,128)(2,1)}, bf16[16,512,128]{2,1,0:T(8,128)(2,1)S(1)}, u32[]{:S(2)}, u32[]{:S(2)}) %collective-permute-start.30) | collective-permute-done | bytes 2097184 | tf_op jit(solution)/shard_map/ppermute | solution.py:364
  678.5 1.3 copy-done.4
  679.8 4.8 placed.7
  (126 shorter events, 8.2 us)
Async XLA Ops:
  6.5 103.2 %all-gather.2.cloned.1.call-start = ((), (), s32[]{:S(2)}) async-start(), calls=%async_computation.5 | async-start | bytes 15728640 | tf_op jit(solution)/shard_map/all_gather | solution.py:308
  7.7 17.9 %collective-permute-start = (bf16[144,128]{1,0:T(8,128)(2,1)S(1)}, bf16[144,128]{1,0:T(8,128)(2,1)S(1)}, u32[]{:S(2)}, u32[]{:S(2)}) collective-permute-start(bf16[144,128]{1,0:T(8,128)(2,1)S(1)} %pad_maximum_fusion), channel_id=1, source_target_pairs={{0,0},{1,1},{2,2},{3,3},{4,8},{5,9},{6,10},{7,11},{8,4},{9,5},{10,... | collective-permute-start | bytes 110600 | tf_op jit(solution)/shard_map/ppermute | solution.py:310
  13.4 12.3 %collective-permute-start.1 = (bf16[144,128]{1,0:T(8,128)(2,1)S(1)}, bf16[144,128]{1,0:T(8,128)(2,1)S(1)}, u32[]{:S(2)}, u32[]{:S(2)}) collective-permute-start(bf16[144,128]{1,0:T(8,128)(2,1)S(1)} %pad_maximum_fusion), channel_id=1, source_target_pairs={{8,0},{9,1},{10,2},{11,3},{12,8},{13,9},{14,10},{15,11},{16,4},{17... | collective-permute-start | bytes 110600 | tf_op jit(solution)/shard_map/ppermute | solution.py:310
  25.7 14.0 %collective-permute-start.2 = (bf16[6,64,512]{2,1,0:T(8,128)(2,1)}, bf16[6,64,512]{2,1,0:T(8,128)(2,1)S(1)}, u32[]{:S(2)}, u32[]{:S(2)}) collective-permute-start(bf16[6,64,512]{2,1,0:T(8,128)(2,1)} %get-tuple-element.88), channel_id=1, source_target_pairs={{0,0},{1,1},{2,2},{3,3},{4,8},{5,9},{6,10},{7,11},{8,4},{9,5},{10,... | collective-permute-start | bytes 1179656 | tf_op jit(solution)/shard_map/ppermute | solution.py:333
  27.6 20.8 %collective-permute-start.3 = (bf16[6,64,512]{2,1,0:T(8,128)(2,1)}, bf16[6,64,512]{2,1,0:T(8,128)(2,1)S(1)}, u32[]{:S(2)}, u32[]{:S(2)}) collective-permute-start(bf16[6,64,512]{2,1,0:T(8,128)(2,1)} %get-tuple-element.89), channel_id=1, source_target_pairs={{0,1},{1,0},{2,3},{3,2},{4,9},{5,8},{6,11},{7,10},{8,5},{9,4},{10,... | collective-permute-start | bytes 1179656 | tf_op jit(solution)/shard_map/ppermute | solution.py:333
  31.2 25.8 %collective-permute-start.4 = (bf16[6,64,512]{2,1,0:T(8,128)(2,1)}, bf16[6,64,512]{2,1,0:T(8,128)(2,1)S(1)}, u32[]{:S(2)}, u32[]{:S(2)}) collective-permute-start(bf16[6,64,512]{2,1,0:T(8,128)(2,1)} %get-tuple-element.90), channel_id=1, source_target_pairs={{0,2},{1,3},{2,0},{3,1},{4,10},{5,11},{6,8},{7,9},{8,6},{9,7},{10,... | collective-permute-start | bytes 1179656 | tf_op jit(solution)/shard_map/ppermute | solution.py:333
  32.2 30.6 %collective-permute-start.5 = (bf16[6,64,512]{2,1,0:T(8,128)(2,1)}, bf16[6,64,512]{2,1,0:T(8,128)(2,1)S(1)}, u32[]{:S(2)}, u32[]{:S(2)}) collective-permute-start(bf16[6,64,512]{2,1,0:T(8,128)(2,1)} %get-tuple-element.91), channel_id=1, source_target_pairs={{0,3},{1,2},{2,1},{3,0},{4,11},{5,10},{6,9},{7,8},{8,7},{9,6},{10,... | collective-permute-start | bytes 1179656 | tf_op jit(solution)/shard_map/ppermute | solution.py:333
  34.7 28.1 %collective-permute-start.6 = (bf16[6,64,512]{2,1,0:T(8,128)(2,1)}, bf16[6,64,512]{2,1,0:T(8,128)(2,1)S(1)}, u32[]{:S(2)}, u32[]{:S(2)}) collective-permute-start(bf16[6,64,512]{2,1,0:T(8,128)(2,1)} %get-tuple-element.92), channel_id=1, source_target_pairs={{0,8},{1,9},{2,10},{3,11},{4,0},{5,1},{6,2},{7,3},{8,12},{9,13},{1... | collective-permute-start | bytes 1179656 | tf_op jit(solution)/shard_map/ppermute | solution.py:333
  39.7 75.0 %copy-start.11 = (bf16[6,64,512]{2,1,0:T(8,128)(2,1)}, bf16[6,64,512]{2,1,0:T(8,128)(2,1)S(1)}, u32[]{:S(2)}) copy-start(bf16[6,64,512]{2,1,0:T(8,128)(2,1)S(1)} %collective-permute-done.2.refs_0_) | copy-start | bytes 1179652
  39.7 30.1 %collective-permute-start.7 = (bf16[6,64,512]{2,1,0:T(8,128)(2,1)}, bf16[6,64,512]{2,1,0:T(8,128)(2,1)S(1)}, u32[]{:S(2)}, u32[]{:S(2)}) collective-permute-start(bf16[6,64,512]{2,1,0:T(8,128)(2,1)} %get-tuple-element.93), channel_id=1, source_target_pairs={{0,9},{1,8},{2,11},{3,10},{4,1},{5,0},{6,3},{7,2},{8,13},{9,12},{1... | collective-permute-start | bytes 1179656 | tf_op jit(solution)/shard_map/ppermute | solution.py:333
  48.4 66.3 %copy-start.12 = (bf16[6,64,512]{2,1,0:T(8,128)(2,1)}, bf16[6,64,512]{2,1,0:T(8,128)(2,1)S(1)}, u32[]{:S(2)}) copy-start(bf16[6,64,512]{2,1,0:T(8,128)(2,1)S(1)} %collective-permute-done.3.refs_1_) | copy-start | bytes 1179652
  48.4 26.4 %collective-permute-start.8 = (bf16[6,64,512]{2,1,0:T(8,128)(2,1)}, bf16[6,64,512]{2,1,0:T(8,128)(2,1)S(1)}, u32[]{:S(2)}, u32[]{:S(2)}) collective-permute-start(bf16[6,64,512]{2,1,0:T(8,128)(2,1)} %get-tuple-element.94), channel_id=1, source_target_pairs={{0,10},{1,11},{2,8},{3,9},{4,2},{5,3},{6,0},{7,1},{8,14},{9,15},{1... | collective-permute-start | bytes 1179656 | tf_op jit(solution)/shard_map/ppermute | solution.py:333
  57.0 57.7 %copy-start.13 = (bf16[6,64,512]{2,1,0:T(8,128)(2,1)}, bf16[6,64,512]{2,1,0:T(8,128)(2,1)S(1)}, u32[]{:S(2)}) copy-start(bf16[6,64,512]{2,1,0:T(8,128)(2,1)S(1)} %collective-permute-done.4.refs_2_) | copy-start | bytes 1179652
  57.0 22.0 %collective-permute-start.9 = (bf16[6,64,512]{2,1,0:T(8,128)(2,1)}, bf16[6,64,512]{2,1,0:T(8,128)(2,1)S(1)}, u32[]{:S(2)}, u32[]{:S(2)}) collective-permute-start(bf16[6,64,512]{2,1,0:T(8,128)(2,1)} %get-tuple-element.95), channel_id=1, source_target_pairs={{0,11},{1,10},{2,9},{3,8},{4,3},{5,2},{6,1},{7,0},{8,15},{9,14},{1... | collective-permute-start | bytes 1179656 | tf_op jit(solution)/shard_map/ppermute | solution.py:333
  62.8 16.2 %copy-start.19 = (bf16[6,64,512]{2,1,0:T(8,128)(2,1)}, bf16[6,64,512]{2,1,0:T(8,128)(2,1)S(1)}, u32[]{:S(2)}) copy-start(bf16[6,64,512]{2,1,0:T(8,128)(2,1)S(1)} %collective-permute-done.5.refs_3_) | copy-start | bytes 1179652
  62.8 43.3 %copy-start.20 = (bf16[6,64,512]{2,1,0:T(8,128)(2,1)}, bf16[6,64,512]{2,1,0:T(8,128)(2,1)S(1)}, u32[]{:S(2)}) copy-start(bf16[6,64,512]{2,1,0:T(8,128)(2,1)S(1)} %collective-permute-done.6.refs_4_) | copy-start | bytes 1179652
  69.8 39.9 %copy-start.21 = (bf16[6,64,512]{2,1,0:T(8,128)(2,1)}, bf16[6,64,512]{2,1,0:T(8,128)(2,1)S(1)}, u32[]{:S(2)}) copy-start(bf16[6,64,512]{2,1,0:T(8,128)(2,1)S(1)} %collective-permute-done.7.refs_5_) | copy-start | bytes 1179652
  74.8 34.9 %copy-start.22 = (bf16[6,64,512]{2,1,0:T(8,128)(2,1)}, bf16[6,64,512]{2,1,0:T(8,128)(2,1)S(1)}, u32[]{:S(2)}) copy-start(bf16[6,64,512]{2,1,0:T(8,128)(2,1)S(1)} %collective-permute-done.8.refs_6_) | copy-start | bytes 1179652
  79.0 30.7 %copy-start.24 = (bf16[6,64,512]{2,1,0:T(8,128)(2,1)}, bf16[6,64,512]{2,1,0:T(8,128)(2,1)S(1)}, u32[]{:S(2)}) copy-start(bf16[6,64,512]{2,1,0:T(8,128)(2,1)S(1)} %collective-permute-done.9.refs_7_) | copy-start | bytes 1179652
  79.0 59.4 %collective-permute-start.10 = (bf16[6,64,512]{2,1,0:T(8,128)(2,1)}, bf16[6,64,512]{2,1,0:T(8,128)(2,1)S(1)}, u32[]{:S(2)}, u32[]{:S(2)}) collective-permute-start(bf16[6,64,512]{2,1,0:T(8,128)(2,1)} %get-tuple-element.96), channel_id=1, source_target_pairs={{0,0},{1,1},{2,2},{3,3},{4,8},{5,9},{6,10},{7,11},{8,4},{9,5},{10,... | collective-permute-start | bytes 1179656 | tf_op jit(solution)/shard_map/ppermute | solution.py:333
  104.1 36.2 %collective-permute-start.11 = (bf16[6,64,512]{2,1,0:T(8,128)(2,1)}, bf16[6,64,512]{2,1,0:T(8,128)(2,1)S(1)}, u32[]{:S(2)}, u32[]{:S(2)}) collective-permute-start(bf16[6,64,512]{2,1,0:T(8,128)(2,1)} %get-tuple-element.97), channel_id=1, source_target_pairs={{0,1},{1,0},{2,3},{3,2},{4,9},{5,8},{6,11},{7,10},{8,5},{9,4},{10,... | collective-permute-start | bytes 1179656 | tf_op jit(solution)/shard_map/ppermute | solution.py:333
  105.0 36.7 %collective-permute-start.12 = (bf16[6,64,512]{2,1,0:T(8,128)(2,1)}, bf16[6,64,512]{2,1,0:T(8,128)(2,1)S(1)}, u32[]{:S(2)}, u32[]{:S(2)}) collective-permute-start(bf16[6,64,512]{2,1,0:T(8,128)(2,1)} %get-tuple-element.98), channel_id=1, source_target_pairs={{0,2},{1,3},{2,0},{3,1},{4,10},{5,11},{6,8},{7,9},{8,6},{9,7},{10,... | collective-permute-start | bytes 1179656 | tf_op jit(solution)/shard_map/ppermute | solution.py:333
  106.1 60.5 %collective-permute-start.13 = (bf16[6,64,512]{2,1,0:T(8,128)(2,1)}, bf16[6,64,512]{2,1,0:T(8,128)(2,1)S(1)}, u32[]{:S(2)}, u32[]{:S(2)}) collective-permute-start(bf16[6,64,512]{2,1,0:T(8,128)(2,1)} %get-tuple-element.99), channel_id=1, source_target_pairs={{0,3},{1,2},{2,1},{3,0},{4,11},{5,10},{6,9},{7,8},{8,7},{9,6},{10,... | collective-permute-start | bytes 1179656 | tf_op jit(solution)/shard_map/ppermute | solution.py:333
  109.7 56.9 %collective-permute-start.14 = (bf16[6,64,512]{2,1,0:T(8,128)(2,1)}, bf16[6,64,512]{2,1,0:T(8,128)(2,1)S(1)}, u32[]{:S(2)}, u32[]{:S(2)}) collective-permute-start(bf16[6,64,512]{2,1,0:T(8,128)(2,1)} %get-tuple-element.100), channel_id=1, source_target_pairs={{0,8},{1,9},{2,10},{3,11},{4,0},{5,1},{6,2},{7,3},{8,12},{9,13},{1... | collective-permute-start | bytes 1179656 | tf_op jit(solution)/shard_map/ppermute | solution.py:333
  133.4 6.9 copy-start.9
  133.4 8.3 %copy-start.8 = (bf16[6,64,512]{2,1,0:T(8,128)(2,1)S(1)}, bf16[6,64,512]{2,1,0:T(8,128)(2,1)}, u32[]{:S(2)}) copy-start(bf16[6,64,512]{2,1,0:T(8,128)(2,1)} %get-tuple-element.103) | copy-start | bytes 1179652
  138.4 28.1 %copy-start.14 = (bf16[6,64,512]{2,1,0:T(8,128)(2,1)}, bf16[6,64,512]{2,1,0:T(8,128)(2,1)S(1)}, u32[]{:S(2)}) copy-start(bf16[6,64,512]{2,1,0:T(8,128)(2,1)S(1)} %collective-permute-done.10.refs_0_) | copy-start | bytes 1179652
  138.5 28.1 %collective-permute-start.15 = (bf16[6,64,512]{2,1,0:T(8,128)(2,1)S(1)}, bf16[6,64,512]{2,1,0:T(8,128)(2,1)S(1)}, u32[]{:S(2)}, u32[]{:S(2)}) collective-permute-start(bf16[6,64,512]{2,1,0:T(8,128)(2,1)S(1)} %copy-done.10), channel_id=1, source_target_pairs={{0,9},{1,8},{2,11},{3,10},{4,1},{5,0},{6,3},{7,2},{8,13},{9,12},{1... | collective-permute-start | bytes 1179656 | tf_op jit(solution)/shard_map/ppermute | solution.py:333
  140.3 26.3 %copy-start.15 = (bf16[6,64,512]{2,1,0:T(8,128)(2,1)}, bf16[6,64,512]{2,1,0:T(8,128)(2,1)S(1)}, u32[]{:S(2)}) copy-start(bf16[6,64,512]{2,1,0:T(8,128)(2,1)S(1)} %collective-permute-done.11.refs_1_) | copy-start | bytes 1179652
  140.3 26.3 %collective-permute-start.16 = (bf16[6,64,512]{2,1,0:T(8,128)(2,1)S(1)}, bf16[6,64,512]{2,1,0:T(8,128)(2,1)S(1)}, u32[]{:S(2)}, u32[]{:S(2)}) collective-permute-start(bf16[6,64,512]{2,1,0:T(8,128)(2,1)S(1)} %copy-done.9), channel_id=1, source_target_pairs={{0,10},{1,11},{2,8},{3,9},{4,2},{5,3},{6,0},{7,1},{8,14},{9,15},{1... | collective-permute-start | bytes 1179656 | tf_op jit(solution)/shard_map/ppermute | solution.py:333
  141.7 24.8 %copy-start.16 = (bf16[6,64,512]{2,1,0:T(8,128)(2,1)}, bf16[6,64,512]{2,1,0:T(8,128)(2,1)S(1)}, u32[]{:S(2)}) copy-start(bf16[6,64,512]{2,1,0:T(8,128)(2,1)S(1)} %collective-permute-done.12.refs_2_) | copy-start | bytes 1179652
  141.7 26.9 %collective-permute-start.17 = (bf16[6,64,512]{2,1,0:T(8,128)(2,1)S(1)}, bf16[6,64,512]{2,1,0:T(8,128)(2,1)S(1)}, u32[]{:S(2)}, u32[]{:S(2)}) collective-permute-start(bf16[6,64,512]{2,1,0:T(8,128)(2,1)S(1)} %copy-done.8), channel_id=1, source_target_pairs={{0,11},{1,10},{2,9},{3,8},{4,3},{5,2},{6,1},{7,0},{8,15},{9,14},{1... | collective-permute-start | bytes 1179656 | tf_op jit(solution)/shard_map/ppermute | solution.py:333
  143.7 31.2 %copy-start.32 = (bf16[4,64,512]{2,1,0:T(8,128)(2,1)S(1)}, bf16[4,64,512]{2,1,0:T(8,128)(2,1)}, u32[]{:S(2)}) copy-start(bf16[4,64,512]{2,1,0:T(8,128)(2,1)} %get-tuple-element.114) | copy-start | bytes 786436
  143.7 31.2 %copy-start.31 = (bf16[4,64,512]{2,1,0:T(8,128)(2,1)S(1)}, bf16[4,64,512]{2,1,0:T(8,128)(2,1)}, u32[]{:S(2)}) copy-start(bf16[4,64,512]{2,1,0:T(8,128)(2,1)} %get-tuple-element.115) | copy-start | bytes 786436
  143.7 34.9 %copy-start.30 = (bf16[4,64,512]{2,1,0:T(8,128)(2,1)S(1)}, bf16[4,64,512]{2,1,0:T(8,128)(2,1)}, u32[]{:S(2)}) copy-start(bf16[4,64,512]{2,1,0:T(8,128)(2,1)} %get-tuple-element.116) | copy-start | bytes 786436
  143.7 37.6 %copy-start.29 = (bf16[4,64,512]{2,1,0:T(8,128)(2,1)S(1)}, bf16[4,64,512]{2,1,0:T(8,128)(2,1)}, u32[]{:S(2)}) copy-start(bf16[4,64,512]{2,1,0:T(8,128)(2,1)} %get-tuple-element.117) | copy-start | bytes 786436
  143.7 44.0 %copy-start.28 = (bf16[4,64,512]{2,1,0:T(8,128)(2,1)S(1)}, bf16[4,64,512]{2,1,0:T(8,128)(2,1)}, u32[]{:S(2)}) copy-start(bf16[4,64,512]{2,1,0:T(8,128)(2,1)} %get-tuple-element.118) | copy-start | bytes 786436
  143.7 45.4 %copy-start.27 = (bf16[4,64,512]{2,1,0:T(8,128)(2,1)S(1)}, bf16[4,64,512]{2,1,0:T(8,128)(2,1)}, u32[]{:S(2)}) copy-start(bf16[4,64,512]{2,1,0:T(8,128)(2,1)} %get-tuple-element.119) | copy-start | bytes 786436
  166.6 22.8 %copy-start.17 = (bf16[6,64,512]{2,1,0:T(8,128)(2,1)}, bf16[6,64,512]{2,1,0:T(8,128)(2,1)S(1)}, u32[]{:S(2)}) copy-start(bf16[6,64,512]{2,1,0:T(8,128)(2,1)S(1)} %collective-permute-done.13.refs_3_) | copy-start | bytes 1179652
  166.6 22.8 %copy-start.18 = (bf16[6,64,512]{2,1,0:T(8,128)(2,1)}, bf16[6,64,512]{2,1,0:T(8,128)(2,1)S(1)}, u32[]{:S(2)}) copy-start(bf16[6,64,512]{2,1,0:T(8,128)(2,1)S(1)} %collective-permute-done.14.refs_4_) | copy-start | bytes 1179652
  166.6 22.7 %copy-start.23 = (bf16[6,64,512]{2,1,0:T(8,128)(2,1)}, bf16[6,64,512]{2,1,0:T(8,128)(2,1)S(1)}, u32[]{:S(2)}) copy-start(bf16[6,64,512]{2,1,0:T(8,128)(2,1)S(1)} %collective-permute-done.15.refs_5_) | copy-start | bytes 1179652
  166.6 22.7 %copy-start.25 = (bf16[6,64,512]{2,1,0:T(8,128)(2,1)}, bf16[6,64,512]{2,1,0:T(8,128)(2,1)S(1)}, u32[]{:S(2)}) copy-start(bf16[6,64,512]{2,1,0:T(8,128)(2,1)S(1)} %collective-permute-done.16.refs_6_) | copy-start | bytes 1179652
  168.7 20.7 %copy-start.26 = (bf16[6,64,512]{2,1,0:T(8,128)(2,1)}, bf16[6,64,512]{2,1,0:T(8,128)(2,1)S(1)}, u32[]{:S(2)}) copy-start(bf16[6,64,512]{2,1,0:T(8,128)(2,1)S(1)} %collective-permute-done.17.refs_7_) | copy-start | bytes 1179652
  168.7 12.7 %collective-permute-start.18 = (bf16[4,64,512]{2,1,0:T(8,128)(2,1)}, bf16[4,64,512]{2,1,0:T(8,128)(2,1)S(1)}, u32[]{:S(2)}, u32[]{:S(2)}) collective-permute-start(bf16[4,64,512]{2,1,0:T(8,128)(2,1)} %get-tuple-element.112), channel_id=1, source_target_pairs={{0,0},{1,1},{2,2},{3,3},{4,8},{5,9},{6,10},{7,11},{8,4},{9,5},{10,... | collective-permute-start | bytes 786440 | tf_op jit(solution)/shard_map/ppermute | solution.py:333
  174.1 13.6 %collective-permute-start.19 = (bf16[4,64,512]{2,1,0:T(8,128)(2,1)}, bf16[4,64,512]{2,1,0:T(8,128)(2,1)S(1)}, u32[]{:S(2)}, u32[]{:S(2)}) collective-permute-start(bf16[4,64,512]{2,1,0:T(8,128)(2,1)} %get-tuple-element.113), channel_id=1, source_target_pairs={{0,1},{1,0},{2,3},{3,2},{4,9},{5,8},{6,11},{7,10},{8,5},{9,4},{10,... | collective-permute-start | bytes 786440 | tf_op jit(solution)/shard_map/ppermute | solution.py:333
  174.9 14.2 %collective-permute-start.20 = (bf16[4,64,512]{2,1,0:T(8,128)(2,1)S(1)}, bf16[4,64,512]{2,1,0:T(8,128)(2,1)S(1)}, u32[]{:S(2)}, u32[]{:S(2)}) collective-permute-start(bf16[4,64,512]{2,1,0:T(8,128)(2,1)S(1)} %copy-done.32), channel_id=1, source_target_pairs={{0,2},{1,3},{2,0},{3,1},{4,10},{5,11},{6,8},{7,9},{8,6},{9,7},{10,... | collective-permute-start | bytes 786440 | tf_op jit(solution)/shard_map/ppermute | solution.py:333
  175.0 37.1 %collective-permute-start.21 = (bf16[4,64,512]{2,1,0:T(8,128)(2,1)S(1)}, bf16[4,64,512]{2,1,0:T(8,128)(2,1)S(1)}, u32[]{:S(2)}, u32[]{:S(2)}) collective-permute-start(bf16[4,64,512]{2,1,0:T(8,128)(2,1)S(1)} %copy-done.31), channel_id=1, source_target_pairs={{0,3},{1,2},{2,1},{3,0},{4,11},{5,10},{6,9},{7,8},{8,7},{9,6},{10,... | collective-permute-start | bytes 786440 | tf_op jit(solution)/shard_map/ppermute | solution.py:333
  178.7 33.5 %collective-permute-start.22 = (bf16[4,64,512]{2,1,0:T(8,128)(2,1)S(1)}, bf16[4,64,512]{2,1,0:T(8,128)(2,1)S(1)}, u32[]{:S(2)}, u32[]{:S(2)}) collective-permute-start(bf16[4,64,512]{2,1,0:T(8,128)(2,1)S(1)} %copy-done.30), channel_id=1, source_target_pairs={{0,8},{1,9},{2,10},{3,11},{4,0},{5,1},{6,2},{7,3},{8,12},{9,13},{1... | collective-permute-start | bytes 786440 | tf_op jit(solution)/shard_map/ppermute | solution.py:333
  181.4 30.7 %copy-start.33 = (bf16[4,64,512]{2,1,0:T(8,128)(2,1)}, bf16[4,64,512]{2,1,0:T(8,128)(2,1)S(1)}, u32[]{:S(2)}) copy-start(bf16[4,64,512]{2,1,0:T(8,128)(2,1)S(1)} %collective-permute-done.18.refs_0_) | copy-start | bytes 786436
  181.4 30.8 %collective-permute-start.23 = (bf16[4,64,512]{2,1,0:T(8,128)(2,1)S(1)}, bf16[4,64,512]{2,1,0:T(8,128)(2,1)S(1)}, u32[]{:S(2)}, u32[]{:S(2)}) collective-permute-start(bf16[4,64,512]{2,1,0:T(8,128)(2,1)S(1)} %copy-done.29), channel_id=1, source_target_pairs={{0,9},{1,8},{2,11},{3,10},{4,1},{5,0},{6,3},{7,2},{8,13},{9,12},{1... | collective-permute-start | bytes 786440 | tf_op jit(solution)/shard_map/ppermute | solution.py:333
  187.7 24.3 %copy-start.34 = (bf16[4,64,512]{2,1,0:T(8,128)(2,1)}, bf16[4,64,512]{2,1,0:T(8,128)(2,1)S(1)}, u32[]{:S(2)}) copy-start(bf16[4,64,512]{2,1,0:T(8,128)(2,1)S(1)} %collective-permute-done.19.refs_1_) | copy-start | bytes 786436
  187.7 24.4 %collective-permute-start.24 = (bf16[4,64,512]{2,1,0:T(8,128)(2,1)S(1)}, bf16[4,64,512]{2,1,0:T(8,128)(2,1)S(1)}, u32[]{:S(2)}, u32[]{:S(2)}) collective-permute-start(bf16[4,64,512]{2,1,0:T(8,128)(2,1)S(1)} %copy-done.28), channel_id=1, source_target_pairs={{0,10},{1,11},{2,8},{3,9},{4,2},{5,3},{6,0},{7,1},{8,14},{9,15},{1... | collective-permute-start | bytes 786440 | tf_op jit(solution)/shard_map/ppermute | solution.py:333
  189.1 22.9 %copy-start.35 = (bf16[4,64,512]{2,1,0:T(8,128)(2,1)}, bf16[4,64,512]{2,1,0:T(8,128)(2,1)S(1)}, u32[]{:S(2)}) copy-start(bf16[4,64,512]{2,1,0:T(8,128)(2,1)S(1)} %collective-permute-done.20.refs_2_) | copy-start | bytes 786436
  189.2 23.0 %collective-permute-start.25 = (bf16[4,64,512]{2,1,0:T(8,128)(2,1)S(1)}, bf16[4,64,512]{2,1,0:T(8,128)(2,1)S(1)}, u32[]{:S(2)}, u32[]{:S(2)}) collective-permute-start(bf16[4,64,512]{2,1,0:T(8,128)(2,1)S(1)} %copy-done.27), channel_id=1, source_target_pairs={{0,11},{1,10},{2,9},{3,8},{4,3},{5,2},{6,1},{7,0},{8,15},{9,14},{1... | collective-permute-start | bytes 786440 | tf_op jit(solution)/shard_map/ppermute | solution.py:333
  213.7 218.9 %all-to-all-start = ((bf16[8,36,64,512]{3,2,1,0:T(8,128)(2,1)}), bf16[8,36,64,512]{3,2,1,0:T(8,128)(2,1)}, u32[]{:S(2)}, u32[]{:S(2)}) async-start(bf16[8,36,64,512]{3,2,1,0:T(8,128)(2,1)} %bitcast.29), calls=%async_computation | async-start | bytes 37748736 | tf_op jit(solution)/shard_map/all_to_all | solution.py:274
  236.0 196.6 %collective-permute-start.26 = (bf16[64,512,128]{2,1,0:T(8,128)(2,1)}, bf16[64,512,128]{2,1,0:T(8,128)(2,1)}, u32[]{:S(2)}, u32[]{:S(2)}) collective-permute-start(bf16[64,512,128]{2,1,0:T(8,128)(2,1)} %bitcast_convert_fusion), channel_id=1, source_target_pairs={{0,16},{1,17},{2,18},{3,19},{4,20},{5,21},{6,22},{7,23},{8,24},{9,... | collective-permute-start | bytes 25165832 | tf_op jit(solution)/shard_map/ppermute | solution.py:351
  432.7 24.0 %all-to-all-start.1 = ((bf16[8,12,16,512]{3,2,1,0:T(8,128)(2,1)}), bf16[8,12,16,512]{3,2,1,0:T(8,128)(2,1)S(1)}, u32[]{:S(2)}, u32[]{:S(2)}) async-start(bf16[8,12,16,512]{3,2,1,0:T(8,128)(2,1)} %bitcast.34), calls=%async_computation.1 | async-start | bytes 3145728 | tf_op jit(solution)/shard_map/all_to_all | solution.py:274
  467.3 38.2 %all-to-all-start.2 = ((bf16[8,12,16,512]{3,2,1,0:T(8,128)(2,1)}), bf16[8,12,16,512]{3,2,1,0:T(8,128)(2,1)S(1)}, u32[]{:S(2)}, u32[]{:S(2)}) async-start(bf16[8,12,16,512]{3,2,1,0:T(8,128)(2,1)} %bitcast.14), calls=%async_computation.2 | async-start | bytes 3145728 | tf_op jit(solution)/shard_map/all_to_all | solution.py:274
  471.0 50.2 %collective-permute-start.27 = (bf16[16,512,128]{2,1,0:T(8,128)(2,1)}, bf16[16,512,128]{2,1,0:T(8,128)(2,1)}, u32[]{:S(2)}, u32[]{:S(2)}) collective-permute-start(bf16[16,512,128]{2,1,0:T(8,128)(2,1)} %finished.4), channel_id=1, source_target_pairs={{0,16},{1,17},{2,18},{3,19},{8,20},{9,21},{10,22},{11,23},{4,24},{... | collective-permute-start | bytes 6291464 | tf_op jit(solution)/shard_map/ppermute | solution.py:364
  521.2 38.0 %all-to-all-start.3 = ((bf16[8,12,16,512]{3,2,1,0:T(8,128)(2,1)}), bf16[8,12,16,512]{3,2,1,0:T(8,128)(2,1)S(1)}, u32[]{:S(2)}, u32[]{:S(2)}) async-start(bf16[8,12,16,512]{3,2,1,0:T(8,128)(2,1)} %bitcast.13), calls=%async_computation.3 | async-start | bytes 3145728 | tf_op jit(solution)/shard_map/all_to_all | solution.py:274
  524.7 50.2 %collective-permute-start.28 = (bf16[16,512,128]{2,1,0:T(8,128)(2,1)}, bf16[16,512,128]{2,1,0:T(8,128)(2,1)}, u32[]{:S(2)}, u32[]{:S(2)}) collective-permute-start(bf16[16,512,128]{2,1,0:T(8,128)(2,1)} %finished.5), channel_id=1, source_target_pairs={{0,16},{1,17},{2,18},{3,19},{8,20},{9,21},{10,22},{11,23},{4,24},{... | collective-permute-start | bytes 6291464 | tf_op jit(solution)/shard_map/ppermute | solution.py:364
  574.9 38.6 %all-to-all-start.4 = ((bf16[8,12,16,512]{3,2,1,0:T(8,128)(2,1)}), bf16[8,12,16,512]{3,2,1,0:T(8,128)(2,1)S(1)}, u32[]{:S(2)}, u32[]{:S(2)}) async-start(bf16[8,12,16,512]{3,2,1,0:T(8,128)(2,1)} %bitcast.12), calls=%async_computation.4 | async-start | bytes 3145728 | tf_op jit(solution)/shard_map/all_to_all | solution.py:274
  578.4 50.2 %collective-permute-start.29 = (bf16[16,512,128]{2,1,0:T(8,128)(2,1)}, bf16[16,512,128]{2,1,0:T(8,128)(2,1)}, u32[]{:S(2)}, u32[]{:S(2)}) collective-permute-start(bf16[16,512,128]{2,1,0:T(8,128)(2,1)} %finished.6), channel_id=1, source_target_pairs={{0,16},{1,17},{2,18},{3,19},{8,20},{9,21},{10,22},{11,23},{4,24},{... | collective-permute-start | bytes 6291464 | tf_op jit(solution)/shard_map/ppermute | solution.py:364
  628.6 49.9 %collective-permute-start.30 = (bf16[16,512,128]{2,1,0:T(8,128)(2,1)}, bf16[16,512,128]{2,1,0:T(8,128)(2,1)S(1)}, u32[]{:S(2)}, u32[]{:S(2)}) collective-permute-start(bf16[16,512,128]{2,1,0:T(8,128)(2,1)} %finished.7), channel_id=1, source_target_pairs={{0,16},{1,17},{2,18},{3,19},{8,20},{9,21},{10,22},{11,23},{4,24},{... | collective-permute-start | bytes 6291464 | tf_op jit(solution)/shard_map/ppermute | solution.py:364
  (14 other events, 17.9 us)
Sparse Core Ops, SparseCore 0:
  8.9 84.6 all-gather.1

commit v7 on v6

--- a/solution.py
+++ b/solution.py
@@ -250,7 +250,7 @@
 
 def placed(rows_in, old, target, row_chunk, shape):
     rows, width, channels = rows_in.shape
-    piece = min(width, 128)
+    piece = min(width, PIECE)
 
     def body(source, before, *refs):
         refs[-1][...] = before[...].astype(jnp.float32) + source[...].astype(jnp.float32)

time: 693 us -> 692 us (level)
  transfers between devices with their start and end apart: 37 -> 37, of which waited for: 20 -> 20; matrix products, arithmetic and copies ran while one was open for 2% -> 2% of each run, Pallas kernels for 24% -> 23%
where the time goes in v7:
time: 692 us; the launch traced here: 690 us
  waiting for transfers between devices  389 us (56%)
  Pallas kernels  173 us (25%)
  starting transfers between devices  95.2 us (14%)
  between operations  13.8 us (2%)
  other arithmetic  10.4 us (2%)
  local copies, waits for them, and re-layouts  9.09 us (1%)
    all_to_all x5, waiting for transfers between devices, exchanged(): lax.all_to_all(values, GROUP, split_axis=0, concat_axis=0, tiled=True)  278 us
    pallas_call x3, Pallas kernels, relayed(): pl.pallas_call(body, grid_spec=pltpu.PrefetchScalarGridSpec(num_scalar_pr...  79.3 us
    ppermute x24, waiting for transfers between devices, delivered(): lax.ppermute(piece, AXES, route)  56.7 us
    ppermute x24, starting transfers between devices, delivered(): lax.ppermute(piece, AXES, route)  54.1 us
    ppermute x4, waiting for transfers between devices, on_device(): lax.ppermute(tied(rows, moved[-1]) if ending else rows, AXES, return_route)  52.7 us
    pallas_call x4, Pallas kernels, finished(): pl.pallas_call(body, grid=(width // piece,), in_specs=[term_block(a, row_...  38.1 us
    pallas_call x6, Pallas kernels, dense(): pl.pallas_call(body, grid_spec=pltpu.PrefetchScalarGridSpec(num_scalar_pr...  28.7 us
    all_to_all x5, starting transfers between devices, exchanged(): lax.all_to_all(values, GROUP, split_axis=0, concat_axis=0, tiled=True)  27.7 us
  transfers between devices with their start and end apart: 37, of which 20 were waited for; matrix products, arithmetic and copies ran while one was open for 2% of the time, Pallas kernels for 23%

profile of v7, /device:TPU:1, one launch (start us, length us, event | category | flops | bytes accessed | tf_op | source)
XLA Modules:
  0.0 690.4 jit_solution(17579240369580312440)
XLA Ops:
  7.7 5.6 collective-permute-start
  13.4 12.2 %spread.1 = (bf16[6,64,512]{2,1,0:T(8,128)(2,1)}, bf16[6,64,512]{2,1,0:T(8,128)(2,1)}, bf16[6,64,512]{2,1,0:T(8,128)(2,1)}, bf16[6,64,512]{2,1,0:T(8,128)(2,1)},...) custom-call(s32[1]{0:T(128)} %bitcast.1.band_ref, ...), custom_call_target="tpu_custom_call" | custom-call | bytes 33554432 | tf_op jit(solution)/shard_map/spread/pallas_call | solution.py:53
  25.7 1.9 collective-permute-start.2
  27.6 3.6 collective-permute-start.3
  32.2 2.6 collective-permute-start.5
  34.7 5.0 collective-permute-done.2.refs_0_
  39.7 8.7 %collective-permute-done.3.refs_1_ = bf16[6,64,512]{2,1,0:T(8,128)(2,1)S(1)} collective-permute-done((bf16[6,64,512]{2,1,0:T(8,128)(2,1)}, bf16[6,64,512]{2,1,0:T(8,128)(2,1)S(1)}, u32[]{:S(2)}, u32[]{:S(2)}) %collective-permute-start.3) | collective-permute-done | bytes 393248 | tf_op jit(solution)/shard_map/ppermute | solution.py:333
  48.4 8.6 %collective-permute-done.4.refs_2_ = bf16[6,64,512]{2,1,0:T(8,128)(2,1)S(1)} collective-permute-done((bf16[6,64,512]{2,1,0:T(8,128)(2,1)}, bf16[6,64,512]{2,1,0:T(8,128)(2,1)S(1)}, u32[]{:S(2)}, u32[]{:S(2)}) %collective-permute-start.4) | collective-permute-done | bytes 393248 | tf_op jit(solution)/shard_map/ppermute | solution.py:333
  57.0 5.8 collective-permute-done.5.refs_3_
  62.8 7.0 %collective-permute-done.7.refs_5_ = bf16[6,64,512]{2,1,0:T(8,128)(2,1)S(1)} collective-permute-done((bf16[6,64,512]{2,1,0:T(8,128)(2,1)}, bf16[6,64,512]{2,1,0:T(8,128)(2,1)S(1)}, u32[]{:S(2)}, u32[]{:S(2)}) %collective-permute-start.7) | collective-permute-done | bytes 393248 | tf_op jit(solution)/shard_map/ppermute | solution.py:333
  69.8 5.0 collective-permute-done.8.refs_6_
  74.8 4.2 collective-permute-done.9.refs_7_
  79.0 25.0 %collective-permute-start.10 = (bf16[6,64,512]{2,1,0:T(8,128)(2,1)}, bf16[6,64,512]{2,1,0:T(8,128)(2,1)S(1)}, u32[]{:S(2)}, u32[]{:S(2)}) collective-permute-start(bf16[6,64,512]{2,1,0:T(8,128)(2,1)} %get-tuple-element.96), channel_id=1, source_target_pairs={{0,0},{1,1},{2,2},{3,3},{4,8},{5,9},{6,10},{7,11},{8,4},{9,5},{10,... | collective-permute-start | bytes 1179656 | tf_op jit(solution)/shard_map/ppermute | solution.py:333
  106.1 3.6 collective-permute-start.13
  109.8 4.9 dense.6.refs_8_
  114.7 4.5 dense.7.refs_9_
  119.2 4.9 dense.8.refs_10_
  124.1 4.9 dense.9.refs_11_
  129.0 4.4 dense.10.refs_12_
  133.4 5.0 dense.11.refs_13_
  138.5 1.8 collective-permute-start.15
  140.3 1.4 collective-permute-start.16
  141.7 2.0 collective-permute-start.17
  143.8 22.8 %relayed.3.refs_14_ = bf16[8,3,12,64,512]{4,3,2,1,0:T(8,128)(2,1)} custom-call(s32[1]{0:T(128)} %bitcast.member_ref, bf16[6,64,512]{2,1,0:T(8,128)(2,1)} %copy-done.11, bf16[6,64,512]{2,1,0:T(8,128)(2,1)} %copy-done.12, bf16[6,64,512]{2,1,0:T(8,128)(2,1)} %copy-done.13, bf16[6,64,512]{2,1,0:T(8,128)(2,1)} %copy-done.19, bf16[6,64,512]{2,1,0:T(8,128)(2,1)} %copy-done.20, ...), custom_call_target="tpu_custom_call" | custom-call | flops 28991029248 | bytes 25165824 | tf_op jit(solution)/shard_map/relayed/pallas_call | solution.py:188
  166.6 2.0 collective-permute-done.17.refs_7_
  168.7 5.5 collective-permute-start.18
  175.0 3.7 collective-permute-start.21
  178.7 2.7 collective-permute-done.18.refs_0_
  181.4 6.4 collective-permute-done.19.refs_1_
  187.7 1.4 collective-permute-done.20.refs_2_
  189.4 22.7 %relayed.4 = bf16[8,3,12,64,512]{4,3,2,1,0:T(8,128)(2,1)} custom-call(s32[1]{0:T(128)} %bitcast.member_ref, bf16[6,64,512]{2,1,0:T(8,128)(2,1)} %copy-done.14, bf16[6,64,512]{2,1,0:T(8,128)(2,1)} %copy-done.15, bf16[6,64,512]{2,1,0:T(8,128)(2,1)} %copy-done.16, bf16[6,64,512]{2,1,0:T(8,128)(2,1)} %copy-done.17, ...), custom_call_target="tpu_custom_call", output_to_operand_aliasing={{}: (15, {})} | custom-call | flops 28991029248 | bytes 25165824 | tf_op jit(solution)/shard_map/relayed/pallas_call | solution.py:188
  213.7 13.1 %all-to-all-start = ((bf16[8,36,64,512]{3,2,1,0:T(8,128)(2,1)}), bf16[8,36,64,512]{3,2,1,0:T(8,128)(2,1)}, u32[]{:S(2)}, u32[]{:S(2)}) async-start(bf16[8,36,64,512]{3,2,1,0:T(8,128)(2,1)} %bitcast.29), calls=%async_computation | async-start | bytes 37748736 | tf_op jit(solution)/shard_map/all_to_all | solution.py:274
  226.9 9.2 %bitcast_convert_fusion = bf16[64,512,128]{2,1,0:T(8,128)(2,1)} fusion(f32[1,64,512,128]{3,2,1,0:T(8,128)} %param.5), kind=kLoop, calls=%fused_computation.14 | loop fusion | flops 4194304 | bytes 25165824 | tf_op jit(solution)/shard_map/convert_element_type | solution.py:351
  236.0 1.4 collective-permute-start.26
  237.4 33.8 %relayed.5 = (bf16[8,3,4,16,512]{4,3,2,1,0:T(8,128)(2,1)}, bf16[8,3,4,16,512]{4,3,2,1,0:T(8,128)(2,1)}, bf16[8,3,4,16,512]{4,3,2,1,0:T(8,128)(2,1)}, bf16[8,3,4,16,512]{4,3,2,1,0:T(8,128)(2,1)}) custom-call(s32[1]{0:T(128)} %bitcast.member_ref, bf16[4,64,512]{2,1,0:T(8,128)(2,1)} %copy-done.33, bf16[4,64,512]{2,1,0:T(8,128)(2,1)} %copy-done.34, ...), custom_call_target="tpu_custom_call" | custom-call | flops 19327352832 | bytes 20971520 | tf_op jit(solution)/shard_map/relayed/pallas_call | solution.py:188
  271.2 161.5 %all-to-all-done = bf16[8,36,64,512]{3,2,1,0:T(8,128)(2,1)} async-done(((bf16[8,36,64,512]{3,2,1,0:T(8,128)(2,1)}), bf16[8,36,64,512]{3,2,1,0:T(8,128)(2,1)}, u32[]{:S(2)}, u32[]{:S(2)}) %all-to-all-start) | async-done | bytes 18874400 | tf_op jit(solution)/shard_map/all_to_all | solution.py:274
  432.7 3.7 all-to-all-start.1
  437.6 19.1 %all-to-all-done.1 = bf16[8,12,16,512]{3,2,1,0:T(8,128)(2,1)S(1)} async-done(((bf16[8,12,16,512]{3,2,1,0:T(8,128)(2,1)}), bf16[8,12,16,512]{3,2,1,0:T(8,128)(2,1)S(1)}, u32[]{:S(2)}, u32[]{:S(2)}) %all-to-all-start.1) | async-done | bytes 1572896 | tf_op jit(solution)/shard_map/all_to_all | solution.py:274
  456.7 1.1 copy-done.1
  457.8 9.5 %finished.4 = bf16[16,512,128]{2,1,0:T(8,128)(2,1)} custom-call(bf16[8,3,12,64,512]{4,3,2,1,0:T(8,128)(2,1)} %bitcast.11.refs_0_, bf16[8,3,4,16,512]{4,3,2,1,0:T(8,128)(2,1)} %bitcast.31, bf16[128,128]{1,0:T(8,128)(2,1)} %slice.28.refs_2_, bf16[128,128]{1,0:T(8,128)(2,1)} %slice.29.refs_3_), custom_call_target="tpu_custom_call" | custom-call | bytes 4718592 | tf_op jit(solution)/shard_map/finished/pallas_call | solution.py:237
  467.3 3.8 all-to-all-start.2
  471.1 1.8 collective-permute-start.27
  472.8 32.8 %all-to-all-done.2 = bf16[8,12,16,512]{3,2,1,0:T(8,128)(2,1)S(1)} async-done(((bf16[8,12,16,512]{3,2,1,0:T(8,128)(2,1)}), bf16[8,12,16,512]{3,2,1,0:T(8,128)(2,1)S(1)}, u32[]{:S(2)}, u32[]{:S(2)}) %all-to-all-start.2) | async-done | bytes 1572896 | tf_op jit(solution)/shard_map/all_to_all | solution.py:274
  505.6 1.2 copy-done.2
  506.7 9.6 %finished.5 = bf16[16,512,128]{2,1,0:T(8,128)(2,1)} custom-call(bf16[8,3,12,64,512]{4,3,2,1,0:T(8,128)(2,1)} %bitcast.11.refs_0_, bf16[8,3,4,16,512]{4,3,2,1,0:T(8,128)(2,1)} %bitcast.32, bf16[128,128]{1,0:T(8,128)(2,1)} %slice.28.refs_2_, bf16[128,128]{1,0:T(8,128)(2,1)} %slice.29.refs_3_), custom_call_target="tpu_custom_call" | custom-call | bytes 4718592 | tf_op jit(solution)/shard_map/finished/pallas_call | solution.py:237
  516.3 4.9 collective-permute-done.27.source
  521.2 3.5 all-to-all-start.3
  524.8 2.0 collective-permute-start.28
  526.7 32.6 %all-to-all-done.3 = bf16[8,12,16,512]{3,2,1,0:T(8,128)(2,1)S(1)} async-done(((bf16[8,12,16,512]{3,2,1,0:T(8,128)(2,1)}), bf16[8,12,16,512]{3,2,1,0:T(8,128)(2,1)S(1)}, u32[]{:S(2)}, u32[]{:S(2)}) %all-to-all-start.3) | async-done | bytes 1572896 | tf_op jit(solution)/shard_map/all_to_all | solution.py:274
  559.3 1.1 copy-done.3
  560.5 9.5 %finished.6 = bf16[16,512,128]{2,1,0:T(8,128)(2,1)} custom-call(bf16[8,3,12,64,512]{4,3,2,1,0:T(8,128)(2,1)} %bitcast.11.refs_0_, bf16[8,3,4,16,512]{4,3,2,1,0:T(8,128)(2,1)} %bitcast.33, bf16[128,128]{1,0:T(8,128)(2,1)} %slice.28.refs_2_, bf16[128,128]{1,0:T(8,128)(2,1)} %slice.29.refs_3_), custom_call_target="tpu_custom_call" | custom-call | bytes 4718592 | tf_op jit(solution)/shard_map/finished/pallas_call | solution.py:237
  570.0 5.0 collective-permute-done.28.source
  574.9 3.5 all-to-all-start.4
  578.4 2.6 collective-permute-start.29
  581.0 32.6 %all-to-all-done.4 = bf16[8,12,16,512]{3,2,1,0:T(8,128)(2,1)S(1)} async-done(((bf16[8,12,16,512]{3,2,1,0:T(8,128)(2,1)}), bf16[8,12,16,512]{3,2,1,0:T(8,128)(2,1)S(1)}, u32[]{:S(2)}, u32[]{:S(2)}) %all-to-all-start.4) | async-done | bytes 1572896 | tf_op jit(solution)/shard_map/all_to_all | solution.py:274
  613.6 1.2 copy-done
  614.8 9.5 %finished.7 = bf16[16,512,128]{2,1,0:T(8,128)(2,1)} custom-call(bf16[8,3,12,64,512]{4,3,2,1,0:T(8,128)(2,1)} %bitcast.11.refs_0_, bf16[8,3,4,16,512]{4,3,2,1,0:T(8,128)(2,1)} %bitcast.30, bf16[128,128]{1,0:T(8,128)(2,1)} %slice.28.refs_2_, bf16[128,128]{1,0:T(8,128)(2,1)} %slice.29.refs_3_), custom_call_target="tpu_custom_call" | custom-call | bytes 4718592 | tf_op jit(solution)/shard_map/finished/pallas_call | solution.py:237
  624.4 4.2 collective-permute-done.29.source
  628.6 3.8 placed.4.refs_0_
  632.4 3.8 placed.5.refs_0_
  636.1 3.8 placed.6.refs_0_
  639.9 38.7 %collective-permute-done.30.source = bf16[16,512,128]{2,1,0:T(8,128)(2,1)S(1)} collective-permute-done((bf16[16,512,128]{2,1,0:T(8,128)(2,1)}, bf16[16,512,128]{2,1,0:T(8,128)(2,1)S(1)}, u32[]{:S(2)}, u32[]{:S(2)}) %collective-permute-start.30) | collective-permute-done | bytes 2097184 | tf_op jit(solution)/shard_map/ppermute | solution.py:364
  678.5 1.3 copy-done.4
  679.8 3.8 placed.7
  (126 shorter events, 8.2 us)
Async XLA Ops:
  6.5 103.2 %all-gather.2.cloned.1.call-start = ((), (), s32[]{:S(2)}) async-start(), calls=%async_computation.5 | async-start | bytes 15728640 | tf_op jit(solution)/shard_map/all_gather | solution.py:308
  7.7 17.9 %collective-permute-start = (bf16[144,128]{1,0:T(8,128)(2,1)S(1)}, bf16[144,128]{1,0:T(8,128)(2,1)S(1)}, u32[]{:S(2)}, u32[]{:S(2)}) collective-permute-start(bf16[144,128]{1,0:T(8,128)(2,1)S(1)} %pad_maximum_fusion), channel_id=1, source_target_pairs={{0,0},{1,1},{2,2},{3,3},{4,8},{5,9},{6,10},{7,11},{8,4},{9,5},{10,... | collective-permute-start | bytes 110600 | tf_op jit(solution)/shard_map/ppermute | solution.py:310
  13.4 12.3 %collective-permute-start.1 = (bf16[144,128]{1,0:T(8,128)(2,1)S(1)}, bf16[144,128]{1,0:T(8,128)(2,1)S(1)}, u32[]{:S(2)}, u32[]{:S(2)}) collective-permute-start(bf16[144,128]{1,0:T(8,128)(2,1)S(1)} %pad_maximum_fusion), channel_id=1, source_target_pairs={{8,0},{9,1},{10,2},{11,3},{12,8},{13,9},{14,10},{15,11},{16,4},{17... | collective-permute-start | bytes 110600 | tf_op jit(solution)/shard_map/ppermute | solution.py:310
  25.7 14.0 %collective-permute-start.2 = (bf16[6,64,512]{2,1,0:T(8,128)(2,1)}, bf16[6,64,512]{2,1,0:T(8,128)(2,1)S(1)}, u32[]{:S(2)}, u32[]{:S(2)}) collective-permute-start(bf16[6,64,512]{2,1,0:T(8,128)(2,1)} %get-tuple-element.88), channel_id=1, source_target_pairs={{0,0},{1,1},{2,2},{3,3},{4,8},{5,9},{6,10},{7,11},{8,4},{9,5},{10,... | collective-permute-start | bytes 1179656 | tf_op jit(solution)/shard_map/ppermute | solution.py:333
  27.6 20.8 %collective-permute-start.3 = (bf16[6,64,512]{2,1,0:T(8,128)(2,1)}, bf16[6,64,512]{2,1,0:T(8,128)(2,1)S(1)}, u32[]{:S(2)}, u32[]{:S(2)}) collective-permute-start(bf16[6,64,512]{2,1,0:T(8,128)(2,1)} %get-tuple-element.89), channel_id=1, source_target_pairs={{0,1},{1,0},{2,3},{3,2},{4,9},{5,8},{6,11},{7,10},{8,5},{9,4},{10,... | collective-permute-start | bytes 1179656 | tf_op jit(solution)/shard_map/ppermute | solution.py:333
  31.2 25.8 %collective-permute-start.4 = (bf16[6,64,512]{2,1,0:T(8,128)(2,1)}, bf16[6,64,512]{2,1,0:T(8,128)(2,1)S(1)}, u32[]{:S(2)}, u32[]{:S(2)}) collective-permute-start(bf16[6,64,512]{2,1,0:T(8,128)(2,1)} %get-tuple-element.90), channel_id=1, source_target_pairs={{0,2},{1,3},{2,0},{3,1},{4,10},{5,11},{6,8},{7,9},{8,6},{9,7},{10,... | collective-permute-start | bytes 1179656 | tf_op jit(solution)/shard_map/ppermute | solution.py:333
  32.2 30.6 %collective-permute-start.5 = (bf16[6,64,512]{2,1,0:T(8,128)(2,1)}, bf16[6,64,512]{2,1,0:T(8,128)(2,1)S(1)}, u32[]{:S(2)}, u32[]{:S(2)}) collective-permute-start(bf16[6,64,512]{2,1,0:T(8,128)(2,1)} %get-tuple-element.91), channel_id=1, source_target_pairs={{0,3},{1,2},{2,1},{3,0},{4,11},{5,10},{6,9},{7,8},{8,7},{9,6},{10,... | collective-permute-start | bytes 1179656 | tf_op jit(solution)/shard_map/ppermute | solution.py:333
  34.7 28.1 %collective-permute-start.6 = (bf16[6,64,512]{2,1,0:T(8,128)(2,1)}, bf16[6,64,512]{2,1,0:T(8,128)(2,1)S(1)}, u32[]{:S(2)}, u32[]{:S(2)}) collective-permute-start(bf16[6,64,512]{2,1,0:T(8,128)(2,1)} %get-tuple-element.92), channel_id=1, source_target_pairs={{0,8},{1,9},{2,10},{3,11},{4,0},{5,1},{6,2},{7,3},{8,12},{9,13},{1... | collective-permute-start | bytes 1179656 | tf_op jit(solution)/shard_map/ppermute | solution.py:333
  39.7 75.0 %copy-start.11 = (bf16[6,64,512]{2,1,0:T(8,128)(2,1)}, bf16[6,64,512]{2,1,0:T(8,128)(2,1)S(1)}, u32[]{:S(2)}) copy-start(bf16[6,64,512]{2,1,0:T(8,128)(2,1)S(1)} %collective-permute-done.2.refs_0_) | copy-start | bytes 1179652
  39.7 30.1 %collective-permute-start.7 = (bf16[6,64,512]{2,1,0:T(8,128)(2,1)}, bf16[6,64,512]{2,1,0:T(8,128)(2,1)S(1)}, u32[]{:S(2)}, u32[]{:S(2)}) collective-permute-start(bf16[6,64,512]{2,1,0:T(8,128)(2,1)} %get-tuple-element.93), channel_id=1, source_target_pairs={{0,9},{1,8},{2,11},{3,10},{4,1},{5,0},{6,3},{7,2},{8,13},{9,12},{1... | collective-permute-start | bytes 1179656 | tf_op jit(solution)/shard_map/ppermute | solution.py:333
  48.4 66.3 %copy-start.12 = (bf16[6,64,512]{2,1,0:T(8,128)(2,1)}, bf16[6,64,512]{2,1,0:T(8,128)(2,1)S(1)}, u32[]{:S(2)}) copy-start(bf16[6,64,512]{2,1,0:T(8,128)(2,1)S(1)} %collective-permute-done.3.refs_1_) | copy-start | bytes 1179652
  48.4 26.4 %collective-permute-start.8 = (bf16[6,64,512]{2,1,0:T(8,128)(2,1)}, bf16[6,64,512]{2,1,0:T(8,128)(2,1)S(1)}, u32[]{:S(2)}, u32[]{:S(2)}) collective-permute-start(bf16[6,64,512]{2,1,0:T(8,128)(2,1)} %get-tuple-element.94), channel_id=1, source_target_pairs={{0,10},{1,11},{2,8},{3,9},{4,2},{5,3},{6,0},{7,1},{8,14},{9,15},{1... | collective-permute-start | bytes 1179656 | tf_op jit(solution)/shard_map/ppermute | solution.py:333
  57.0 57.7 %copy-start.13 = (bf16[6,64,512]{2,1,0:T(8,128)(2,1)}, bf16[6,64,512]{2,1,0:T(8,128)(2,1)S(1)}, u32[]{:S(2)}) copy-start(bf16[6,64,512]{2,1,0:T(8,128)(2,1)S(1)} %collective-permute-done.4.refs_2_) | copy-start | bytes 1179652
  57.0 22.0 %collective-permute-start.9 = (bf16[6,64,512]{2,1,0:T(8,128)(2,1)}, bf16[6,64,512]{2,1,0:T(8,128)(2,1)S(1)}, u32[]{:S(2)}, u32[]{:S(2)}) collective-permute-start(bf16[6,64,512]{2,1,0:T(8,128)(2,1)} %get-tuple-element.95), channel_id=1, source_target_pairs={{0,11},{1,10},{2,9},{3,8},{4,3},{5,2},{6,1},{7,0},{8,15},{9,14},{1... | collective-permute-start | bytes 1179656 | tf_op jit(solution)/shard_map/ppermute | solution.py:333
  62.8 16.2 %copy-start.19 = (bf16[6,64,512]{2,1,0:T(8,128)(2,1)}, bf16[6,64,512]{2,1,0:T(8,128)(2,1)S(1)}, u32[]{:S(2)}) copy-start(bf16[6,64,512]{2,1,0:T(8,128)(2,1)S(1)} %collective-permute-done.5.refs_3_) | copy-start | bytes 1179652
  62.8 43.3 %copy-start.20 = (bf16[6,64,512]{2,1,0:T(8,128)(2,1)}, bf16[6,64,512]{2,1,0:T(8,128)(2,1)S(1)}, u32[]{:S(2)}) copy-start(bf16[6,64,512]{2,1,0:T(8,128)(2,1)S(1)} %collective-permute-done.6.refs_4_) | copy-start | bytes 1179652
  69.8 39.9 %copy-start.21 = (bf16[6,64,512]{2,1,0:T(8,128)(2,1)}, bf16[6,64,512]{2,1,0:T(8,128)(2,1)S(1)}, u32[]{:S(2)}) copy-start(bf16[6,64,512]{2,1,0:T(8,128)(2,1)S(1)} %collective-permute-done.7.refs_5_) | copy-start | bytes 1179652
  74.8 34.9 %copy-start.22 = (bf16[6,64,512]{2,1,0:T(8,128)(2,1)}, bf16[6,64,512]{2,1,0:T(8,128)(2,1)S(1)}, u32[]{:S(2)}) copy-start(bf16[6,64,512]{2,1,0:T(8,128)(2,1)S(1)} %collective-permute-done.8.refs_6_) | copy-start | bytes 1179652
  79.0 30.7 %copy-start.24 = (bf16[6,64,512]{2,1,0:T(8,128)(2,1)}, bf16[6,64,512]{2,1,0:T(8,128)(2,1)S(1)}, u32[]{:S(2)}) copy-start(bf16[6,64,512]{2,1,0:T(8,128)(2,1)S(1)} %collective-permute-done.9.refs_7_) | copy-start | bytes 1179652
  79.0 59.4 %collective-permute-start.10 = (bf16[6,64,512]{2,1,0:T(8,128)(2,1)}, bf16[6,64,512]{2,1,0:T(8,128)(2,1)S(1)}, u32[]{:S(2)}, u32[]{:S(2)}) collective-permute-start(bf16[6,64,512]{2,1,0:T(8,128)(2,1)} %get-tuple-element.96), channel_id=1, source_target_pairs={{0,0},{1,1},{2,2},{3,3},{4,8},{5,9},{6,10},{7,11},{8,4},{9,5},{10,... | collective-permute-start | bytes 1179656 | tf_op jit(solution)/shard_map/ppermute | solution.py:333
  104.1 36.2 %collective-permute-start.11 = (bf16[6,64,512]{2,1,0:T(8,128)(2,1)}, bf16[6,64,512]{2,1,0:T(8,128)(2,1)S(1)}, u32[]{:S(2)}, u32[]{:S(2)}) collective-permute-start(bf16[6,64,512]{2,1,0:T(8,128)(2,1)} %get-tuple-element.97), channel_id=1, source_target_pairs={{0,1},{1,0},{2,3},{3,2},{4,9},{5,8},{6,11},{7,10},{8,5},{9,4},{10,... | collective-permute-start | bytes 1179656 | tf_op jit(solution)/shard_map/ppermute | solution.py:333
  105.0 36.7 %collective-permute-start.12 = (bf16[6,64,512]{2,1,0:T(8,128)(2,1)}, bf16[6,64,512]{2,1,0:T(8,128)(2,1)S(1)}, u32[]{:S(2)}, u32[]{:S(2)}) collective-permute-start(bf16[6,64,512]{2,1,0:T(8,128)(2,1)} %get-tuple-element.98), channel_id=1, source_target_pairs={{0,2},{1,3},{2,0},{3,1},{4,10},{5,11},{6,8},{7,9},{8,6},{9,7},{10,... | collective-permute-start | bytes 1179656 | tf_op jit(solution)/shard_map/ppermute | solution.py:333
  106.1 60.5 %collective-permute-start.13 = (bf16[6,64,512]{2,1,0:T(8,128)(2,1)}, bf16[6,64,512]{2,1,0:T(8,128)(2,1)S(1)}, u32[]{:S(2)}, u32[]{:S(2)}) collective-permute-start(bf16[6,64,512]{2,1,0:T(8,128)(2,1)} %get-tuple-element.99), channel_id=1, source_target_pairs={{0,3},{1,2},{2,1},{3,0},{4,11},{5,10},{6,9},{7,8},{8,7},{9,6},{10,... | collective-permute-start | bytes 1179656 | tf_op jit(solution)/shard_map/ppermute | solution.py:333
  109.7 56.9 %collective-permute-start.14 = (bf16[6,64,512]{2,1,0:T(8,128)(2,1)}, bf16[6,64,512]{2,1,0:T(8,128)(2,1)S(1)}, u32[]{:S(2)}, u32[]{:S(2)}) collective-permute-start(bf16[6,64,512]{2,1,0:T(8,128)(2,1)} %get-tuple-element.100), channel_id=1, source_target_pairs={{0,8},{1,9},{2,10},{3,11},{4,0},{5,1},{6,2},{7,3},{8,12},{9,13},{1... | collective-permute-start | bytes 1179656 | tf_op jit(solution)/shard_map/ppermute | solution.py:333
  133.4 6.8 copy-start.9
  133.4 8.3 %copy-start.8 = (bf16[6,64,512]{2,1,0:T(8,128)(2,1)S(1)}, bf16[6,64,512]{2,1,0:T(8,128)(2,1)}, u32[]{:S(2)}) copy-start(bf16[6,64,512]{2,1,0:T(8,128)(2,1)} %get-tuple-element.103) | copy-start | bytes 1179652
  138.5 28.1 %copy-start.14 = (bf16[6,64,512]{2,1,0:T(8,128)(2,1)}, bf16[6,64,512]{2,1,0:T(8,128)(2,1)S(1)}, u32[]{:S(2)}) copy-start(bf16[6,64,512]{2,1,0:T(8,128)(2,1)S(1)} %collective-permute-done.10.refs_0_) | copy-start | bytes 1179652
  138.5 28.1 %collective-permute-start.15 = (bf16[6,64,512]{2,1,0:T(8,128)(2,1)S(1)}, bf16[6,64,512]{2,1,0:T(8,128)(2,1)S(1)}, u32[]{:S(2)}, u32[]{:S(2)}) collective-permute-start(bf16[6,64,512]{2,1,0:T(8,128)(2,1)S(1)} %copy-done.10), channel_id=1, source_target_pairs={{0,9},{1,8},{2,11},{3,10},{4,1},{5,0},{6,3},{7,2},{8,13},{9,12},{1... | collective-permute-start | bytes 1179656 | tf_op jit(solution)/shard_map/ppermute | solution.py:333
  140.3 26.3 %copy-start.15 = (bf16[6,64,512]{2,1,0:T(8,128)(2,1)}, bf16[6,64,512]{2,1,0:T(8,128)(2,1)S(1)}, u32[]{:S(2)}) copy-start(bf16[6,64,512]{2,1,0:T(8,128)(2,1)S(1)} %collective-permute-done.11.refs_1_) | copy-start | bytes 1179652
  140.3 26.4 %collective-permute-start.16 = (bf16[6,64,512]{2,1,0:T(8,128)(2,1)S(1)}, bf16[6,64,512]{2,1,0:T(8,128)(2,1)S(1)}, u32[]{:S(2)}, u32[]{:S(2)}) collective-permute-start(bf16[6,64,512]{2,1,0:T(8,128)(2,1)S(1)} %copy-done.9), channel_id=1, source_target_pairs={{0,10},{1,11},{2,8},{3,9},{4,2},{5,3},{6,0},{7,1},{8,14},{9,15},{1... | collective-permute-start | bytes 1179656 | tf_op jit(solution)/shard_map/ppermute | solution.py:333
  141.7 24.8 %copy-start.16 = (bf16[6,64,512]{2,1,0:T(8,128)(2,1)}, bf16[6,64,512]{2,1,0:T(8,128)(2,1)S(1)}, u32[]{:S(2)}) copy-start(bf16[6,64,512]{2,1,0:T(8,128)(2,1)S(1)} %collective-permute-done.12.refs_2_) | copy-start | bytes 1179652
  141.7 26.9 %collective-permute-start.17 = (bf16[6,64,512]{2,1,0:T(8,128)(2,1)S(1)}, bf16[6,64,512]{2,1,0:T(8,128)(2,1)S(1)}, u32[]{:S(2)}, u32[]{:S(2)}) collective-permute-start(bf16[6,64,512]{2,1,0:T(8,128)(2,1)S(1)} %copy-done.8), channel_id=1, source_target_pairs={{0,11},{1,10},{2,9},{3,8},{4,3},{5,2},{6,1},{7,0},{8,15},{9,14},{1... | collective-permute-start | bytes 1179656 | tf_op jit(solution)/shard_map/ppermute | solution.py:333
  143.7 31.2 %copy-start.32 = (bf16[4,64,512]{2,1,0:T(8,128)(2,1)S(1)}, bf16[4,64,512]{2,1,0:T(8,128)(2,1)}, u32[]{:S(2)}) copy-start(bf16[4,64,512]{2,1,0:T(8,128)(2,1)} %get-tuple-element.114) | copy-start | bytes 786436
  143.7 31.2 %copy-start.31 = (bf16[4,64,512]{2,1,0:T(8,128)(2,1)S(1)}, bf16[4,64,512]{2,1,0:T(8,128)(2,1)}, u32[]{:S(2)}) copy-start(bf16[4,64,512]{2,1,0:T(8,128)(2,1)} %get-tuple-element.115) | copy-start | bytes 786436
  143.7 34.9 %copy-start.30 = (bf16[4,64,512]{2,1,0:T(8,128)(2,1)S(1)}, bf16[4,64,512]{2,1,0:T(8,128)(2,1)}, u32[]{:S(2)}) copy-start(bf16[4,64,512]{2,1,0:T(8,128)(2,1)} %get-tuple-element.116) | copy-start | bytes 786436
  143.7 37.6 %copy-start.29 = (bf16[4,64,512]{2,1,0:T(8,128)(2,1)S(1)}, bf16[4,64,512]{2,1,0:T(8,128)(2,1)}, u32[]{:S(2)}) copy-start(bf16[4,64,512]{2,1,0:T(8,128)(2,1)} %get-tuple-element.117) | copy-start | bytes 786436
  143.7 44.0 %copy-start.28 = (bf16[4,64,512]{2,1,0:T(8,128)(2,1)S(1)}, bf16[4,64,512]{2,1,0:T(8,128)(2,1)}, u32[]{:S(2)}) copy-start(bf16[4,64,512]{2,1,0:T(8,128)(2,1)} %get-tuple-element.118) | copy-start | bytes 786436
  143.8 45.4 %copy-start.27 = (bf16[4,64,512]{2,1,0:T(8,128)(2,1)S(1)}, bf16[4,64,512]{2,1,0:T(8,128)(2,1)}, u32[]{:S(2)}) copy-start(bf16[4,64,512]{2,1,0:T(8,128)(2,1)} %get-tuple-element.119) | copy-start | bytes 786436
  166.6 22.8 %copy-start.17 = (bf16[6,64,512]{2,1,0:T(8,128)(2,1)}, bf16[6,64,512]{2,1,0:T(8,128)(2,1)S(1)}, u32[]{:S(2)}) copy-start(bf16[6,64,512]{2,1,0:T(8,128)(2,1)S(1)} %collective-permute-done.13.refs_3_) | copy-start | bytes 1179652
  166.6 22.8 %copy-start.18 = (bf16[6,64,512]{2,1,0:T(8,128)(2,1)}, bf16[6,64,512]{2,1,0:T(8,128)(2,1)S(1)}, u32[]{:S(2)}) copy-start(bf16[6,64,512]{2,1,0:T(8,128)(2,1)S(1)} %collective-permute-done.14.refs_4_) | copy-start | bytes 1179652
  166.6 22.7 %copy-start.23 = (bf16[6,64,512]{2,1,0:T(8,128)(2,1)}, bf16[6,64,512]{2,1,0:T(8,128)(2,1)S(1)}, u32[]{:S(2)}) copy-start(bf16[6,64,512]{2,1,0:T(8,128)(2,1)S(1)} %collective-permute-done.15.refs_5_) | copy-start | bytes 1179652
  166.6 22.7 %copy-start.25 = (bf16[6,64,512]{2,1,0:T(8,128)(2,1)}, bf16[6,64,512]{2,1,0:T(8,128)(2,1)S(1)}, u32[]{:S(2)}) copy-start(bf16[6,64,512]{2,1,0:T(8,128)(2,1)S(1)} %collective-permute-done.16.refs_6_) | copy-start | bytes 1179652
  168.7 20.7 %copy-start.26 = (bf16[6,64,512]{2,1,0:T(8,128)(2,1)}, bf16[6,64,512]{2,1,0:T(8,128)(2,1)S(1)}, u32[]{:S(2)}) copy-start(bf16[6,64,512]{2,1,0:T(8,128)(2,1)S(1)} %collective-permute-done.17.refs_7_) | copy-start | bytes 1179652
  168.7 12.7 %collective-permute-start.18 = (bf16[4,64,512]{2,1,0:T(8,128)(2,1)}, bf16[4,64,512]{2,1,0:T(8,128)(2,1)S(1)}, u32[]{:S(2)}, u32[]{:S(2)}) collective-permute-start(bf16[4,64,512]{2,1,0:T(8,128)(2,1)} %get-tuple-element.112), channel_id=1, source_target_pairs={{0,0},{1,1},{2,2},{3,3},{4,8},{5,9},{6,10},{7,11},{8,4},{9,5},{10,... | collective-permute-start | bytes 786440 | tf_op jit(solution)/shard_map/ppermute | solution.py:333
  174.1 13.6 %collective-permute-start.19 = (bf16[4,64,512]{2,1,0:T(8,128)(2,1)}, bf16[4,64,512]{2,1,0:T(8,128)(2,1)S(1)}, u32[]{:S(2)}, u32[]{:S(2)}) collective-permute-start(bf16[4,64,512]{2,1,0:T(8,128)(2,1)} %get-tuple-element.113), channel_id=1, source_target_pairs={{0,1},{1,0},{2,3},{3,2},{4,9},{5,8},{6,11},{7,10},{8,5},{9,4},{10,... | collective-permute-start | bytes 786440 | tf_op jit(solution)/shard_map/ppermute | solution.py:333
  174.9 14.2 %collective-permute-start.20 = (bf16[4,64,512]{2,1,0:T(8,128)(2,1)S(1)}, bf16[4,64,512]{2,1,0:T(8,128)(2,1)S(1)}, u32[]{:S(2)}, u32[]{:S(2)}) collective-permute-start(bf16[4,64,512]{2,1,0:T(8,128)(2,1)S(1)} %copy-done.32), channel_id=1, source_target_pairs={{0,2},{1,3},{2,0},{3,1},{4,10},{5,11},{6,8},{7,9},{8,6},{9,7},{10,... | collective-permute-start | bytes 786440 | tf_op jit(solution)/shard_map/ppermute | solution.py:333
  175.0 37.2 %collective-permute-start.21 = (bf16[4,64,512]{2,1,0:T(8,128)(2,1)S(1)}, bf16[4,64,512]{2,1,0:T(8,128)(2,1)S(1)}, u32[]{:S(2)}, u32[]{:S(2)}) collective-permute-start(bf16[4,64,512]{2,1,0:T(8,128)(2,1)S(1)} %copy-done.31), channel_id=1, source_target_pairs={{0,3},{1,2},{2,1},{3,0},{4,11},{5,10},{6,9},{7,8},{8,7},{9,6},{10,... | collective-permute-start | bytes 786440 | tf_op jit(solution)/shard_map/ppermute | solution.py:333
  178.7 33.5 %collective-permute-start.22 = (bf16[4,64,512]{2,1,0:T(8,128)(2,1)S(1)}, bf16[4,64,512]{2,1,0:T(8,128)(2,1)S(1)}, u32[]{:S(2)}, u32[]{:S(2)}) collective-permute-start(bf16[4,64,512]{2,1,0:T(8,128)(2,1)S(1)} %copy-done.30), channel_id=1, source_target_pairs={{0,8},{1,9},{2,10},{3,11},{4,0},{5,1},{6,2},{7,3},{8,12},{9,13},{1... | collective-permute-start | bytes 786440 | tf_op jit(solution)/shard_map/ppermute | solution.py:333
  181.4 30.7 %copy-start.33 = (bf16[4,64,512]{2,1,0:T(8,128)(2,1)}, bf16[4,64,512]{2,1,0:T(8,128)(2,1)S(1)}, u32[]{:S(2)}) copy-start(bf16[4,64,512]{2,1,0:T(8,128)(2,1)S(1)} %collective-permute-done.18.refs_0_) | copy-start | bytes 786436
  181.4 30.8 %collective-permute-start.23 = (bf16[4,64,512]{2,1,0:T(8,128)(2,1)S(1)}, bf16[4,64,512]{2,1,0:T(8,128)(2,1)S(1)}, u32[]{:S(2)}, u32[]{:S(2)}) collective-permute-start(bf16[4,64,512]{2,1,0:T(8,128)(2,1)S(1)} %copy-done.29), channel_id=1, source_target_pairs={{0,9},{1,8},{2,11},{3,10},{4,1},{5,0},{6,3},{7,2},{8,13},{9,12},{1... | collective-permute-start | bytes 786440 | tf_op jit(solution)/shard_map/ppermute | solution.py:333
  187.7 24.4 %copy-start.34 = (bf16[4,64,512]{2,1,0:T(8,128)(2,1)}, bf16[4,64,512]{2,1,0:T(8,128)(2,1)S(1)}, u32[]{:S(2)}) copy-start(bf16[4,64,512]{2,1,0:T(8,128)(2,1)S(1)} %collective-permute-done.19.refs_1_) | copy-start | bytes 786436
  187.7 24.4 %collective-permute-start.24 = (bf16[4,64,512]{2,1,0:T(8,128)(2,1)S(1)}, bf16[4,64,512]{2,1,0:T(8,128)(2,1)S(1)}, u32[]{:S(2)}, u32[]{:S(2)}) collective-permute-start(bf16[4,64,512]{2,1,0:T(8,128)(2,1)S(1)} %copy-done.28), channel_id=1, source_target_pairs={{0,10},{1,11},{2,8},{3,9},{4,2},{5,3},{6,0},{7,1},{8,14},{9,15},{1... | collective-permute-start | bytes 786440 | tf_op jit(solution)/shard_map/ppermute | solution.py:333
  189.2 23.0 %copy-start.35 = (bf16[4,64,512]{2,1,0:T(8,128)(2,1)}, bf16[4,64,512]{2,1,0:T(8,128)(2,1)S(1)}, u32[]{:S(2)}) copy-start(bf16[4,64,512]{2,1,0:T(8,128)(2,1)S(1)} %collective-permute-done.20.refs_2_) | copy-start | bytes 786436
  189.2 23.1 %collective-permute-start.25 = (bf16[4,64,512]{2,1,0:T(8,128)(2,1)S(1)}, bf16[4,64,512]{2,1,0:T(8,128)(2,1)S(1)}, u32[]{:S(2)}, u32[]{:S(2)}) collective-permute-start(bf16[4,64,512]{2,1,0:T(8,128)(2,1)S(1)} %copy-done.27), channel_id=1, source_target_pairs={{0,11},{1,10},{2,9},{3,8},{4,3},{5,2},{6,1},{7,0},{8,15},{9,14},{1... | collective-permute-start | bytes 786440 | tf_op jit(solution)/shard_map/ppermute | solution.py:333
  213.7 218.9 %all-to-all-start = ((bf16[8,36,64,512]{3,2,1,0:T(8,128)(2,1)}), bf16[8,36,64,512]{3,2,1,0:T(8,128)(2,1)}, u32[]{:S(2)}, u32[]{:S(2)}) async-start(bf16[8,36,64,512]{3,2,1,0:T(8,128)(2,1)} %bitcast.29), calls=%async_computation | async-start | bytes 37748736 | tf_op jit(solution)/shard_map/all_to_all | solution.py:274
  236.0 196.6 %collective-permute-start.26 = (bf16[64,512,128]{2,1,0:T(8,128)(2,1)}, bf16[64,512,128]{2,1,0:T(8,128)(2,1)}, u32[]{:S(2)}, u32[]{:S(2)}) collective-permute-start(bf16[64,512,128]{2,1,0:T(8,128)(2,1)} %bitcast_convert_fusion), channel_id=1, source_target_pairs={{0,16},{1,17},{2,18},{3,19},{4,20},{5,21},{6,22},{7,23},{8,24},{9,... | collective-permute-start | bytes 25165832 | tf_op jit(solution)/shard_map/ppermute | solution.py:351
  432.7 24.0 %all-to-all-start.1 = ((bf16[8,12,16,512]{3,2,1,0:T(8,128)(2,1)}), bf16[8,12,16,512]{3,2,1,0:T(8,128)(2,1)S(1)}, u32[]{:S(2)}, u32[]{:S(2)}) async-start(bf16[8,12,16,512]{3,2,1,0:T(8,128)(2,1)} %bitcast.34), calls=%async_computation.1 | async-start | bytes 3145728 | tf_op jit(solution)/shard_map/all_to_all | solution.py:274
  467.3 38.3 %all-to-all-start.2 = ((bf16[8,12,16,512]{3,2,1,0:T(8,128)(2,1)}), bf16[8,12,16,512]{3,2,1,0:T(8,128)(2,1)S(1)}, u32[]{:S(2)}, u32[]{:S(2)}) async-start(bf16[8,12,16,512]{3,2,1,0:T(8,128)(2,1)} %bitcast.14), calls=%async_computation.2 | async-start | bytes 3145728 | tf_op jit(solution)/shard_map/all_to_all | solution.py:274
  471.1 50.2 %collective-permute-start.27 = (bf16[16,512,128]{2,1,0:T(8,128)(2,1)}, bf16[16,512,128]{2,1,0:T(8,128)(2,1)}, u32[]{:S(2)}, u32[]{:S(2)}) collective-permute-start(bf16[16,512,128]{2,1,0:T(8,128)(2,1)} %finished.4), channel_id=1, source_target_pairs={{0,16},{1,17},{2,18},{3,19},{8,20},{9,21},{10,22},{11,23},{4,24},{... | collective-permute-start | bytes 6291464 | tf_op jit(solution)/shard_map/ppermute | solution.py:364
  521.2 38.1 %all-to-all-start.3 = ((bf16[8,12,16,512]{3,2,1,0:T(8,128)(2,1)}), bf16[8,12,16,512]{3,2,1,0:T(8,128)(2,1)S(1)}, u32[]{:S(2)}, u32[]{:S(2)}) async-start(bf16[8,12,16,512]{3,2,1,0:T(8,128)(2,1)} %bitcast.13), calls=%async_computation.3 | async-start | bytes 3145728 | tf_op jit(solution)/shard_map/all_to_all | solution.py:274
  524.8 50.2 %collective-permute-start.28 = (bf16[16,512,128]{2,1,0:T(8,128)(2,1)}, bf16[16,512,128]{2,1,0:T(8,128)(2,1)}, u32[]{:S(2)}, u32[]{:S(2)}) collective-permute-start(bf16[16,512,128]{2,1,0:T(8,128)(2,1)} %finished.5), channel_id=1, source_target_pairs={{0,16},{1,17},{2,18},{3,19},{8,20},{9,21},{10,22},{11,23},{4,24},{... | collective-permute-start | bytes 6291464 | tf_op jit(solution)/shard_map/ppermute | solution.py:364
  574.9 38.7 %all-to-all-start.4 = ((bf16[8,12,16,512]{3,2,1,0:T(8,128)(2,1)}), bf16[8,12,16,512]{3,2,1,0:T(8,128)(2,1)S(1)}, u32[]{:S(2)}, u32[]{:S(2)}) async-start(bf16[8,12,16,512]{3,2,1,0:T(8,128)(2,1)} %bitcast.12), calls=%async_computation.4 | async-start | bytes 3145728 | tf_op jit(solution)/shard_map/all_to_all | solution.py:274
  578.4 50.2 %collective-permute-start.29 = (bf16[16,512,128]{2,1,0:T(8,128)(2,1)}, bf16[16,512,128]{2,1,0:T(8,128)(2,1)}, u32[]{:S(2)}, u32[]{:S(2)}) collective-permute-start(bf16[16,512,128]{2,1,0:T(8,128)(2,1)} %finished.6), channel_id=1, source_target_pairs={{0,16},{1,17},{2,18},{3,19},{8,20},{9,21},{10,22},{11,23},{4,24},{... | collective-permute-start | bytes 6291464 | tf_op jit(solution)/shard_map/ppermute | solution.py:364
  628.6 49.9 %collective-permute-start.30 = (bf16[16,512,128]{2,1,0:T(8,128)(2,1)}, bf16[16,512,128]{2,1,0:T(8,128)(2,1)S(1)}, u32[]{:S(2)}, u32[]{:S(2)}) collective-permute-start(bf16[16,512,128]{2,1,0:T(8,128)(2,1)} %finished.7), channel_id=1, source_target_pairs={{0,16},{1,17},{2,18},{3,19},{8,20},{9,21},{10,22},{11,23},{4,24},{... | collective-permute-start | bytes 6291464 | tf_op jit(solution)/shard_map/ppermute | solution.py:364
  (14 other events, 17.9 us)
Sparse Core Ops, SparseCore 0:
  8.9 84.6 all-gather.1
